TPU v7x, 32 devices: a whole 2x2x4 slice. The times are simulated.
32 devices in a mesh: fsdp: 32 (over z, y, x, core).
Axes of the slice: x: 2, y: 2, z: 4, core: 2. Of those that a mesh axis runs over, the one named last changes fastest.
Arguments:
- inputs: float32 [2, 32, 256, 384], P(None, 'fsdp'), may hold values from -6 to 6
- cond: float32 [2, 32, 384], P(None, 'fsdp'), may hold values from -6 to 6
- live: int32 [2, 32], P(None, 'fsdp'), may hold values from 0 to 1, as said below
- ada_w: bfloat16 [1, 2304, 384], P(None, 'fsdp'), may hold values from -0.3125 to 0.3125
- attn_w: bfloat16 [1, 1536, 384], P(None, 'fsdp'), may hold values from -0.3125 to 0.3125
- fc1_w: bfloat16 [1, 1536, 384], P(None, 'fsdp'), may hold values from -0.3125 to 0.3125
- fc2_w: bfloat16 [1, 1536, 384], P(None, 'fsdp'), may hold values from -0.15625 to 0.15625
- biases: bfloat16 [1, 5376], P(None, 'fsdp'), may hold values from -3 to 3
- grad_out: float32 [2, 32, 256, 384], P(None, 'fsdp'), may hold values from -6 to 6
Outputs:
- outputs: float32 [2, 32, 256, 384], P(None, 'fsdp')
- d_inputs: float32 [2, 32, 256, 384], P(None, 'fsdp')
- d_cond: float32 [2, 32, 384], P(None, 'fsdp')
- d_ada_w: float32 [1, 2304, 384], P(None, 'fsdp')
- d_attn_w: float32 [1, 1536, 384], P(None, 'fsdp')
- d_fc1_w: float32 [1, 1536, 384], P(None, 'fsdp')
- d_fc2_w: float32 [1, 1536, 384], P(None, 'fsdp')
- d_biases: float32 [1, 5376], P(None, 'fsdp')
Inputs may be any that keep to these rules, and one draw needn't show every extreme that they name: `live`: in each micro-batch exactly 17 of the 32 slots hold a latent (1), the others none (0).
All inputs are finite; a program needn't handle non-finite values.
Results may differ from a plain program's by a relative error of at most 0.012.
The roundings to bfloat16 on the way count: a program that leaves them out, or rounds other values in their place, can miss the bound.
Values may be sent and summed in bfloat16 or wider, within the bound.
No kernel may reach another device: no remote copies, remote signals or barrier semaphores. Data moves between devices by JAX's collectives and lax.ppermute only.
A program may use at most 128 MiB of HBM per device.

v0:
```python
import math

import jax
import jax.numpy as jnp
from jax import lax
from jax.sharding import PartitionSpec as P

HEADS = 6


NORM_EPS = 1e-06


def product(form, left, right):
    return jnp.einsum(form, left, right, preferred_element_type=jnp.float32)


def layer_norm(values):
    center = values - jnp.mean(values, axis=-1, keepdims=True)
    inv_std = lax.rsqrt(jnp.mean(center * center, axis=-1, keepdims=True) + NORM_EPS)
    return (center * inv_std, inv_std)


def norm_back(grad_norm, normed, inv_std):
    return inv_std * (
        grad_norm
        - jnp.mean(grad_norm, axis=-1, keepdims=True)
        - normed * jnp.mean(grad_norm * normed, axis=-1, keepdims=True)
    )


def gelu_tanh(pre_act):
    return jax.nn.gelu(pre_act, approximate=True)


def forward_layer(layer_in, sc_b, layer_w):
    ada_rows, attn_rows, fc_in, fc_out, bias_row = layer_w
    width_n = layer_in.shape[1]
    hidden = fc_in.shape[0]
    tokens_n = layer_in.shape[0]
    head_dim = width_n // HEADS
    scaling = 1.0 / math.sqrt(head_dim)
    bias_f = bias_row.astype(jnp.float32)
    modulation = product("ed,d->e", ada_rows, sc_b) + bias_f[: 6 * width_n]
    shift_a, scale_a, gate_a, shift_b, scale_b, gate_b = jnp.split(modulation, 6)
    normed, inv_std = layer_norm(layer_in)
    h_in = (normed * (1.0 + scale_a) + shift_a).astype(jnp.bfloat16)
    qkv_bias = jnp.concatenate(
        [
            bias_f[6 * width_n : 7 * width_n],
            jnp.zeros((width_n,), jnp.float32),
            bias_f[7 * width_n : 8 * width_n],
        ]
    )
    qkv_rows = (product("td,ed->te", h_in, attn_rows[: 3 * width_n]) + qkv_bias).astype(
        jnp.bfloat16
    )
    queries = qkv_rows[:, :width_n].reshape(tokens_n, HEADS, head_dim)
    key_rows = qkv_rows[:, width_n : 2 * width_n].reshape(tokens_n, HEADS, head_dim)
    value_rows = qkv_rows[:, 2 * width_n :].reshape(tokens_n, HEADS, head_dim)
    scores = product("thd,shd->hts", queries, key_rows) * scaling
    row_max = jnp.max(scores, axis=-1, keepdims=True)
    log_total = row_max + jnp.log(jnp.sum(jnp.exp(scores - row_max), axis=-1, keepdims=True))
    probs_b = jnp.exp(scores - log_total).astype(jnp.bfloat16)
    context = (
        product("hts,shd->thd", probs_b, value_rows).reshape(tokens_n, width_n).astype(jnp.bfloat16)
    )
    attn_out = (
        product("te,de->td", context, attn_rows[3 * width_n :]) + bias_f[8 * width_n : 9 * width_n]
    )
    middle = layer_in + gate_a * attn_out
    normed_two, inv_std_two = layer_norm(middle)
    h_mid = (normed_two * (1.0 + scale_b) + shift_b).astype(jnp.bfloat16)
    pre_act = product("td,fd->tf", h_mid, fc_in) + bias_f[9 * width_n : 9 * width_n + hidden]
    act_b = gelu_tanh(pre_act).astype(jnp.bfloat16)
    mlp_out = product("tf,fd->td", act_b, fc_out) + bias_f[9 * width_n + hidden :]
    layer_out = middle + gate_b * mlp_out
    kept_acts = (
        modulation,
        normed,
        inv_std,
        h_in,
        queries,
        key_rows,
        value_rows,
        log_total,
        context,
        attn_out,
        normed_two,
        inv_std_two,
        h_mid,
        pre_act,
        act_b,
        mlp_out,
    )
    return (layer_out, kept_acts)


def backward_layer(grad_y, sc_b, layer_w, kept_acts):
    ada_rows, attn_rows, fc_in, fc_out, bias_row = layer_w
    (
        modulation,
        normed,
        inv_std,
        h_in,
        queries,
        key_rows,
        value_rows,
        log_total,
        context,
        attn_out,
        normed_two,
        inv_std_two,
        h_mid,
        pre_act,
        act_b,
        mlp_out,
    ) = kept_acts
    width_n = grad_y.shape[1]
    tokens_n = grad_y.shape[0]
    head_dim = width_n // HEADS
    scaling = 1.0 / math.sqrt(head_dim)
    shift_a, scale_a, gate_a, shift_b, scale_b, gate_b = jnp.split(modulation, 6)
    d_gate_b = jnp.sum(grad_y * mlp_out, axis=0)
    d_mlp = gate_b * grad_y
    d_mlp_b = d_mlp.astype(jnp.bfloat16)
    g_fc_out = product("tf,td->fd", act_b, d_mlp_b)
    d_act = product("td,fd->tf", d_mlp_b, fc_out)
    d_pre = jax.vjp(gelu_tanh, pre_act)[1](d_act)[0]
    d_pre_b = d_pre.astype(jnp.bfloat16)
    g_fc_in = product("tf,td->fd", d_pre_b, h_mid)
    d_hmid = product("tf,fd->td", d_pre_b, fc_in)
    d_scale_b = jnp.sum(d_hmid * normed_two, axis=0)
    d_shift_b = jnp.sum(d_hmid, axis=0)
    d_middle = grad_y + norm_back(d_hmid * (1.0 + scale_b), normed_two, inv_std_two)
    d_gate_a = jnp.sum(d_middle * attn_out, axis=0)
    d_attn = gate_a * d_middle
    d_attn_b = d_attn.astype(jnp.bfloat16)
    g_out_proj = product("td,te->de", d_attn_b, context)
    d_context = (
        product("td,de->te", d_attn_b, attn_rows[3 * width_n :])
        .astype(jnp.bfloat16)
        .reshape(tokens_n, HEADS, head_dim)
    )
    scores = product("thd,shd->hts", queries, key_rows) * scaling
    probs_f = jnp.exp(scores - log_total)
    probs_b = probs_f.astype(jnp.bfloat16)
    d_values = product("hts,thd->shd", probs_b, d_context)
    d_probs = product("thd,shd->hts", d_context, value_rows)
    row_dot = jnp.sum(probs_f * d_probs, axis=-1, keepdims=True)
    d_scores_b = (probs_f * (d_probs - row_dot)).astype(jnp.bfloat16)
    d_queries = product("hts,shd->thd", d_scores_b, key_rows).reshape(tokens_n, width_n) * scaling
    d_keys = product("hts,thd->shd", d_scores_b, queries).reshape(tokens_n, width_n) * scaling
    d_values = d_values.reshape(tokens_n, width_n)
    d_qkv_b = jnp.concatenate([d_queries, d_keys, d_values], axis=1).astype(jnp.bfloat16)
    g_qkv = product("te,td->ed", d_qkv_b, h_in)
    d_hin = product("te,ed->td", d_qkv_b, attn_rows[: 3 * width_n])
    d_scale_a = jnp.sum(d_hin * normed, axis=0)
    d_shift_a = jnp.sum(d_hin, axis=0)
    d_input = d_middle + norm_back(d_hin * (1.0 + scale_a), normed, inv_std)
    d_mod = jnp.concatenate([d_shift_a, d_scale_a, d_gate_a, d_shift_b, d_scale_b, d_gate_b])
    g_ada = d_mod[:, None] * sc_b.astype(jnp.float32)[None, :]
    d_sc = jnp.dot(d_mod, ada_rows.astype(jnp.float32), precision=lax.Precision.HIGHEST)
    g_bias = jnp.concatenate(
        [
            d_mod,
            jnp.sum(d_queries, axis=0),
            jnp.sum(d_values, axis=0),
            jnp.sum(d_attn, axis=0),
            jnp.sum(d_pre, axis=0),
            jnp.sum(d_mlp, axis=0),
        ]
    )
    g_attn = jnp.concatenate([g_qkv, g_out_proj], axis=0)
    return (d_input, d_sc, d_mod, (g_ada, g_attn, g_fc_in, g_fc_out, g_bias))


def run_forward(layer_in, cond_row, weights):
    sc_b = (cond_row * jax.nn.sigmoid(cond_row)).astype(jnp.bfloat16)
    current = layer_in
    layer_w = tuple((stack_w[0] for stack_w in weights))
    current, kept_acts = forward_layer(current, sc_b, layer_w)
    kept_all = [kept_acts]
    return (current, sc_b, kept_all)


def run_backward(grad_row, cond_row, sc_b, kept_all, weights):
    n_layers = weights[0].shape[0]
    grad_cur = grad_row
    d_sc_sum = jnp.zeros(cond_row.shape, jnp.float32)
    per_layer = [None] * n_layers
    mod_rows = [None] * n_layers
    for layer_idx in reversed(range(n_layers)):
        layer_w = tuple((stack_w[layer_idx] for stack_w in weights))
        grad_cur, d_sc, d_mod, layer_grads = backward_layer(
            grad_cur, sc_b, layer_w, kept_all[layer_idx]
        )
        d_sc_sum = d_sc
        per_layer[layer_idx] = layer_grads
        mod_rows[layer_idx] = d_mod
    sigmoid_c = jax.nn.sigmoid(cond_row)
    d_cond_row = d_sc_sum * sigmoid_c * (1.0 + cond_row * (1.0 - sigmoid_c))
    return (grad_cur, d_cond_row, per_layer, jnp.stack(mod_rows))


def local(inputs, cond, live, ada_w, attn_w, fc1_w, fc2_w, biases, grad_out):
    group_n = lax.axis_size("fsdp")
    shards = (ada_w, attn_w, fc1_w, fc2_w, biases)
    first_member = 1
    totals = [
        [jnp.zeros((shard_w.shape[1] * group_n,) + shard_w.shape[2:], jnp.float32)]
        for shard_w in shards
    ]
    out_rows, d_in_rows, d_cond_rows = ([], [], [])
    mod_list, sc_list = ([], [])
    for batch_idx in range(inputs.shape[0]):
        weights = (
            lax.all_gather(ada_w, "fsdp", axis=1, tiled=True),
            lax.all_gather(attn_w, "fsdp", axis=1, tiled=True),
            lax.all_gather(fc1_w, "fsdp", axis=1, tiled=True),
            lax.all_gather(fc2_w, "fsdp", axis=1, tiled=True),
            lax.all_gather(biases, "fsdp", axis=1, tiled=True),
        )
        slot_idx = 0
        forward_all = [run_forward(inputs[batch_idx, slot_idx], cond[batch_idx, slot_idx], weights)]
        weights = (
            lax.all_gather(ada_w, "fsdp", axis=1, tiled=True),
            lax.all_gather(attn_w, "fsdp", axis=1, tiled=True),
            lax.all_gather(fc1_w, "fsdp", axis=1, tiled=True),
            lax.all_gather(fc2_w, "fsdp", axis=1, tiled=True),
            lax.all_gather(biases, "fsdp", axis=1, tiled=True),
        )
        batch_out, batch_din, batch_dcond = ([], [], [])
        slot_idx = 0
        live_flag = live[batch_idx, slot_idx].astype(jnp.float32)
        last_out, sc_b, kept_all = forward_all[slot_idx]
        d_in, d_cond_row, per_layer, mod_stack = run_backward(
            live_flag * grad_out[batch_idx, slot_idx],
            cond[batch_idx, slot_idx],
            sc_b,
            kept_all,
            weights,
        )
        for member in range(first_member, 5):
            totals[member][0] = totals[member][0] + per_layer[0][member]
        mod_list.append(mod_stack)
        sc_list.append(sc_b.astype(jnp.float32))
        batch_out.append(live_flag * last_out)
        batch_din.append(d_in)
        batch_dcond.append(d_cond_row)
        out_rows.append(jnp.stack(batch_out))
        d_in_rows.append(jnp.stack(batch_din))
        d_cond_rows.append(jnp.stack(batch_dcond))
    stacked = [None] + [jnp.stack(totals[member]) for member in range(1, 5)]
    own_rows = ada_w.shape[1]
    row_start = lax.axis_index("fsdp") * own_rows
    mods = jnp.stack(mod_list)
    conds = jnp.stack(sc_list)
    own_mods = lax.dynamic_slice_in_dim(
        lax.all_gather(mods, "fsdp", axis=0, tiled=True), row_start, own_rows, 2
    )
    d_ada = jnp.einsum(
        "klr,kd->lrd",
        own_mods,
        lax.all_gather(conds, "fsdp", axis=0, tiled=True),
        precision=lax.Precision.HIGHEST,
    )
    rest = (
        lax.psum_scatter(stacked[1], "fsdp", scatter_dimension=1, tiled=True),
        lax.psum_scatter(stacked[2], "fsdp", scatter_dimension=1, tiled=True),
        lax.psum_scatter(stacked[3], "fsdp", scatter_dimension=1, tiled=True),
        lax.psum_scatter(stacked[4], "fsdp", scatter_dimension=1, tiled=True),
    )
    owned = (d_ada, rest[0], rest[1], rest[2], rest[3])
    return (
        jnp.stack(out_rows),
        jnp.stack(d_in_rows),
        jnp.stack(d_cond_rows),
        owned[0],
        owned[1],
        owned[2],
        owned[3],
        owned[4],
    )


def solution(mesh):
    return jax.shard_map(
        local,
        mesh=mesh,
        in_specs=(
            P(None, "fsdp", None, None),
            P(None, "fsdp", None),
            P(None, "fsdp"),
            P(None, "fsdp", None),
            P(None, "fsdp", None),
            P(None, "fsdp", None),
            P(None, "fsdp", None),
            P(None, "fsdp"),
            P(None, "fsdp", None, None),
        ),
        out_specs=(
            P(None, "fsdp", None, None),
            P(None, "fsdp", None, None),
            P(None, "fsdp", None),
            P(None, "fsdp", None),
            P(None, "fsdp", None),
            P(None, "fsdp", None),
            P(None, "fsdp", None),
            P(None, "fsdp"),
        ),
        check_vma=False,
    )
```

profile of v0, /device:TPU:0, one launch (start us, length us, event | category | flops | bytes accessed | tf_op | source)
XLA Modules:
  0.0 590.7 jit_solution(7924536084425494169)
XLA Ops:
  11.0 42.2 %all-reduce = bf16[5376]{0:T(1024)(128)(2,1)S(1)} all-reduce(bf16[5376]{0:T(1024)(128)(2,1)S(1)} %dynamic-update-slice), channel_id=1, replica_groups=mesh['fsdp'=32] {'fsdp'}, use_global_device_ids=true, to_apply=%add | all-reduce | flops 5376 | bytes 21504
  55.3 1.3 slice_reduce_fusion.9
  60.1 40.7 %all-gather = f32[32,2,384]{2,1,0:T(2,128)S(1)} all-gather(f32[1,2,384]{2,1,0:T(2,128)S(1)} %fusion.106), channel_id=1, replica_groups=mesh['fsdp'=32] {'fsdp'}, dimensions={0}, use_global_device_ids=true | all-gather | bytes 101376 | tf_op jit(solution)/shard_map/all_gather | solution.py:265
  101.5 2.2 fusion.44
  105.0 20.1 %all-gather.8.cloned.1.call-done = bf16[1,1536,384]{2,1,0:T(8,128)(2,1)} async-done(((bf16[1,48,384]{2,1,0:T(8,128)(2,1)}), bf16[1,1536,384]{2,1,0:T(8,128)(2,1)}) %all-gather.8.cloned.1.call-update) | async-done | bytes 1179664 | tf_op jit(solution)/shard_map/all_gather | solution.py:219
  125.1 1.7 fusion.2
  133.1 1.4 convolution_add_fusion.8
  134.9 2.1 fusion.133
  139.1 41.7 %all-gather.10.cloned.1.call-done = bf16[1,1536,384]{2,1,0:T(8,128)(2,1)} async-done(((bf16[1,48,384]{2,1,0:T(8,128)(2,1)}), bf16[1,1536,384]{2,1,0:T(8,128)(2,1)}) %all-gather.10.cloned.1.call-update) | async-done | bytes 1179664 | tf_op jit(solution)/shard_map/all_gather | solution.py:220
  180.8 3.2 convolution_add_fusion.4
  184.0 52.4 %all-gather.12.cloned.1.call-done = bf16[1,1536,384]{2,1,0:T(8,128)(2,1)} async-done(((bf16[1,48,384]{2,1,0:T(8,128)(2,1)}), bf16[1,1536,384]{2,1,0:T(8,128)(2,1)}) %all-gather.12.cloned.1.call-update) | async-done | bytes 1179664 | tf_op jit(solution)/shard_map/all_gather | solution.py:221
  236.4 4.0 fusion.148
  244.5 2.5 fusion.69
  247.7 1.9 convolution_convert_fusion
  249.7 1.7 copy.69
  251.4 3.4 multiply_reduce_fusion
  254.8 1.6 fusion.137
  256.5 2.2 fusion.147
  258.7 2.1 fusion.62
  265.0 3.2 multiply_reduce_fusion.1
  272.4 3.8 fusion
  277.0 1.7 multiply_convert_fusion.1
  284.1 1.9 multiply_reduce_fusion.7
  288.1 1.7 maximum_add_fusion
  291.2 1.9 fusion.76
  293.2 2.3 fusion.1
  295.5 1.5 copy-done.1
  302.2 39.6 %all-reduce.1 = f32[1,5376]{1,0:T(1,128)S(1)} all-reduce(f32[1,5376]{1,0:T(1,128)S(1)} %add.345), channel_id=5, replica_groups=mesh['fsdp'=32] {'fsdp'}, use_global_device_ids=true, to_apply=%region_47.0.clone | all-reduce | flops 5376 | bytes 43008
  343.1 41.7 %all_gather.19 = f32[64,1,2304]{2,1,0:T(1,128)S(1)} all-gather(f32[2,1,2304]{2,1,0:T(1,128)S(1)} %pad_maximum_fusion.8), channel_id=1, replica_groups=mesh['fsdp'=32] {'fsdp'}, dimensions={0}, use_global_device_ids=true | all-gather | bytes 608256 | tf_op jit(solution)/shard_map/all_gather | solution.py:260
  388.5 1.5 add_bitcast_fusion.1
  392.3 87.1 %reduce-scatter.5.cloned.1.call-done = f32[1,48,384]{2,1,0:T(8,128)} async-done(((f32[1,1536,384]{2,1,0:T(8,128)}), f32[1,48,384]{2,1,0:T(8,128)}) %reduce-scatter.5.cloned.1.call-update) | async-done | bytes 73744 | tf_op jit(solution)/shard_map/reduce_scatter | solution.py:269
  479.4 104.5 %reduce-scatter.9.cloned.1.call-done = f32[1,48,384]{2,1,0:T(8,128)} async-done(((f32[1,1536,384]{2,1,0:T(8,128)}), f32[1,48,384]{2,1,0:T(8,128)}) %reduce-scatter.9.cloned.1.call-update) | async-done | bytes 73744 | tf_op jit(solution)/shard_map/reduce_scatter | solution.py:271
  (393 shorter events, 52.8 us)
Async XLA Ops:
  7.2 94.3 %copy-start.69 = (f32[2,1,384]{2,1,0:T(1,128)S(1)}, f32[2,1,384]{2,1,0:T(1,128)}, u32[]{:S(2)}) copy-start(f32[2,1,384]{2,1,0:T(1,128)} %param.10) | copy-start | bytes 9220
  7.2 50.7 %copy-start.2 = (f32[2,1,256,384]{3,2,1,0:T(8,128)S(1)}, f32[2,1,256,384]{3,2,1,0:T(8,128)}, u32[]{:S(2)}) copy-start(f32[2,1,256,384]{3,2,1,0:T(8,128)} %param.9) | copy-start | bytes 2359300
  7.2 51.0 %copy-start.122 = (s32[2,1]{0,1:T(1,128)S(1)}, s32[2,1]{0,1:T(1,128)}, u32[]{:S(2)}) copy-start(s32[2,1]{0,1:T(1,128)} %param.11) | copy-start | bytes 28
  7.2 94.3 %all-gather.6.cloned.1.call-start = ((), (), s32[]{:S(2)}) async-start(), calls=%async_computation.3 | async-start | bytes 1824768 | tf_op jit(solution)/shard_map/all_gather | solution.py:218
  7.9 117.1 %all-gather.8.cloned.1.call-start = ((), (), s32[]{:S(2)}) async-start(), calls=%async_computation.4 | async-start | bytes 1216512 | tf_op jit(solution)/shard_map/all_gather | solution.py:219
  8.7 172.1 %all-gather.10.cloned.1.call-start = ((), (), s32[]{:S(2)}) async-start(), calls=%async_computation.5 | async-start | bytes 1216512 | tf_op jit(solution)/shard_map/all_gather | solution.py:220
  9.4 227.0 %all-gather.12.cloned.1.call-start = ((), (), s32[]{:S(2)}) async-start(), calls=%async_computation.6 | async-start | bytes 1216512 | tf_op jit(solution)/shard_map/all_gather | solution.py:221
  10.0 382.3 %reduce-scatter.7.cloned.1.call-start = ((), (), s32[]{:S(2)}) async-start(), calls=%async_computation.8 | async-start | bytes 2433024 | tf_op jit(solution)/shard_map/reduce_scatter | solution.py:270
  57.8 67.2 %copy-start.86 = (f32[256]{0:T(256)}, f32[256]{0:T(256)S(1)}, u32[]{:S(2)}) copy-start(f32[256]{0:T(256)S(1)} %get-tuple-element.118) | copy-start | bytes 3076
  57.8 70.0 %copy-start.84 = (f32[256]{0:T(256)}, f32[256]{0:T(256)S(1)}, u32[]{:S(2)}) copy-start(f32[256]{0:T(256)S(1)} %get-tuple-element.117) | copy-start | bytes 3076
  58.1 66.9 %copy-start.90 = (f32[256]{0:T(256)}, f32[256]{0:T(256)S(1)}, u32[]{:S(2)}) copy-start(f32[256]{0:T(256)S(1)} %add_rsqrt_fusion.3) | copy-start | bytes 3076
  58.1 69.7 %copy-start.93 = (f32[256]{0:T(256)}, f32[256]{0:T(256)S(1)}, u32[]{:S(2)}) copy-start(f32[256]{0:T(256)S(1)} %add_rsqrt_fusion.1) | copy-start | bytes 3076
  105.0 20.1 %copy-start.73 = (f32[384]{0:T(512)}, f32[384]{0:T(512)S(1)}, u32[]{:S(2)}) copy-start(f32[384]{0:T(512)S(1)} %get-tuple-element.77) | copy-start | bytes 4612
  105.0 20.1 %copy-start.99 = (f32[384]{0:T(512)}, f32[384]{0:T(512)S(1)}, u32[]{:S(2)}) copy-start(f32[384]{0:T(512)S(1)} %get-tuple-element.76) | copy-start | bytes 4612
  105.0 22.9 %copy-start.75 = (f32[384]{0:T(512)}, f32[384]{0:T(512)S(1)}, u32[]{:S(2)}) copy-start(f32[384]{0:T(512)S(1)} %get-tuple-element.112) | copy-start | bytes 4612
  105.0 22.9 %copy-start.101 = (f32[384]{0:T(512)}, f32[384]{0:T(512)S(1)}, u32[]{:S(2)}) copy-start(f32[384]{0:T(512)S(1)} %get-tuple-element.113) | copy-start | bytes 4612
  236.4 4.0 copy-start.11
  236.4 4.0 copy-start.15
  236.4 4.0 copy-start.78
  236.4 4.0 copy-start.83
  236.4 4.0 copy-start.96
  251.4 3.4 copy-start.35
  251.4 5.0 copy-start.49
  251.4 5.0 copy-start.124
  268.2 4.2 copy-start.12
  276.3 203.1 %reduce-scatter.5.cloned.1.call-start = ((), (), s32[]{:S(2)}) async-start(), calls=%async_computation.7 | async-start | bytes 2433024 | tf_op jit(solution)/shard_map/reduce_scatter | solution.py:269
  277.0 3.3 copy-start.24
  282.6 3.4 copy-start.52
  289.8 294.0 %reduce-scatter.9.cloned.1.call-start = ((), (), s32[]{:S(2)}) async-start(), calls=%async_computation.9 | async-start | bytes 2433024 | tf_op jit(solution)/shard_map/reduce_scatter | solution.py:271
  297.8 87.1 %copy-start.53 = (f32[64,384]{1,0:T(8,128)S(1)}, f32[64,384]{1,0:T(8,128)}, u32[]{:S(2)}) copy-start(f32[64,384]{1,0:T(8,128)} %reshape.707) | copy-start | bytes 294916
  297.8 90.7 %copy-start.92 = (f32[256]{0:T(256)S(1)}, f32[256]{0:T(256)}, u32[]{:S(2)}) copy-start(f32[256]{0:T(256)} %copy-done.90) | copy-start | bytes 3076
  297.9 90.7 %copy-start.95 = (f32[256]{0:T(256)S(1)}, f32[256]{0:T(256)}, u32[]{:S(2)}) copy-start(f32[256]{0:T(256)} %copy-done.93) | copy-start | bytes 3076
  (100 other events, 160.9 us)
Sparse Core Ops, SparseCore 0:
  10.8 58.3 all-gather.5
  72.1 52.9 all-gather.7
  128.0 52.8 all-gather.9
  183.6 52.8 all-gather.11
  276.4 98.4 reduce-scatter.6
  380.6 98.6 reduce-scatter.4
  485.2 98.5 reduce-scatter.8
where the time goes:
time: 592 us; the launch traced here: 591 us
  waiting for transfers between devices  308 us (52%)
  blocking collectives  164 us (28%)
  matrix products  57.1 us (10%)
  local copies, waits for them, and re-layouts  26 us (4%)
  other arithmetic  17.3 us (3%)
  between operations  17.1 us (3%)
    reduce_scatter x1, waiting for transfers between devices, local(): lax.psum_scatter(stacked[3], 'fsdp', scatter_dimension=1, tiled=True)  104 us
    reduce_scatter x1, waiting for transfers between devices, local(): lax.psum_scatter(stacked[1], 'fsdp', scatter_dimension=1, tiled=True)  87.1 us
    unnamed x2, blocking collectives  81.9 us
    dot_general x38, matrix products, product(): return jnp.einsum(form, left, right, preferred_element_type=jnp.float32)  54.5 us
    all_gather x1, waiting for transfers between devices, local(): lax.all_gather(fc2_w, 'fsdp', axis=1, tiled=True)  52.4 us
    all_gather x1, blocking collectives, local(): lax.all_gather(mods, 'fsdp', axis=0, tiled=True)  41.7 us
    all_gather x1, waiting for transfers between devices, local(): lax.all_gather(fc1_w, 'fsdp', axis=1, tiled=True)  41.7 us
    all_gather x1, blocking collectives, local(): lax.all_gather(conds, 'fsdp', axis=0, tiled=True)  40.7 us
  transfers between devices with their start and end apart: 7, of which 5 were waited for; matrix products, arithmetic and copies ran while one was open for 9% of the time, Pallas kernels for 0%

commit v1 on v0

--- a/solution.py
+++ b/solution.py
@@ -203,84 +203,127 @@
     return (grad_cur, d_cond_row, per_layer, jnp.stack(mod_rows))
 
 
+def gather_orders(count):
+    high = list(range(count - 1, 2, -1))
+    near = [k for k in (2, 1) if k < count]
+    return high + near + [0], high + near[::-1] + [0]
+
+
+def exchange(value, bit_idx, group_n):
+    return lax.ppermute(value, "fsdp", [(dev, dev ^ (1 << bit_idx)) for dev in range(group_n)])
+
+
+def own_bit(bit_idx):
+    return (lax.axis_index("fsdp") >> bit_idx) & 1
+
+
+def gather_blocks(block, order):
+    count = len(order)
+    cur = block.reshape((1,) * count + block.shape)
+    for bit_idx in order:
+        other = exchange(cur, bit_idx, 1 << count)
+        upper = own_bit(bit_idx) == 1
+        cur = jnp.concatenate(
+            [jnp.where(upper, other, cur), jnp.where(upper, cur, other)], axis=count - 1 - bit_idx
+        )
+    return cur
+
+
+def scatter_sum(blocks, order):
+    count = len(order)
+    cur = blocks
+    for step, bit_idx in enumerate(order):
+        axis = count - 1 - bit_idx
+        mine = own_bit(bit_idx)
+        other = exchange(
+            lax.dynamic_index_in_dim(cur, 1 - mine, axis, keepdims=True), bit_idx, 1 << count
+        )
+        kept = lax.dynamic_index_in_dim(cur, mine, axis, keepdims=True)
+        total = kept.astype(jnp.float32) + other.astype(jnp.float32)
+        cur = total if step == count - 1 else total.astype(jnp.bfloat16)
+    return cur.reshape(blocks.shape[count:])
+
+
+def swap_blocks(blocks, order):
+    count = len(order)
+    cur = blocks
+    for bit_idx in order:
+        axis = count - 1 - bit_idx
+        mine = own_bit(bit_idx)
+        other = exchange(
+            lax.dynamic_index_in_dim(cur, 1 - mine, axis, keepdims=True), bit_idx, 1 << count
+        )
+        kept = lax.dynamic_index_in_dim(cur, mine, axis, keepdims=True)
+        upper = mine == 1
+        cur = jnp.concatenate(
+            [jnp.where(upper, other, kept), jnp.where(upper, kept, other)], axis=axis
+        )
+    return cur
+
+
 def local(inputs, cond, live, ada_w, attn_w, fc1_w, fc2_w, biases, grad_out):
     group_n = lax.axis_size("fsdp")
-    shards = (ada_w, attn_w, fc1_w, fc2_w, biases)
-    first_member = 1
-    totals = [
-        [jnp.zeros((shard_w.shape[1] * group_n,) + shard_w.shape[2:], jnp.float32)]
-        for shard_w in shards
+    count = group_n.bit_length() - 1
+    first, second = gather_orders(count)
+    width_n = attn_w.shape[2]
+    batches = inputs.shape[0]
+    own_ada, own_bias = ada_w.shape[1], biases.shape[1]
+    sc_own = (cond[:, 0] * jax.nn.sigmoid(cond[:, 0])).astype(jnp.bfloat16)
+    bias_line = jnp.pad(biases, ((0, 0), (0, width_n - own_bias)))
+    side_rows = own_ada + 1 + batches
+    pad_rows = -side_rows % 16
+    side = jnp.concatenate(
+        [ada_w[0], bias_line, sc_own, jnp.zeros((pad_rows, width_n), jnp.bfloat16)], axis=0
+    )
+    side_all = gather_blocks(side, second).reshape(group_n, side_rows + pad_rows, width_n)
+    attn_all = gather_blocks(attn_w[0], first).reshape(1, -1, width_n)
+    fc1_all = gather_blocks(fc1_w[0], first).reshape(1, -1, width_n)
+    fc2_all = gather_blocks(fc2_w[0], second).reshape(1, -1, width_n)
+    ada_all = side_all[:, :own_ada].reshape(1, -1, width_n)
+    bias_all = side_all[:, own_ada, :own_bias].reshape(1, -1)
+    sc_all = side_all[:, own_ada + 1 : own_ada + 1 + batches]
+    weights = (ada_all, attn_all, fc1_all, fc2_all, bias_all)
+    totals = [0.0] * 5
+    out_rows, d_in_rows, d_cond_rows, mod_list = ([], [], [], [])
+    for batch_idx in range(batches):
+        live_flag = live[batch_idx, 0].astype(jnp.float32)
+        last_out, sc_b, kept_all = run_forward(inputs[batch_idx, 0], cond[batch_idx, 0], weights)
+        d_in, d_cond_row, per_layer, mod_stack = run_backward(
+            live_flag * grad_out[batch_idx, 0], cond[batch_idx, 0], sc_b, kept_all, weights
+        )
+        for member in range(1, 5):
+            totals[member] = totals[member] + per_layer[0][member]
+        mod_list.append(mod_stack[0])
+        out_rows.append((live_flag * last_out)[None])
+        d_in_rows.append(d_in[None])
+        d_cond_rows.append(d_cond_row[None])
+    cube = (2,) * count
+    sums = [
+        scatter_sum(totals[member].astype(jnp.bfloat16).reshape(cube + (-1, width_n)), order[::-1])
+        for member, order in ((1, first), (2, first), (3, second))
     ]
-    out_rows, d_in_rows, d_cond_rows = ([], [], [])
-    mod_list, sc_list = ([], [])
-    for batch_idx in range(inputs.shape[0]):
-        weights = (
-            lax.all_gather(ada_w, "fsdp", axis=1, tiled=True),
-            lax.all_gather(attn_w, "fsdp", axis=1, tiled=True),
-            lax.all_gather(fc1_w, "fsdp", axis=1, tiled=True),
-            lax.all_gather(fc2_w, "fsdp", axis=1, tiled=True),
-            lax.all_gather(biases, "fsdp", axis=1, tiled=True),
-        )
-        slot_idx = 0
-        forward_all = [run_forward(inputs[batch_idx, slot_idx], cond[batch_idx, slot_idx], weights)]
-        weights = (
-            lax.all_gather(ada_w, "fsdp", axis=1, tiled=True),
-            lax.all_gather(attn_w, "fsdp", axis=1, tiled=True),
-            lax.all_gather(fc1_w, "fsdp", axis=1, tiled=True),
-            lax.all_gather(fc2_w, "fsdp", axis=1, tiled=True),
-            lax.all_gather(biases, "fsdp", axis=1, tiled=True),
-        )
-        batch_out, batch_din, batch_dcond = ([], [], [])
-        slot_idx = 0
-        live_flag = live[batch_idx, slot_idx].astype(jnp.float32)
-        last_out, sc_b, kept_all = forward_all[slot_idx]
-        d_in, d_cond_row, per_layer, mod_stack = run_backward(
-            live_flag * grad_out[batch_idx, slot_idx],
-            cond[batch_idx, slot_idx],
-            sc_b,
-            kept_all,
-            weights,
-        )
-        for member in range(first_member, 5):
-            totals[member][0] = totals[member][0] + per_layer[0][member]
-        mod_list.append(mod_stack)
-        sc_list.append(sc_b.astype(jnp.float32))
-        batch_out.append(live_flag * last_out)
-        batch_din.append(d_in)
-        batch_dcond.append(d_cond_row)
-        out_rows.append(jnp.stack(batch_out))
-        d_in_rows.append(jnp.stack(batch_din))
-        d_cond_rows.append(jnp.stack(batch_dcond))
-    stacked = [None] + [jnp.stack(totals[member]) for member in range(1, 5)]
-    own_rows = ada_w.shape[1]
-    row_start = lax.axis_index("fsdp") * own_rows
-    mods = jnp.stack(mod_list)
-    conds = jnp.stack(sc_list)
-    own_mods = lax.dynamic_slice_in_dim(
-        lax.all_gather(mods, "fsdp", axis=0, tiled=True), row_start, own_rows, 2
-    )
+    mods = jnp.stack(mod_list).reshape(batches, group_n, own_ada)
+    side_grads = jnp.concatenate(
+        [mods[idx] for idx in range(batches)] + [totals[4].reshape(group_n, own_bias)], axis=1
+    )
+    swapped = swap_blocks(side_grads.reshape(cube + (1, -1)), second[::-1]).reshape(group_n, -1)
+    own_mods = swapped[:, : batches * own_ada].reshape(group_n * batches, own_ada)
+    d_bias = jnp.sum(swapped[:, batches * own_ada :], axis=0)
     d_ada = jnp.einsum(
-        "klr,kd->lrd",
+        "kr,kd->rd",
         own_mods,
-        lax.all_gather(conds, "fsdp", axis=0, tiled=True),
+        sc_all.reshape(group_n * batches, width_n).astype(jnp.float32),
         precision=lax.Precision.HIGHEST,
     )
-    rest = (
-        lax.psum_scatter(stacked[1], "fsdp", scatter_dimension=1, tiled=True),
-        lax.psum_scatter(stacked[2], "fsdp", scatter_dimension=1, tiled=True),
-        lax.psum_scatter(stacked[3], "fsdp", scatter_dimension=1, tiled=True),
-        lax.psum_scatter(stacked[4], "fsdp", scatter_dimension=1, tiled=True),
-    )
-    owned = (d_ada, rest[0], rest[1], rest[2], rest[3])
     return (
         jnp.stack(out_rows),
         jnp.stack(d_in_rows),
         jnp.stack(d_cond_rows),
-        owned[0],
-        owned[1],
-        owned[2],
-        owned[3],
-        owned[4],
+        d_ada[None],
+        sums[0][None],
+        sums[1][None],
+        sums[2][None],
+        d_bias[None],
     )
 
 

time: 592 us -> 202 us (0.34)
  waiting for transfers between devices: 308 us -> 33.2 us
  blocking collectives: 164 us -> 0 us
  starting transfers between devices: 0.49 us -> 44.8 us
  local copies, waits for them, and re-layouts: 26 us -> 44.3 us
  between operations: 17.1 us -> 4.18 us
  matrix products: 57.1 us -> 49.9 us
  other arithmetic: 17.3 us -> 24.5 us
    reduce_scatter x3 -> x0, waiting for transfers between devices: 192 us -> none  [the longest x1 104 us: local(): lax.psum_scatter(stacked[3], 'fsdp', scatter_dimension=1, tiled=True)]
    all_gather x4 -> x0, waiting for transfers between devices: 114 us -> none  [the longest x1 52.4 us: local(): lax.all_gather(fc2_w, 'fsdp', axis=1, tiled=True)]
    all_gather x2 -> x0, blocking collectives: 82.4 us -> none  [the longest x1 41.7 us: local(): lax.all_gather(mods, 'fsdp', axis=0, tiled=True)]
    unnamed x2 -> x0, blocking collectives: 81.9 us -> none
    ppermute x0 -> x40, starting transfers between devices: none -> 44.8 us  [exchange(): lax.ppermute(value, 'fsdp', [(dev, dev ^ 1 << bit_idx) for dev in range(g...]
    ppermute x0 -> x40, waiting for transfers between devices: none -> 33.2 us  [exchange(): lax.ppermute(value, 'fsdp', [(dev, dev ^ 1 << bit_idx) for dev in range(g...]
    unnamed x284 -> x294, local copies, waits for them, and re-layouts: 13.5 us -> 24.8 us
    dot_general x38, matrix products: 54.5 us -> 47.3 us  [product(): return jnp.einsum(form, left, right, preferred_element_type=jnp.float32)]
  transfers between devices with their start and end apart: 7 -> 40, of which waited for: 5 -> 19; matrix products, arithmetic and copies ran while one was open for 9% -> 15% of each run, Pallas kernels for 0% -> 0%
where the time goes in v1:
time: 202 us; the launch traced here: 201 us
  matrix products  49.9 us (25%)
  starting transfers between devices  44.8 us (22%)
  local copies, waits for them, and re-layouts  44.3 us (22%)
  waiting for transfers between devices  33.2 us (16%)
  other arithmetic  24.5 us (12%)
  between operations  4.18 us (2%)
    dot_general x38, matrix products, product(): return jnp.einsum(form, left, right, preferred_element_type=jnp.float32)  47.3 us
    ppermute x40, starting transfers between devices, exchange(): lax.ppermute(value, 'fsdp', [(dev, dev ^ 1 << bit_idx) for dev in range(g...  44.8 us
    ppermute x40, waiting for transfers between devices, exchange(): lax.ppermute(value, 'fsdp', [(dev, dev ^ 1 << bit_idx) for dev in range(g...  33.2 us
    unnamed x294, local copies, waits for them, and re-layouts  24.8 us
    convert_element_type x12, other arithmetic, scatter_sum(): cur = total if step == count - 1 else total.astype(jnp.bfloat16)  4.1 us
  transfers between devices with their start and end apart: 40, of which 19 were waited for; matrix products, arithmetic and copies ran while one was open for 15% of the time, Pallas kernels for 0%

profile of v1, /device:TPU:0, one launch (start us, length us, event | category | flops | bytes accessed | tf_op | source)
XLA Modules:
  0.0 200.7 jit_solution(1742716158578604677)
XLA Ops:
  0.7 4.1 %collective-permute-start.15 = (bf16[1,1,1,1,1,48,384]{6,5,4,3,2,1,0:T(8,128)(2,1)}, bf16[1,1,1,1,1,48,384]{6,5,4,3,2,1,0:T(8,128)(2,1)S(1)}, u32[]{:S(2)}, u32[]{:S(2)}) collective-permute-start(bf16[1,1,1,1,1,48,384]{6,5,4,3,2,1,0:T(8,128)(2,1)} %bitcast.281), channel_id=1, source_target_pairs={{0,16},{1,17},{2,18},{3,19},{4,20},{5,21},{6,22},{7,23},{8,24},{9,... | collective-permute-start | bytes 110600 | tf_op jit(solution)/shard_map/ppermute | solution.py:213
  4.9 2.8 %collective-permute-start.5 = (bf16[1,1,1,1,1,48,384]{6,5,4,3,2,1,0:T(8,128)(2,1)}, bf16[1,1,1,1,1,48,384]{6,5,4,3,2,1,0:T(8,128)(2,1)S(1)}, u32[]{:S(2)}, u32[]{:S(2)}) collective-permute-start(bf16[1,1,1,1,1,48,384]{6,5,4,3,2,1,0:T(8,128)(2,1)} %bitcast.280), channel_id=1, source_target_pairs={{0,16},{1,17},{2,18},{3,19},{4,20},{5,21},{6,22},{7,23},{8,24},{9,... | collective-permute-start | bytes 110600 | tf_op jit(solution)/shard_map/ppermute | solution.py:213
  15.6 1.9 collective-permute-start.6
  17.8 1.9 collective-permute-start.16
  20.9 1.8 collective-permute-start.7
  22.8 1.6 collective-permute-start.12
  29.6 1.6 collective-permute-done.17
  32.4 4.1 %collective-permute-done.2 = bf16[2,2,1,1,1,80,384]{6,5,4,3,2,1,0:T(8,128)(2,1)S(1)} collective-permute-done((bf16[2,2,1,1,1,80,384]{6,5,4,3,2,1,0:T(8,128)(2,1)S(1)}, bf16[2,2,1,1,1,80,384]{6,5,4,3,2,1,0:T(8,128)(2,1)S(1)}, u32[]{:S(2)}, u32[]{:S(2)}) %collective-permute-start.2) | collective-permute-done | bytes 245792 | tf_op jit(solution)/shard_map/ppermute | solution.py:213
  37.7 4.9 %collective-permute-done.8 = bf16[2,2,2,1,1,48,384]{6,5,4,3,2,1,0:T(8,128)(2,1)S(1)} collective-permute-done((bf16[2,2,2,1,1,48,384]{6,5,4,3,2,1,0:T(8,128)(2,1)S(1)}, bf16[2,2,2,1,1,48,384]{6,5,4,3,2,1,0:T(8,128)(2,1)S(1)}, u32[]{:S(2)}, u32[]{:S(2)}) %collective-permute-start.8) | collective-permute-done | bytes 294944 | tf_op jit(solution)/shard_map/ppermute | solution.py:213
  42.9 2.9 %collective-permute-done.13 = bf16[2,2,2,1,1,48,384]{6,5,4,3,2,1,0:T(8,128)(2,1)S(1)} collective-permute-done((bf16[2,2,2,1,1,48,384]{6,5,4,3,2,1,0:T(8,128)(2,1)S(1)}, bf16[2,2,2,1,1,48,384]{6,5,4,3,2,1,0:T(8,128)(2,1)S(1)}, u32[]{:S(2)}, u32[]{:S(2)}) %collective-permute-start.13) | collective-permute-done | bytes 294944 | tf_op jit(solution)/shard_map/ppermute | solution.py:213
  64.5 1.7 fusion.115
  67.9 2.2 %fusion.129 = (f32[1536]{0:T(1024)}, bf16[256,1536]{1,0:T(8,128)(2,1)S(1)}) fusion(f32[256,1536]{1,0:T(8,128)S(1)} %convolution_add_fusion.5, bf16[1536,384]{1,0:T(8,128)(2,1)S(1)} %bitcast.259, f32[2,1,256,384]{3,2,1,0:T(8,128)S(1)} %copy-done.58, f32[384]{0:T(512)S(1)} %copy-done.124, f32[]{:T(128)} %bitcast), kind=kOutput, calls=%fused_computation.398 | convolution fusion | flops 310540800 | bytes 3940356 | tf_op jit(solution)/shard_map/td,fd->tf/dot_general | solution.py:15
  74.3 2.2 %fusion.49 = f32[1536,384]{1,0:T(8,128)} fusion(f32[2,1,256,384]{3,2,1,0:T(8,128)S(1)} %copy-done.58, f32[]{:T(128)} %bitcast, f32[384]{0:T(512)S(1)} %copy-done.124, f32[256,1536]{1,0:T(8,128)S(1)} %convolution_add_fusion.5), kind=kOutput, calls=%fused_computation.178 | convolution fusion | flops 305823744 | bytes 4327428 | tf_op jit(solution)/shard_map/tf,td->fd/dot_general | solution.py:15
  76.4 1.8 copy.65
  78.2 2.6 %fusion.121 = (f32[6,64]{1,0:T(8,128)}, bf16[256,6,64]{0,2,1:T(8,128)(2,1)}) fusion(bf16[256,6,64]{0,2,1:T(8,128)(2,1)} %bitcast.255, f32[6,256,256]{1,2,0:T(8,128)S(1)} %get-tuple-element.164, f32[6,256]{1,0:T(8,128)S(1)} %log_add_fusion.1), kind=kOutput, calls=%fused_computation.390 | convolution fusion | flops 51314304 | bytes 1973760 | tf_op jit(solution)/shard_map/hts,thd->shd/dot_general | solution.py:15
  86.9 2.0 %fusion.130 = (f32[1536]{0:T(1024)}, bf16[256,1536]{1,0:T(8,128)(2,1)S(1)}) fusion(f32[256,1536]{1,0:T(8,128)S(1)} %convolution_add_fusion.4, bf16[1536,384]{1,0:T(8,128)(2,1)S(1)} %bitcast.261, f32[2,1,256,384]{3,2,1,0:T(8,128)S(1)} %copy-done.59, f32[384]{0:T(512)S(1)} %copy-done.123, f32[]{:T(128)} %bitcast.18), kind=kOutput, calls=%fused_computation.399 | convolution fusion | flops 310540800 | bytes 3940356 | tf_op jit(solution)/shard_map/td,fd->tf/dot_general | solution.py:15
  90.2 2.4 %fusion.41 = (f32[384]{0:T(512)}, f32[384]{0:T(512)}, f32[384]{0:T(512)}, f32[384]{0:T(512)S(1)}, f32[384]{0:T(512)}, /*index=5*/f32[384]{0:T(512)}, f32[256,384...) fusion(f32[2,1,256,384]{3,2,1,0:T(8,128)S(1)} %copy-done.59, f32[]{:T(128)} %bitcast.18, ...), kind=kOutput, calls=%fused_computation.148 | convolution fusion | flops 308377344 | bytes 6707712 | tf_op jit(solution)/shard_map/tf,fd->td/dot_general | solution.py:15
  95.1 2.1 %fusion.32 = f32[1536,384]{1,0:T(8,128)} fusion(bf16[256,1536]{1,0:T(8,128)(2,1)S(1)} %copy-done.49, f32[256,384]{1,0:T(8,128)S(1)} %get-tuple-element.43, f32[384]{0:T(512)S(1)} %copy-done.92, f32[384]{0:T(512)S(1)} %copy-done.74, f32[256]{0:T(256)S(1)} %copy-done.104, f32[256]{0:T(256)S(1)} %copy-done.77), kind=kOutput, calls=%fused_computation.127 | convolution fusion | flops 302481408 | bytes 3544064 | tf_op jit(solution)/shard_map/tf,td->fd/dot_general | solution.py:15
  102.5 2.2 %multiply_reduce_fusion.7 = (f32[384]{0:T(512)S(1)}, f32[256]{0:T(256)}, f32[256]{0:T(256)}, f32[384]{0:T(512)}, f32[256]{0:T(256)}, /*index=5*/f32[256]{0:T(256...) fusion(f32[256]{0:T(256)S(1)} %copy-done.106, f32[256]{0:T(256)S(1)} %copy-done.99, ...), kind=kOutput, calls=%fused_computation.115 | convolution fusion | flops 230028800 | bytes 3065856 | tf_op jit(solution)/shard_map/te,ed->td/dot_general | solution.py:15
  125.1 2.8 %fusion.42 = f32[1152,384]{1,0:T(8,128)} fusion(bf16[256,384]{0,1:T(8,128)(2,1)} %bitcast.276, bf16[256,384]{0,1:T(8,128)(2,1)S(1)} %bitcast.270, bf16[256,384]{0,1:T(8,128)(2,1)S(1)} %bitcast.272, f32[384]{0:T(512)} %copy-done.114, f32[384]{0:T(512)} %copy-done.87, f32[2,1,256,384]{3,2,1,0:T(8,128)S(1)} %copy-done.4, f32[256]{0:T(256)} %copy-done.108, ...), kind=kOutput, calls=%fused_computation.176 | convolution fusion | flops 228753408 | bytes 2757632 | tf_op jit(solution)/shard_map/te,td->ed/dot_general | solution.py:15
  128.0 2.8 %fusion.43 = f32[1152,384]{1,0:T(8,128)} fusion(bf16[256,384]{0,1:T(8,128)(2,1)} %bitcast.273, bf16[256,384]{0,1:T(8,128)(2,1)S(1)} %bitcast.266, bf16[256,384]{0,1:T(8,128)(2,1)S(1)} %bitcast.268, f32[384]{0:T(512)} %copy-done.113, f32[384]{0:T(512)} %copy-done.84, f32[2,1,256,384]{3,2,1,0:T(8,128)S(1)} %copy-done.4, f32[256]{0:T(256)} %copy-done.105, ...), kind=kOutput, calls=%fused_computation.177 | convolution fusion | flops 228753408 | bytes 2757632 | tf_op jit(solution)/shard_map/te,td->ed/dot_general | solution.py:15
  132.3 2.8 %fusion.1 = bf16[1536,384]{1,0:T(8,128)(2,1)S(1)} fusion(f32[1536,384]{1,0:T(8,128)} %fusion.49, f32[2,1,256,384]{3,2,1,0:T(8,128)} %param.17, f32[]{:T(128)} %bitcast.18, f32[384]{0:T(512)} %get-tuple-element.190, f32[256,1536]{1,0:T(8,128)S(1)} %copy-done.37), kind=kOutput, calls=%fused_computation.5 | convolution fusion | flops 307003392 | bytes 5507584 | tf_op jit(solution)/shard_map/tf,td->fd/dot_general | solution.py:15
  137.4 2.7 %fusion = bf16[1536,384]{1,0:T(8,128)(2,1)S(1)} fusion(f32[1536,384]{1,0:T(8,128)} %fusion.32, bf16[256,1536]{1,0:T(8,128)(2,1)} %copy-done.44, f32[256,384]{1,0:T(8,128)S(1)} %copy-done.11, f32[384]{0:T(512)S(1)} %copy-done.83, f32[384]{0:T(512)S(1)} %copy-done.81, f32[256]{0:T(256)S(1)} %copy-done.112, f32[256]{0:T(256)S(1)} %copy-done.94), kind=kOutput, calls=%fused_computation.4 | convolution fusion | flops 303661056 | bytes 4723712 | tf_op jit(solution)/shard_map/tf,td->fd/dot_general | solution.py:15
  144.4 2.1 %fusion.4 = bf16[1536,384]{1,0:T(8,128)(2,1)S(1)} fusion(f32[384,384]{1,0:T(8,128)} %fusion.75, f32[1152,384]{1,0:T(8,128)} %fusion.43, f32[384,384]{1,0:T(8,128)} %fusion.76, f32[1152,384]{1,0:T(8,128)S(1)} %copy-done.8), kind=kLoop, calls=%fused_computation.11 | loop fusion | flops 2359296 | bytes 5898240 | tf_op jit(solution)/shard_map/convert_element_type | solution.py:302
  151.1 2.3 %collective-permute-done.21 = f32[2,2,1,2,2,1,312]{6,4,3,2,1,0,5:T(2,128)S(1)} collective-permute-done((f32[2,2,1,2,2,1,312]{6,4,3,2,1,0,5:T(2,128)S(1)}, f32[2,2,1,2,2,1,312]{6,4,3,2,1,0,5:T(2,128)S(1)}, u32[]{:S(2)}, u32[]{:S(2)}) %collective-permute-start.21) | collective-permute-done | bytes 20000 | tf_op jit(solution)/shard_map/ppermute | solution.py:213
  159.1 2.2 %collective-permute-done.23 = f32[2,1,2,2,2,1,312]{6,4,3,2,1,0,5:T(2,128)S(1)} collective-permute-done((f32[2,1,2,2,2,1,312]{6,4,3,2,1,0,5:T(2,128)S(1)}, f32[2,1,2,2,2,1,312]{6,4,3,2,1,0,5:T(2,128)S(1)}, u32[]{:S(2)}, u32[]{:S(2)}) %collective-permute-start.23) | collective-permute-done | bytes 20000 | tf_op jit(solution)/shard_map/ppermute | solution.py:213
  161.4 2.6 %collective-permute-start.24 = (f32[1,2,2,2,2,1,312]{6,4,3,2,1,0,5:T(2,128)S(1)}, f32[1,2,2,2,2,1,312]{6,4,3,2,1,0,5:T(2,128)S(1)}, u32[]{:S(2)}, u32[]{:S(2)}) collective-permute-start(f32[1,2,2,2,2,1,312]{6,4,3,2,1,0,5:T(2,128)S(1)} %fusion.83), channel_id=1, source_target_pairs={{0,16},{1,17},{2,18},{3,19},{4,20},{5,21},{6,22},{7,23},{8,24},{9,... | collective-permute-start | bytes 59912 | tf_op jit(solution)/shard_map/ppermute | solution.py:213
  169.5 1.6 collective-permute-start.36
  177.9 3.6 %collective-permute-done.31 = bf16[2,2,2,1,1,48,384]{6,5,4,3,2,1,0:T(8,128)(2,1)S(1)} collective-permute-done((bf16[2,2,2,1,1,48,384]{6,5,4,3,2,1,0:T(8,128)(2,1)S(1)}, bf16[2,2,2,1,1,48,384]{6,5,4,3,2,1,0:T(8,128)(2,1)S(1)}, u32[]{:S(2)}, u32[]{:S(2)}) %collective-permute-start.31) | collective-permute-done | bytes 294944 | tf_op jit(solution)/shard_map/ppermute | solution.py:213
  182.3 2.4 %collective-permute-done.26 = bf16[2,2,2,1,1,48,384]{6,5,4,3,2,1,0:T(8,128)(2,1)S(1)} collective-permute-done((bf16[2,2,2,1,1,48,384]{6,5,4,3,2,1,0:T(8,128)(2,1)S(1)}, bf16[2,2,2,1,1,48,384]{6,5,4,3,2,1,0:T(8,128)(2,1)S(1)}, u32[]{:S(2)}, u32[]{:S(2)}) %collective-permute-start.26) | collective-permute-done | bytes 294944 | tf_op jit(solution)/shard_map/ppermute | solution.py:213
  191.6 1.8 collective-permute-start.39
  194.8 2.1 %collective-permute-start.29 = (bf16[1,1,1,1,1,48,384]{6,5,4,3,2,1,0:T(8,128)(2,1)S(1)}, bf16[1,1,1,1,1,48,384]{6,5,4,3,2,1,0:T(8,128)(2,1)S(1)}, u32[]{:S(2)}, u32[]{:S(2)}) collective-permute-start(bf16[1,1,1,1,1,48,384]{6,5,4,3,2,1,0:T(8,128)(2,1)S(1)} %constant_dynamic-slice_fusion.10), channel_id=1, source_target_pairs={{0,16},{1,17},{2,18},{3,19},{4,20},{5,21},{6,22},{7,23},{8,24},{9,... | collective-permute-start | bytes 110600 | tf_op jit(solution)/shard_map/ppermute | solution.py:213
  (546 shorter events, 117.9 us)
Async XLA Ops:
  0.7 17.1 %collective-permute-start.15 = (bf16[1,1,1,1,1,48,384]{6,5,4,3,2,1,0:T(8,128)(2,1)}, bf16[1,1,1,1,1,48,384]{6,5,4,3,2,1,0:T(8,128)(2,1)S(1)}, u32[]{:S(2)}, u32[]{:S(2)}) collective-permute-start(bf16[1,1,1,1,1,48,384]{6,5,4,3,2,1,0:T(8,128)(2,1)} %bitcast.281), channel_id=1, source_target_pairs={{0,16},{1,17},{2,18},{3,19},{4,20},{5,21},{6,22},{7,23},{8,24},{9,... | collective-permute-start | bytes 110600 | tf_op jit(solution)/shard_map/ppermute | solution.py:213
  4.8 10.7 %collective-permute-start.10 = (bf16[1,1,1,1,1,48,384]{6,5,4,3,2,1,0:T(8,128)(2,1)}, bf16[1,1,1,1,1,48,384]{6,5,4,3,2,1,0:T(8,128)(2,1)S(1)}, u32[]{:S(2)}, u32[]{:S(2)}) collective-permute-start(bf16[1,1,1,1,1,48,384]{6,5,4,3,2,1,0:T(8,128)(2,1)} %bitcast.279), channel_id=1, source_target_pairs={{0,16},{1,17},{2,18},{3,19},{4,20},{5,21},{6,22},{7,23},{8,24},{9,... | collective-permute-start | bytes 110600 | tf_op jit(solution)/shard_map/ppermute | solution.py:213
  4.9 10.6 %collective-permute-start.5 = (bf16[1,1,1,1,1,48,384]{6,5,4,3,2,1,0:T(8,128)(2,1)}, bf16[1,1,1,1,1,48,384]{6,5,4,3,2,1,0:T(8,128)(2,1)S(1)}, u32[]{:S(2)}, u32[]{:S(2)}) collective-permute-start(bf16[1,1,1,1,1,48,384]{6,5,4,3,2,1,0:T(8,128)(2,1)} %bitcast.280), channel_id=1, source_target_pairs={{0,16},{1,17},{2,18},{3,19},{4,20},{5,21},{6,22},{7,23},{8,24},{9,... | collective-permute-start | bytes 110600 | tf_op jit(solution)/shard_map/ppermute | solution.py:213
  9.5 10.3 %collective-permute-start = (bf16[1,1,1,1,1,80,384]{6,5,4,3,2,1,0:T(8,128)(2,1)S(1)}, bf16[1,1,1,1,1,80,384]{6,5,4,3,2,1,0:T(8,128)(2,1)S(1)}, u32[]{:S(2)}, u32[]{:S(2)}) collective-permute-start(bf16[1,1,1,1,1,80,384]{6,5,4,3,2,1,0:T(8,128)(2,1)S(1)} %fusion.80), channel_id=1, source_target_pairs={{0,16},{1,17},{2,18},{3,19},{4,20},{5,21},{6,22},{7,23},{8,24},{9,... | collective-permute-start | bytes 184328 | tf_op jit(solution)/shard_map/ppermute | solution.py:213
  15.6 5.2 %collective-permute-start.6 = (bf16[2,1,1,1,1,48,384]{6,5,4,3,2,1,0:T(8,128)(2,1)S(1)}, bf16[2,1,1,1,1,48,384]{6,5,4,3,2,1,0:T(8,128)(2,1)S(1)}, u32[]{:S(2)}, u32[]{:S(2)}) collective-permute-start(bf16[2,1,1,1,1,48,384]{6,5,4,3,2,1,0:T(8,128)(2,1)S(1)} %pad_maximum_fusion.25), channel_id=1, source_target_pairs={{0,8},{1,9},{2,10},{3,11},{4,12},{5,13},{6,14},{7,15},{8,0},{9,1},... | collective-permute-start | bytes 221192 | tf_op jit(solution)/shard_map/ppermute | solution.py:213
  17.5 5.2 %collective-permute-start.11 = (bf16[2,1,1,1,1,48,384]{6,5,4,3,2,1,0:T(8,128)(2,1)S(1)}, bf16[2,1,1,1,1,48,384]{6,5,4,3,2,1,0:T(8,128)(2,1)S(1)}, u32[]{:S(2)}, u32[]{:S(2)}) collective-permute-start(bf16[2,1,1,1,1,48,384]{6,5,4,3,2,1,0:T(8,128)(2,1)S(1)} %pad_maximum_fusion.26), channel_id=1, source_target_pairs={{0,8},{1,9},{2,10},{3,11},{4,12},{5,13},{6,14},{7,15},{8,0},{9,1},... | collective-permute-start | bytes 221192 | tf_op jit(solution)/shard_map/ppermute | solution.py:213
  17.8 6.6 %collective-permute-start.16 = (bf16[2,1,1,1,1,48,384]{6,5,4,3,2,1,0:T(8,128)(2,1)S(1)}, bf16[2,1,1,1,1,48,384]{6,5,4,3,2,1,0:T(8,128)(2,1)S(1)}, u32[]{:S(2)}, u32[]{:S(2)}) collective-permute-start(bf16[2,1,1,1,1,48,384]{6,5,4,3,2,1,0:T(8,128)(2,1)S(1)} %pad_maximum_fusion.27), channel_id=1, source_target_pairs={{0,8},{1,9},{2,10},{3,11},{4,12},{5,13},{6,14},{7,15},{8,0},{9,1},... | collective-permute-start | bytes 221192 | tf_op jit(solution)/shard_map/ppermute | solution.py:213
  19.9 6.1 %collective-permute-start.1 = (bf16[2,1,1,1,1,80,384]{6,5,4,3,2,1,0:T(8,128)(2,1)S(1)}, bf16[2,1,1,1,1,80,384]{6,5,4,3,2,1,0:T(8,128)(2,1)S(1)}, u32[]{:S(2)}, u32[]{:S(2)}) collective-permute-start(bf16[2,1,1,1,1,80,384]{6,5,4,3,2,1,0:T(8,128)(2,1)S(1)} %pad_maximum_fusion.24), channel_id=1, source_target_pairs={{0,8},{1,9},{2,10},{3,11},{4,12},{5,13},{6,14},{7,15},{8,0},{9,1},... | collective-permute-start | bytes 368648 | tf_op jit(solution)/shard_map/ppermute | solution.py:213
  20.9 6.0 %collective-permute-start.7 = (bf16[2,2,1,1,1,48,384]{6,5,4,3,2,1,0:T(8,128)(2,1)S(1)}, bf16[2,2,1,1,1,48,384]{6,5,4,3,2,1,0:T(8,128)(2,1)S(1)}, u32[]{:S(2)}, u32[]{:S(2)}) collective-permute-start(bf16[2,2,1,1,1,48,384]{6,5,4,3,2,1,0:T(8,128)(2,1)S(1)} %pad_maximum_fusion.21), channel_id=1, source_target_pairs={{0,4},{1,5},{2,6},{3,7},{4,0},{5,1},{6,2},{7,3},{8,12},{9,13},{10,... | collective-permute-start | bytes 442376 | tf_op jit(solution)/shard_map/ppermute | solution.py:213
  22.8 5.5 %collective-permute-start.12 = (bf16[2,2,1,1,1,48,384]{6,5,4,3,2,1,0:T(8,128)(2,1)S(1)}, bf16[2,2,1,1,1,48,384]{6,5,4,3,2,1,0:T(8,128)(2,1)S(1)}, u32[]{:S(2)}, u32[]{:S(2)}) collective-permute-start(bf16[2,2,1,1,1,48,384]{6,5,4,3,2,1,0:T(8,128)(2,1)S(1)} %pad_maximum_fusion.22), channel_id=1, source_target_pairs={{0,4},{1,5},{2,6},{3,7},{4,0},{5,1},{6,2},{7,3},{8,12},{9,13},{10,... | collective-permute-start | bytes 442376 | tf_op jit(solution)/shard_map/ppermute | solution.py:213
  24.4 6.8 %collective-permute-start.17 = (bf16[2,2,1,1,1,48,384]{6,5,4,3,2,1,0:T(8,128)(2,1)S(1)}, bf16[2,2,1,1,1,48,384]{6,5,4,3,2,1,0:T(8,128)(2,1)S(1)}, u32[]{:S(2)}, u32[]{:S(2)}) collective-permute-start(bf16[2,2,1,1,1,48,384]{6,5,4,3,2,1,0:T(8,128)(2,1)S(1)} %pad_maximum_fusion.23), channel_id=1, source_target_pairs={{0,2},{1,3},{2,0},{3,1},{4,6},{5,7},{6,4},{7,5},{8,10},{9,11},{10,... | collective-permute-start | bytes 442376 | tf_op jit(solution)/shard_map/ppermute | solution.py:213
  26.1 10.4 %collective-permute-start.2 = (bf16[2,2,1,1,1,80,384]{6,5,4,3,2,1,0:T(8,128)(2,1)S(1)}, bf16[2,2,1,1,1,80,384]{6,5,4,3,2,1,0:T(8,128)(2,1)S(1)}, u32[]{:S(2)}, u32[]{:S(2)}) collective-permute-start(bf16[2,2,1,1,1,80,384]{6,5,4,3,2,1,0:T(8,128)(2,1)S(1)} %pad_maximum_fusion.16), channel_id=1, source_target_pairs={{0,2},{1,3},{2,0},{3,1},{4,6},{5,7},{6,4},{7,5},{8,10},{9,11},{10,... | collective-permute-start | bytes 737288 | tf_op jit(solution)/shard_map/ppermute | solution.py:213
  26.9 15.7 %collective-permute-start.8 = (bf16[2,2,2,1,1,48,384]{6,5,4,3,2,1,0:T(8,128)(2,1)S(1)}, bf16[2,2,2,1,1,48,384]{6,5,4,3,2,1,0:T(8,128)(2,1)S(1)}, u32[]{:S(2)}, u32[]{:S(2)}) collective-permute-start(bf16[2,2,2,1,1,48,384]{6,5,4,3,2,1,0:T(8,128)(2,1)S(1)} %pad_maximum_fusion.13), channel_id=1, source_target_pairs={{0,2},{1,3},{2,0},{3,1},{4,6},{5,7},{6,4},{7,5},{8,10},{9,11},{10,... | collective-permute-start | bytes 884744 | tf_op jit(solution)/shard_map/ppermute | solution.py:213
  28.4 17.4 %collective-permute-start.13 = (bf16[2,2,2,1,1,48,384]{6,5,4,3,2,1,0:T(8,128)(2,1)S(1)}, bf16[2,2,2,1,1,48,384]{6,5,4,3,2,1,0:T(8,128)(2,1)S(1)}, u32[]{:S(2)}, u32[]{:S(2)}) collective-permute-start(bf16[2,2,2,1,1,48,384]{6,5,4,3,2,1,0:T(8,128)(2,1)S(1)} %pad_maximum_fusion.14), channel_id=1, source_target_pairs={{0,2},{1,3},{2,0},{3,1},{4,6},{5,7},{6,4},{7,5},{8,10},{9,11},{10,... | collective-permute-start | bytes 884744 | tf_op jit(solution)/shard_map/ppermute | solution.py:213
  31.3 14.8 %collective-permute-start.18 = (bf16[2,2,1,2,1,48,384]{6,5,4,3,2,1,0:T(8,128)(2,1)S(1)}, bf16[2,2,1,2,1,48,384]{6,5,4,3,2,1,0:T(8,128)(2,1)S(1)}, u32[]{:S(2)}, u32[]{:S(2)}) collective-permute-start(bf16[2,2,1,2,1,48,384]{6,5,4,3,2,1,0:T(8,128)(2,1)S(1)} %pad_maximum_fusion.15), channel_id=1, source_target_pairs={{0,4},{1,5},{2,6},{3,7},{4,0},{5,1},{6,2},{7,3},{8,12},{9,13},{10,... | collective-permute-start | bytes 884744 | tf_op jit(solution)/shard_map/ppermute | solution.py:213
  36.6 10.2 %collective-permute-start.3 = (bf16[2,2,1,2,1,80,384]{6,5,4,3,2,1,0:T(8,128)(2,1)S(1)}, bf16[2,2,1,2,1,80,384]{6,5,4,3,2,1,0:T(8,128)(2,1)S(1)}, u32[]{:S(2)}, u32[]{:S(2)}) collective-permute-start(bf16[2,2,1,2,1,80,384]{6,5,4,3,2,1,0:T(8,128)(2,1)S(1)} %pad_maximum_fusion.12), channel_id=1, source_target_pairs={{0,4},{1,5},{2,6},{3,7},{4,0},{5,1},{6,2},{7,3},{8,12},{9,13},{10,... | collective-permute-start | bytes 1474568 | tf_op jit(solution)/shard_map/ppermute | solution.py:213
  137.0 31.2 %collective-permute-start.35 = (bf16[2,2,2,2,1,48,384]{6,5,4,3,2,1,0:T(8,128)(2,1)}, bf16[2,2,2,2,1,48,384]{6,5,4,3,2,1,0:T(8,128)(2,1)}, u32[]{:S(2)}, u32[]{:S(2)}) collective-permute-start(bf16[2,2,2,2,1,48,384]{6,5,4,3,2,1,0:T(8,128)(2,1)} %constant_dynamic-slice_fusion.4), channel_id=1, source_target_pairs={{0,1},{1,0},{2,3},{3,2},{4,5},{5,4},{6,7},{7,6},{8,9},{9,8},{10,11... | collective-permute-start | bytes 1769480 | tf_op jit(solution)/shard_map/ppermute | solution.py:213
  142.1 29.0 %collective-permute-start.30 = (bf16[2,2,2,2,1,48,384]{6,5,4,3,2,1,0:T(8,128)(2,1)}, bf16[2,2,2,2,1,48,384]{6,5,4,3,2,1,0:T(8,128)(2,1)}, u32[]{:S(2)}, u32[]{:S(2)}) collective-permute-start(bf16[2,2,2,2,1,48,384]{6,5,4,3,2,1,0:T(8,128)(2,1)} %constant_dynamic-slice_fusion.9), channel_id=1, source_target_pairs={{0,1},{1,0},{2,3},{3,2},{4,5},{5,4},{6,7},{7,6},{8,9},{9,8},{10,11... | collective-permute-start | bytes 1769480 | tf_op jit(solution)/shard_map/ppermute | solution.py:213
  144.1 5.4 %collective-permute-start.20 = (f32[2,2,2,2,1,1,312]{6,4,3,2,1,0,5:T(1,128)S(1)}, f32[2,2,2,2,1,1,312]{6,4,3,2,1,0,5:T(1,128)S(1)}, u32[]{:S(2)}, u32[]{:S(2)}) collective-permute-start(f32[2,2,2,2,1,1,312]{6,4,3,2,1,0,5:T(1,128)S(1)} %constant_dynamic-slice_fusion.15), channel_id=1, source_target_pairs={{0,1},{1,0},{2,3},{3,2},{4,5},{5,4},{6,7},{7,6},{8,9},{9,8},{10,11... | collective-permute-start | bytes 59912 | tf_op jit(solution)/shard_map/ppermute | solution.py:213
  147.6 26.3 %collective-permute-start.25 = (bf16[2,2,2,2,1,48,384]{6,5,4,3,2,1,0:T(8,128)(2,1)}, bf16[2,2,2,2,1,48,384]{6,5,4,3,2,1,0:T(8,128)(2,1)}, u32[]{:S(2)}, u32[]{:S(2)}) collective-permute-start(bf16[2,2,2,2,1,48,384]{6,5,4,3,2,1,0:T(8,128)(2,1)} %constant_dynamic-slice_fusion.14), channel_id=1, source_target_pairs={{0,1},{1,0},{2,3},{3,2},{4,5},{5,4},{6,7},{7,6},{8,9},{9,8},{10,11... | collective-permute-start | bytes 1769480 | tf_op jit(solution)/shard_map/ppermute | solution.py:213
  161.4 5.1 %collective-permute-start.24 = (f32[1,2,2,2,2,1,312]{6,4,3,2,1,0,5:T(2,128)S(1)}, f32[1,2,2,2,2,1,312]{6,4,3,2,1,0,5:T(2,128)S(1)}, u32[]{:S(2)}, u32[]{:S(2)}) collective-permute-start(f32[1,2,2,2,2,1,312]{6,4,3,2,1,0,5:T(2,128)S(1)} %fusion.83), channel_id=1, source_target_pairs={{0,16},{1,17},{2,18},{3,19},{4,20},{5,21},{6,22},{7,23},{8,24},{9,... | collective-permute-start | bytes 59912 | tf_op jit(solution)/shard_map/ppermute | solution.py:213
  169.5 6.8 %collective-permute-start.36 = (bf16[2,2,1,2,1,48,384]{6,5,4,3,2,1,0:T(8,128)(2,1)S(1)}, bf16[2,2,1,2,1,48,384]{6,5,4,3,2,1,0:T(8,128)(2,1)S(1)}, u32[]{:S(2)}, u32[]{:S(2)}) collective-permute-start(bf16[2,2,1,2,1,48,384]{6,5,4,3,2,1,0:T(8,128)(2,1)S(1)} %constant_dynamic-slice_fusion.3), channel_id=1, source_target_pairs={{0,4},{1,5},{2,6},{3,7},{4,0},{5,1},{6,2},{7,3},{8,12},{9,13},{10,... | collective-permute-start | bytes 884744 | tf_op jit(solution)/shard_map/ppermute | solution.py:213
  172.3 9.2 %collective-permute-start.31 = (bf16[2,2,2,1,1,48,384]{6,5,4,3,2,1,0:T(8,128)(2,1)S(1)}, bf16[2,2,2,1,1,48,384]{6,5,4,3,2,1,0:T(8,128)(2,1)S(1)}, u32[]{:S(2)}, u32[]{:S(2)}) collective-permute-start(bf16[2,2,2,1,1,48,384]{6,5,4,3,2,1,0:T(8,128)(2,1)S(1)} %constant_dynamic-slice_fusion.8), channel_id=1, source_target_pairs={{0,2},{1,3},{2,0},{3,1},{4,6},{5,7},{6,4},{7,5},{8,10},{9,11},{10,... | collective-permute-start | bytes 884744 | tf_op jit(solution)/shard_map/ppermute | solution.py:213
  175.2 9.6 %collective-permute-start.26 = (bf16[2,2,2,1,1,48,384]{6,5,4,3,2,1,0:T(8,128)(2,1)S(1)}, bf16[2,2,2,1,1,48,384]{6,5,4,3,2,1,0:T(8,128)(2,1)S(1)}, u32[]{:S(2)}, u32[]{:S(2)}) collective-permute-start(bf16[2,2,2,1,1,48,384]{6,5,4,3,2,1,0:T(8,128)(2,1)S(1)} %constant_dynamic-slice_fusion.13), channel_id=1, source_target_pairs={{0,2},{1,3},{2,0},{3,1},{4,6},{5,7},{6,4},{7,5},{8,10},{9,11},{10,... | collective-permute-start | bytes 884744 | tf_op jit(solution)/shard_map/ppermute | solution.py:213
  176.4 9.9 %collective-permute-start.37 = (bf16[2,2,1,1,1,48,384]{6,5,4,3,2,1,0:T(8,128)(2,1)S(1)}, bf16[2,2,1,1,1,48,384]{6,5,4,3,2,1,0:T(8,128)(2,1)S(1)}, u32[]{:S(2)}, u32[]{:S(2)}) collective-permute-start(bf16[2,2,1,1,1,48,384]{6,5,4,3,2,1,0:T(8,128)(2,1)S(1)} %constant_dynamic-slice_fusion.2), channel_id=1, source_target_pairs={{0,2},{1,3},{2,0},{3,1},{4,6},{5,7},{6,4},{7,5},{8,10},{9,11},{10,... | collective-permute-start | bytes 442376 | tf_op jit(solution)/shard_map/ppermute | solution.py:213
  181.7 5.4 %collective-permute-start.32 = (bf16[2,2,1,1,1,48,384]{6,5,4,3,2,1,0:T(8,128)(2,1)S(1)}, bf16[2,2,1,1,1,48,384]{6,5,4,3,2,1,0:T(8,128)(2,1)S(1)}, u32[]{:S(2)}, u32[]{:S(2)}) collective-permute-start(bf16[2,2,1,1,1,48,384]{6,5,4,3,2,1,0:T(8,128)(2,1)S(1)} %constant_dynamic-slice_fusion.7), channel_id=1, source_target_pairs={{0,4},{1,5},{2,6},{3,7},{4,0},{5,1},{6,2},{7,3},{8,12},{9,13},{10,... | collective-permute-start | bytes 442376 | tf_op jit(solution)/shard_map/ppermute | solution.py:213
  184.8 5.2 %collective-permute-start.27 = (bf16[2,2,1,1,1,48,384]{6,5,4,3,2,1,0:T(8,128)(2,1)S(1)}, bf16[2,2,1,1,1,48,384]{6,5,4,3,2,1,0:T(8,128)(2,1)S(1)}, u32[]{:S(2)}, u32[]{:S(2)}) collective-permute-start(bf16[2,2,1,1,1,48,384]{6,5,4,3,2,1,0:T(8,128)(2,1)S(1)} %constant_dynamic-slice_fusion.12), channel_id=1, source_target_pairs={{0,4},{1,5},{2,6},{3,7},{4,0},{5,1},{6,2},{7,3},{8,12},{9,13},{10,... | collective-permute-start | bytes 442376 | tf_op jit(solution)/shard_map/ppermute | solution.py:213
  186.4 5.2 %collective-permute-start.38 = (bf16[2,1,1,1,1,48,384]{6,5,4,3,2,1,0:T(8,128)(2,1)S(1)}, bf16[2,1,1,1,1,48,384]{6,5,4,3,2,1,0:T(8,128)(2,1)S(1)}, u32[]{:S(2)}, u32[]{:S(2)}) collective-permute-start(bf16[2,1,1,1,1,48,384]{6,5,4,3,2,1,0:T(8,128)(2,1)S(1)} %constant_dynamic-slice_fusion.1), channel_id=1, source_target_pairs={{0,8},{1,9},{2,10},{3,11},{4,12},{5,13},{6,14},{7,15},{8,0},{9,1},... | collective-permute-start | bytes 221192 | tf_op jit(solution)/shard_map/ppermute | solution.py:213
  187.2 6.2 %collective-permute-start.33 = (bf16[2,1,1,1,1,48,384]{6,5,4,3,2,1,0:T(8,128)(2,1)S(1)}, bf16[2,1,1,1,1,48,384]{6,5,4,3,2,1,0:T(8,128)(2,1)S(1)}, u32[]{:S(2)}, u32[]{:S(2)}) collective-permute-start(bf16[2,1,1,1,1,48,384]{6,5,4,3,2,1,0:T(8,128)(2,1)S(1)} %constant_dynamic-slice_fusion.6), channel_id=1, source_target_pairs={{0,8},{1,9},{2,10},{3,11},{4,12},{5,13},{6,14},{7,15},{8,0},{9,1},... | collective-permute-start | bytes 221192 | tf_op jit(solution)/shard_map/ppermute | solution.py:213
  191.6 5.3 %collective-permute-start.39 = (bf16[1,1,1,1,1,48,384]{6,5,4,3,2,1,0:T(8,128)(2,1)S(1)}, bf16[1,1,1,1,1,48,384]{6,5,4,3,2,1,0:T(8,128)(2,1)S(1)}, u32[]{:S(2)}, u32[]{:S(2)}) collective-permute-start(bf16[1,1,1,1,1,48,384]{6,5,4,3,2,1,0:T(8,128)(2,1)S(1)} %constant_dynamic-slice_fusion), channel_id=1, source_target_pairs={{0,16},{1,17},{2,18},{3,19},{4,20},{5,21},{6,22},{7,23},{8,24},{9,... | collective-permute-start | bytes 110600 | tf_op jit(solution)/shard_map/ppermute | solution.py:213
  193.4 4.9 %collective-permute-start.34 = (bf16[1,1,1,1,1,48,384]{6,5,4,3,2,1,0:T(8,128)(2,1)S(1)}, bf16[1,1,1,1,1,48,384]{6,5,4,3,2,1,0:T(8,128)(2,1)S(1)}, u32[]{:S(2)}, u32[]{:S(2)}) collective-permute-start(bf16[1,1,1,1,1,48,384]{6,5,4,3,2,1,0:T(8,128)(2,1)S(1)} %constant_dynamic-slice_fusion.5), channel_id=1, source_target_pairs={{0,16},{1,17},{2,18},{3,19},{4,20},{5,21},{6,22},{7,23},{8,24},{9,... | collective-permute-start | bytes 110600 | tf_op jit(solution)/shard_map/ppermute | solution.py:213
  194.8 5.3 %collective-permute-start.29 = (bf16[1,1,1,1,1,48,384]{6,5,4,3,2,1,0:T(8,128)(2,1)S(1)}, bf16[1,1,1,1,1,48,384]{6,5,4,3,2,1,0:T(8,128)(2,1)S(1)}, u32[]{:S(2)}, u32[]{:S(2)}) collective-permute-start(bf16[1,1,1,1,1,48,384]{6,5,4,3,2,1,0:T(8,128)(2,1)S(1)} %constant_dynamic-slice_fusion.10), channel_id=1, source_target_pairs={{0,16},{1,17},{2,18},{3,19},{4,20},{5,21},{6,22},{7,23},{8,24},{9,... | collective-permute-start | bytes 110600 | tf_op jit(solution)/shard_map/ppermute | solution.py:213
  (145 other events, 707.6 us)

commit v2 on v1

v2 whole, which is shorter than its diff:
```python
import functools
import math

import jax
import jax.numpy as jnp
from jax import lax
from jax.experimental import pallas as pl
from jax.experimental.pallas import tpu as pltpu
from jax.sharding import PartitionSpec as P

HEADS = 6

CHUNK = 512

NORM_EPS = 1e-06


def product(form, left, right):
    return jnp.einsum(form, left, right, preferred_element_type=jnp.float32)


def dot_nn(left, right):
    return lax.dot_general(left, right, (((1,), (0,)), ((), ())), preferred_element_type=jnp.float32)


def dot_nt(left, right):
    return lax.dot_general(left, right, (((1,), (1,)), ((), ())), preferred_element_type=jnp.float32)


def dot_tn(left, right):
    return lax.dot_general(left, right, (((0,), (0,)), ((), ())), preferred_element_type=jnp.float32)


def layer_norm(values):
    center = values - jnp.mean(values, axis=-1, keepdims=True)
    inv_std = lax.rsqrt(jnp.mean(center * center, axis=-1, keepdims=True) + NORM_EPS)
    return (center * inv_std, inv_std)


def norm_back(grad_norm, normed, inv_std):
    return inv_std * (
        grad_norm
        - jnp.mean(grad_norm, axis=-1, keepdims=True)
        - normed * jnp.mean(grad_norm * normed, axis=-1, keepdims=True)
    )


def token_sum(values):
    return jnp.sum(values, axis=0, keepdims=True)


def pair_masks(rows, pair_w):
    lane = lax.broadcasted_iota(jnp.int32, (rows, pair_w), 1)
    return (lane < pair_w // 2, lane >= pair_w // 2)


def attend_kernel(batches, x_ref, mod_ref, w_ref, bias_ref, h_ref, qkv_ref, p_ref, ctx_ref, ao_ref, mid_ref):
    tokens_n, width_n = x_ref.shape[0] // batches, x_ref.shape[1]
    pair_w = 2 * (width_n // HEADS)
    scaling = 1.0 / math.sqrt(width_n // HEADS)
    for b in range(batches):
        rows = pl.ds(b * tokens_n, tokens_n)
        normed, _ = layer_norm(x_ref[rows, :])
        shift = mod_ref[b, 0:1, :]
        scale = mod_ref[b, 1:2, :]
        h_ref[rows, :] = (normed * (1.0 + scale) + shift).astype(jnp.bfloat16)
    for part, bias_row in ((0, 6), (1, None), (2, 7)):
        cols = pl.ds(part * width_n, width_n)
        value = dot_nt(h_ref[...], w_ref[cols, :])
        if bias_row is not None:
            value = value + bias_ref[bias_row : bias_row + 1, :]
        qkv_ref[:, cols] = value.astype(jnp.bfloat16)
    masks = pair_masks(tokens_n, pair_w)
    for b in range(batches):
        rows = pl.ds(b * tokens_n, tokens_n)
        for pair in range(HEADS // 2):
            q_pair = qkv_ref[rows, pl.ds(pair * pair_w, pair_w)]
            k_pair = qkv_ref[rows, pl.ds(width_n + pair * pair_w, pair_w)]
            v_pair = qkv_ref[rows, pl.ds(2 * width_n + pair * pair_w, pair_w)]
            found = []
            for side in range(2):
                q_one = jnp.where(masks[side], q_pair, jnp.zeros_like(q_pair)) * jnp.bfloat16(scaling)
                scores = dot_nt(q_one, k_pair)
                expd = jnp.exp(scores - jnp.max(scores, axis=-1, keepdims=True))
                share = 1.0 / jnp.sum(expd, axis=-1, keepdims=True)
                probs = (expd * share).astype(jnp.bfloat16)
                p_ref[b * HEADS + 2 * pair + side] = probs
                found.append(dot_nn(probs, v_pair))
            ctx_ref[rows, pl.ds(pair * pair_w, pair_w)] = jnp.where(masks[0], *found).astype(jnp.bfloat16)
    attn_out = dot_nt(ctx_ref[...], w_ref[pl.ds(3 * width_n, width_n), :]) + bias_ref[8:9, :]
    ao_ref[...] = attn_out
    for b in range(batches):
        rows = pl.ds(b * tokens_n, tokens_n)
        mid_ref[rows, :] = x_ref[rows, :] + mod_ref[b, 2:3, :] * ao_ref[rows, :]


def mlp_kernel(
    batches, live_ref, mid_ref, grad_ref, mod_ref, bias_ref, b_in_ref, w_in_ref, w_out_ref,
    out_ref, dmid_ref, g_in_ref, g_out_ref, gb_in_ref, gb_out_ref, dmod_ref,
    h_ref, dmlp_ref, mlp_ref, dh_ref,
):
    step = pl.program_id(0)
    tokens_n, width_n = mid_ref.shape[0] // batches, mid_ref.shape[1]

    @pl.when(step == 0)
    def _():
        total = jnp.zeros((1, width_n), jnp.float32)
        for b in range(batches):
            rows = pl.ds(b * tokens_n, tokens_n)
            normed, _ = layer_norm(mid_ref[rows, :])
            h_ref[rows, :] = (normed * (1.0 + mod_ref[b, 4:5, :]) + mod_ref[b, 3:4, :]).astype(jnp.bfloat16)
            d_mlp = mod_ref[b, 5:6, :] * (live_ref[b].astype(jnp.float32) * grad_ref[rows, :])
            total = total + token_sum(d_mlp)
            dmlp_ref[rows, :] = d_mlp.astype(jnp.bfloat16)
        gb_out_ref[...] = total
        mlp_ref[...] = jnp.zeros_like(mlp_ref)
        dh_ref[...] = jnp.zeros_like(dh_ref)

    pre = dot_nt(h_ref[...], w_in_ref[...]) + b_in_ref[...]
    root = math.sqrt(2.0 / math.pi)
    square = pre * pre
    tanh = jnp.tanh(root * (pre + 0.044715 * (square * pre)))
    half = 0.5 * (1.0 + tanh)
    act = (pre * half).astype(jnp.bfloat16)
    slope = half + (0.5 * pre) * (1.0 - tanh * tanh) * (root + (3.0 * 0.044715 * root) * square)
    d_pre = dot_nt(dmlp_ref[...], w_out_ref[...]) * slope
    mlp_ref[...] += dot_nn(act, w_out_ref[...])
    g_out_ref[...] = dot_tn(act, dmlp_ref[...]).astype(jnp.bfloat16)
    gb_in_ref[...] = token_sum(d_pre)
    d_pre_b = d_pre.astype(jnp.bfloat16)
    dh_ref[...] += dot_nn(d_pre_b, w_in_ref[...])
    g_in_ref[...] = dot_tn(d_pre_b, h_ref[...]).astype(jnp.bfloat16)

    @pl.when(step == pl.num_programs(0) - 1)
    def _():
        for b in range(batches):
            rows = pl.ds(b * tokens_n, tokens_n)
            live = live_ref[b].astype(jnp.float32)
            middle = mid_ref[rows, :]
            d_y = live * grad_ref[rows, :]
            mlp_out = mlp_ref[rows, :] + bias_ref[13:14, :]
            out_ref[rows, :] = live * (middle + mod_ref[b, 5:6, :] * mlp_out)
            normed, inv_std = layer_norm(middle)
            d_h = dh_ref[rows, :]
            dmod_ref[b, 0:1, :] = token_sum(d_h)
            dmod_ref[b, 1:2, :] = token_sum(d_h * normed)
            dmod_ref[b, 2:3, :] = token_sum(d_y * mlp_out)
            dmid_ref[rows, :] = d_y + norm_back(d_h * (1.0 + mod_ref[b, 4:5, :]), normed, inv_std)


def attend_back_kernel(
    batches, x_ref, mod_ref, w_ref, h_ref, qkv_ref, p_ref, ctx_ref, ao_ref, dmid_ref,
    dx_ref, g_ref, gb_ref, dmod_ref, dattn_ref, dctx_ref, dqkv_ref,
):
    tokens_n, width_n = x_ref.shape[0] // batches, x_ref.shape[1]
    pair_w = 2 * (width_n // HEADS)
    scaling = 1.0 / math.sqrt(width_n // HEADS)
    total = jnp.zeros((1, width_n), jnp.float32)
    for b in range(batches):
        rows = pl.ds(b * tokens_n, tokens_n)
        d_mid = dmid_ref[rows, :]
        dmod_ref[b, 2:3, :] = token_sum(d_mid * ao_ref[rows, :])
        d_attn = mod_ref[b, 2:3, :] * d_mid
        total = total + token_sum(d_attn)
        dattn_ref[rows, :] = d_attn.astype(jnp.bfloat16)
    gb_ref[2:3, :] = total
    dctx_ref[...] = dot_nn(dattn_ref[...], w_ref[pl.ds(3 * width_n, width_n), :]).astype(jnp.bfloat16)
    g_ref[pl.ds(3 * width_n, width_n), :] = dot_tn(dattn_ref[...], ctx_ref[...]).astype(jnp.bfloat16)
    masks = pair_masks(tokens_n, pair_w)
    for pair in range(HEADS // 2):
        cols = pl.ds(pair * pair_w, pair_w)
        q_total = jnp.zeros((1, pair_w), jnp.float32)
        v_total = jnp.zeros((1, pair_w), jnp.float32)
        for b in range(batches):
            rows = pl.ds(b * tokens_n, tokens_n)
            q_pair = qkv_ref[rows, cols]
            k_pair = qkv_ref[rows, pl.ds(width_n + pair * pair_w, pair_w)]
            v_pair = qkv_ref[rows, pl.ds(2 * width_n + pair * pair_w, pair_w)]
            dc_pair = dctx_ref[rows, cols]
            d_q, d_k, d_v = [], [], []
            for side in range(2):
                probs_b = p_ref[b * HEADS + 2 * pair + side]
                probs = probs_b.astype(jnp.float32)
                dc_one = jnp.where(masks[side], dc_pair, jnp.zeros_like(dc_pair))
                d_probs = dot_nt(dc_one, v_pair)
                row_dot = jnp.sum(probs * d_probs, axis=-1, keepdims=True)
                d_scores = (probs * (d_probs - row_dot)).astype(jnp.bfloat16)
                d_v.append(dot_tn(probs_b, dc_pair))
                d_q.append(dot_nn(d_scores, k_pair))
                d_k.append(dot_tn(d_scores, q_pair))
            d_query = jnp.where(masks[0], *d_q) * scaling
            d_key = jnp.where(masks[0], *d_k) * scaling
            d_value = jnp.where(masks[0], *d_v)
            q_total = q_total + token_sum(d_query)
            v_total = v_total + token_sum(d_value)
            dqkv_ref[rows, cols] = d_query.astype(jnp.bfloat16)
            dqkv_ref[rows, pl.ds(width_n + pair * pair_w, pair_w)] = d_key.astype(jnp.bfloat16)
            dqkv_ref[rows, pl.ds(2 * width_n + pair * pair_w, pair_w)] = d_value.astype(jnp.bfloat16)
        gb_ref[0:1, cols] = q_total
        gb_ref[1:2, cols] = v_total
    for part in range(3):
        cols = pl.ds(part * width_n, width_n)
        g_ref[cols, :] = dot_tn(dqkv_ref[:, cols], h_ref[...]).astype(jnp.bfloat16)
    d_h_all = dot_nn(dqkv_ref[...], w_ref[pl.ds(0, 3 * width_n), :])
    for b in range(batches):
        rows = pl.ds(b * tokens_n, tokens_n)
        normed, inv_std = layer_norm(x_ref[rows, :])
        d_h = d_h_all[b * tokens_n : (b + 1) * tokens_n]
        dmod_ref[b, 0:1, :] = token_sum(d_h)
        dmod_ref[b, 1:2, :] = token_sum(d_h * normed)
        dx_ref[rows, :] = dmid_ref[rows, :] + norm_back(d_h * (1.0 + mod_ref[b, 1:2, :]), normed, inv_std)


def shaped(shape, dtype):
    return jax.ShapeDtypeStruct(shape, dtype)


def attend(x_rows, mods, weight, bias_rows):
    batches = mods.shape[0]
    total_n, width_n = x_rows.shape
    tokens_n = total_n // batches
    return pl.pallas_call(
        functools.partial(attend_kernel, batches),
        out_shape=(
            shaped((total_n, width_n), jnp.bfloat16),
            shaped((total_n, 3 * width_n), jnp.bfloat16),
            shaped((batches * HEADS, tokens_n, tokens_n), jnp.bfloat16),
            shaped((total_n, width_n), jnp.bfloat16),
            shaped((total_n, width_n), jnp.float32),
            shaped((total_n, width_n), jnp.float32),
        ),
        name="attend",
    )(x_rows, mods, weight, bias_rows)


def mlp(live_flags, middle, grad_rows, mods, bias_rows, bias_in, w_in, w_out):
    batches = mods.shape[0]
    total_n, width_n = middle.shape
    hidden = w_in.shape[0]
    chunk = CHUNK
    whole = lambda *shape: pl.BlockSpec(shape, lambda i: (0,) * len(shape))
    part = pl.BlockSpec((chunk, width_n), lambda i: (i, 0))
    line = pl.BlockSpec((1, chunk), lambda i: (0, i))
    return pl.pallas_call(
        functools.partial(mlp_kernel, batches),
        grid=(hidden // chunk,),
        in_specs=[
            pl.BlockSpec(memory_space=pltpu.SMEM),
            whole(total_n, width_n),
            whole(total_n, width_n),
            whole(*mods.shape),
            whole(*bias_rows.shape),
            line,
            part,
            part,
        ],
        out_specs=(
            whole(total_n, width_n),
            whole(total_n, width_n),
            part,
            part,
            line,
            whole(1, width_n),
            whole(batches, 3, width_n),
        ),
        out_shape=(
            shaped((total_n, width_n), jnp.float32),
            shaped((total_n, width_n), jnp.float32),
            shaped((hidden, width_n), jnp.bfloat16),
            shaped((hidden, width_n), jnp.bfloat16),
            shaped((1, hidden), jnp.float32),
            shaped((1, width_n), jnp.float32),
            shaped((batches, 3, width_n), jnp.float32),
        ),
        scratch_shapes=[
            pltpu.VMEM((total_n, width_n), jnp.bfloat16),
            pltpu.VMEM((total_n, width_n), jnp.bfloat16),
            pltpu.VMEM((total_n, width_n), jnp.float32),
            pltpu.VMEM((total_n, width_n), jnp.float32),
        ],
        name="mlp",
    )(live_flags, middle, grad_rows, mods, bias_rows, bias_in, w_in, w_out)


def attend_back(x_rows, mods, weight, kept, d_mid):
    batches = mods.shape[0]
    total_n, width_n = x_rows.shape
    return pl.pallas_call(
        functools.partial(attend_back_kernel, batches),
        out_shape=(
            shaped((total_n, width_n), jnp.float32),
            shaped((4 * width_n, width_n), jnp.bfloat16),
            shaped((3, width_n), jnp.float32),
            shaped((batches, 3, width_n), jnp.float32),
        ),
        scratch_shapes=[
            pltpu.VMEM((total_n, width_n), jnp.bfloat16),
            pltpu.VMEM((total_n, width_n), jnp.bfloat16),
            pltpu.VMEM((total_n, 3 * width_n), jnp.bfloat16),
        ],
        name="attend_back",
    )(x_rows, mods, weight, *kept, d_mid)


def gather_orders(count):
    high = list(range(count - 1, 2, -1))
    near = [k for k in (2, 1) if k < count]
    return high + near + [0], high + near[::-1] + [0]


def exchange(value, bit_idx, group_n):
    return lax.ppermute(value, "fsdp", [(dev, dev ^ (1 << bit_idx)) for dev in range(group_n)])


def own_bit(bit_idx):
    return (lax.axis_index("fsdp") >> bit_idx) & 1


def gather_blocks(block, order):
    count = len(order)
    cur = block.reshape((1,) * count + block.shape)
    for bit_idx in order:
        other = exchange(cur, bit_idx, 1 << count)
        upper = own_bit(bit_idx) == 1
        cur = jnp.concatenate(
            [jnp.where(upper, other, cur), jnp.where(upper, cur, other)], axis=count - 1 - bit_idx
        )
    return cur


def scatter_sum(blocks, order):
    count = len(order)
    cur = blocks
    for step, bit_idx in enumerate(order):
        axis = count - 1 - bit_idx
        mine = own_bit(bit_idx)
        other = exchange(
            lax.dynamic_index_in_dim(cur, 1 - mine, axis, keepdims=True), bit_idx, 1 << count
        )
        kept = lax.dynamic_index_in_dim(cur, mine, axis, keepdims=True)
        total = kept.astype(jnp.float32) + other.astype(jnp.float32)
        cur = total if step == count - 1 else total.astype(jnp.bfloat16)
    return cur.reshape(blocks.shape[count:])


def swap_blocks(blocks, order):
    count = len(order)
    cur = blocks
    for bit_idx in order:
        axis = count - 1 - bit_idx
        mine = own_bit(bit_idx)
        other = exchange(
            lax.dynamic_index_in_dim(cur, 1 - mine, axis, keepdims=True), bit_idx, 1 << count
        )
        kept = lax.dynamic_index_in_dim(cur, mine, axis, keepdims=True)
        upper = mine == 1
        cur = jnp.concatenate(
            [jnp.where(upper, other, kept), jnp.where(upper, kept, other)], axis=axis
        )
    return cur


def local(inputs, cond, live, ada_w, attn_w, fc1_w, fc2_w, biases, grad_out):
    group_n = lax.axis_size("fsdp")
    count = group_n.bit_length() - 1
    first, second = gather_orders(count)
    width_n = attn_w.shape[2]
    batches = inputs.shape[0]
    own_ada, own_bias = ada_w.shape[1], biases.shape[1]
    cond_rows = cond[:, 0]
    sigmoid_c = jax.nn.sigmoid(cond_rows)
    sc_own = (cond_rows * sigmoid_c).astype(jnp.bfloat16)
    bias_line = jnp.pad(biases, ((0, 0), (0, width_n - own_bias)))
    side_rows = own_ada + 1 + batches
    pad_rows = -side_rows % 16
    side = jnp.concatenate(
        [ada_w[0], bias_line, sc_own, jnp.zeros((pad_rows, width_n), jnp.bfloat16)], axis=0
    )
    side_all = gather_blocks(side, second).reshape(group_n, side_rows + pad_rows, width_n)
    attn_all = gather_blocks(attn_w[0], first).reshape(-1, width_n)
    fc1_all = gather_blocks(fc1_w[0], first).reshape(-1, width_n)
    fc2_all = gather_blocks(fc2_w[0], second).reshape(-1, width_n)
    ada_all = side_all[:, :own_ada].reshape(-1, width_n)
    bias_rows = side_all[:, own_ada, :own_bias].reshape(-1, width_n).astype(jnp.float32)
    sc_all = side_all[:, own_ada + 1 : own_ada + 1 + batches]
    hidden = fc1_all.shape[0]
    mods = product("ed,bd->be", ada_all, sc_own).reshape(batches, 6, width_n) + bias_rows[:6]
    x_rows = inputs.reshape(-1, width_n)
    h_in, qkv, probs, context, attn_out, middle = attend(x_rows, mods, attn_all, bias_rows)
    out, d_mid, g_fc1, g_fc2, gb_in, gb_out, dmod_b = mlp(
        live[:, 0],
        middle,
        grad_out.reshape(-1, width_n),
        mods,
        bias_rows,
        bias_rows[9:13].reshape(1, hidden),
        fc1_all,
        fc2_all,
    )
    d_x, g_attn, gb_attn, dmod_a = attend_back(
        x_rows, mods, attn_all, (h_in, qkv, probs, context, attn_out), d_mid
    )
    d_mods = jnp.concatenate([dmod_a, dmod_b], axis=1)
    d_sc = jnp.einsum(
        "be,ed->bd",
        d_mods.reshape(batches, -1),
        ada_all.astype(jnp.float32),
        precision=lax.Precision.HIGHEST,
    )
    d_cond = d_sc * sigmoid_c * (1.0 + cond_rows * (1.0 - sigmoid_c))
    g_bias = jnp.concatenate(
        [jnp.sum(d_mods, axis=0), gb_attn, gb_in.reshape(-1, width_n), gb_out], axis=0
    )
    cube = (2,) * count
    sums = [
        scatter_sum(value.reshape(cube + (-1, width_n)), order[::-1])
        for value, order in ((g_attn, first), (g_fc1, first), (g_fc2, second))
    ]
    mod_blocks = d_mods.reshape(batches, group_n, own_ada)
    side_grads = jnp.concatenate(
        [mod_blocks[idx] for idx in range(batches)] + [g_bias.reshape(group_n, own_bias)], axis=1
    )
    swapped = swap_blocks(side_grads.reshape(cube + (1, -1)), second[::-1]).reshape(group_n, -1)
    own_mods = swapped[:, : batches * own_ada].reshape(group_n * batches, own_ada)
    d_bias = jnp.sum(swapped[:, batches * own_ada :], axis=0)
    d_ada = jnp.einsum(
        "kr,kd->rd",
        own_mods,
        sc_all.reshape(group_n * batches, width_n).astype(jnp.float32),
        precision=lax.Precision.HIGHEST,
    )
    return (
        out.reshape(inputs.shape),
        d_x.reshape(inputs.shape),
        d_cond[:, None],
        d_ada[None],
        sums[0][None],
        sums[1][None],
        sums[2][None],
        d_bias[None],
    )


def solution(mesh):
    return jax.shard_map(
        local,
        mesh=mesh,
        in_specs=(
            P(None, "fsdp", None, None),
            P(None, "fsdp", None),
            P(None, "fsdp"),
            P(None, "fsdp", None),
            P(None, "fsdp", None),
            P(None, "fsdp", None),
            P(None, "fsdp", None),
            P(None, "fsdp"),
            P(None, "fsdp", None, None),
        ),
        out_specs=(
            P(None, "fsdp", None, None),
            P(None, "fsdp", None, None),
            P(None, "fsdp", None),
            P(None, "fsdp", None),
            P(None, "fsdp", None),
            P(None, "fsdp", None),
            P(None, "fsdp", None),
            P(None, "fsdp"),
        ),
        check_vma=False,
    )
```

time: 202 us -> 150 us (0.74)
  matrix products: 49.9 us -> 3.08 us
  local copies, waits for them, and re-layouts: 44.3 us -> 14.5 us
  Pallas kernels: 0 us -> 26.8 us
  between operations: 4.18 us -> 1.35 us
  waiting for transfers between devices: 33.2 us -> 35.4 us
    dot_general x38 -> x1, matrix products: 47.3 us -> 0.56 us  [product(): return jnp.einsum(form, left, right, preferred_element_type=jnp.float32)]
    pallas_call x0 -> x3, Pallas kernels: none -> 26.8 us  [the longest x1 11.1 us: mlp(): pl.pallas_call(functools.partial(mlp_kernel, batches), grid=(hidden // ch...]
    unnamed x294 -> x30, local copies, waits for them, and re-layouts: 24.8 us -> 2.53 us
    slice x13 -> x4, local copies, waits for them, and re-layouts: 7.19 us -> 1.83 us  [the longest x1 1.66 us: local(): ada_all = side_all[:, :own_ada].reshape(-1, width_n)]
    concatenate x6 -> x3, local copies, waits for them, and re-layouts: 4.12 us -> 0.29 us  [local(): jnp.concatenate([mod_blocks[idx] for idx in range(batches)] + [g_bias.res...]
    reduce_sum x7 -> x1, other arithmetic: 4.29 us -> 1.33 us  [local(): jnp.sum(d_mods, axis=0)]
    another operation x4 -> x0, other arithmetic: 2.85 us -> none  [the longest x2 1.34 us: local(): jnp.stack(d_in_rows)]
    select_n x19, other arithmetic: 1.47 us -> 3.85 us  [gather_blocks(): jnp.where(upper, other, cur)]
  transfers between devices with their start and end apart: 40 -> 40, of which waited for: 19 -> 22; matrix products, arithmetic and copies ran while one was open for 15% -> 22% of each run, Pallas kernels for 0% -> 0%
where the time goes in v2:
time: 150 us; the launch traced here: 148 us
  starting transfers between devices  43.2 us (29%)
  waiting for transfers between devices  35.4 us (24%)
  Pallas kernels  26.8 us (18%)
  other arithmetic  24 us (16%)
  local copies, waits for them, and re-layouts  14.5 us (10%)
  matrix products  3.08 us (2%)
    ppermute x40, starting transfers between devices, exchange(): lax.ppermute(value, 'fsdp', [(dev, dev ^ 1 << bit_idx) for dev in range(g...  43.2 us
    ppermute x40, waiting for transfers between devices, exchange(): lax.ppermute(value, 'fsdp', [(dev, dev ^ 1 << bit_idx) for dev in range(g...  35.4 us
    pallas_call x1, Pallas kernels, mlp(): pl.pallas_call(functools.partial(mlp_kernel, batches), grid=(hidden // ch...  11.1 us
    pallas_call x1, Pallas kernels, attend_back(): pl.pallas_call(functools.partial(attend_back_kernel, batches), out_shape=...  9.6 us
    pallas_call x1, Pallas kernels, attend(): pl.pallas_call(functools.partial(attend_kernel, batches), out_shape=(shap...  6.17 us
    concatenate x20, other arithmetic, gather_blocks(): jnp.concatenate([jnp.where(upper, other, cur), jnp.where(upper, cur, othe...  4.45 us
    convert_element_type x12, other arithmetic, scatter_sum(): cur = total if step == count - 1 else total.astype(jnp.bfloat16)  4.18 us
    select_n x19, other arithmetic, gather_blocks(): jnp.where(upper, other, cur)  3.85 us
  transfers between devices with their start and end apart: 40, of which 22 were waited for; matrix products, arithmetic and copies ran while one was open for 22% of the time, Pallas kernels for 0%

profile of v2, /device:TPU:0, one launch (start us, length us, event | category | flops | bytes accessed | tf_op | source)
XLA Modules:
  0.0 148.5 jit_solution(949175257018638890)
XLA Ops:
  0.6 4.1 %collective-permute-start.15 = (bf16[1,1,1,1,1,48,384]{6,5,4,3,2,1,0:T(8,128)(2,1)}, bf16[1,1,1,1,1,48,384]{6,5,4,3,2,1,0:T(8,128)(2,1)S(1)}, u32[]{:S(2)}, u32[]{:S(2)}) collective-permute-start(bf16[1,1,1,1,1,48,384]{6,5,4,3,2,1,0:T(8,128)(2,1)} %bitcast.105), channel_id=1, source_target_pairs={{0,16},{1,17},{2,18},{3,19},{4,20},{5,21},{6,22},{7,23},{8,24},{9,... | collective-permute-start | bytes 110600 | tf_op jit(solution)/shard_map/ppermute | solution.py:312
  4.8 2.8 %collective-permute-start.5 = (bf16[1,1,1,1,1,48,384]{6,5,4,3,2,1,0:T(8,128)(2,1)}, bf16[1,1,1,1,1,48,384]{6,5,4,3,2,1,0:T(8,128)(2,1)S(1)}, u32[]{:S(2)}, u32[]{:S(2)}) collective-permute-start(bf16[1,1,1,1,1,48,384]{6,5,4,3,2,1,0:T(8,128)(2,1)} %bitcast.107), channel_id=1, source_target_pairs={{0,16},{1,17},{2,18},{3,19},{4,20},{5,21},{6,22},{7,23},{8,24},{9,... | collective-permute-start | bytes 110600 | tf_op jit(solution)/shard_map/ppermute | solution.py:312
  11.1 1.9 %collective-permute-start.11 = (bf16[2,1,1,1,1,48,384]{6,5,4,3,2,1,0:T(8,128)(2,1)S(1)}, bf16[2,1,1,1,1,48,384]{6,5,4,3,2,1,0:T(8,128)(2,1)S(1)}, u32[]{:S(2)}, u32[]{:S(2)}) collective-permute-start(bf16[2,1,1,1,1,48,384]{6,5,4,3,2,1,0:T(8,128)(2,1)S(1)} %pad_maximum_fusion.18), channel_id=1, source_target_pairs={{0,8},{1,9},{2,10},{3,11},{4,12},{5,13},{6,14},{7,15},{8,0},{9,1},... | collective-permute-start | bytes 221192 | tf_op jit(solution)/shard_map/ppermute | solution.py:312
  14.1 1.9 %collective-permute-start.6 = (bf16[2,1,1,1,1,48,384]{6,5,4,3,2,1,0:T(8,128)(2,1)S(1)}, bf16[2,1,1,1,1,48,384]{6,5,4,3,2,1,0:T(8,128)(2,1)S(1)}, u32[]{:S(2)}, u32[]{:S(2)}) collective-permute-start(bf16[2,1,1,1,1,48,384]{6,5,4,3,2,1,0:T(8,128)(2,1)S(1)} %pad_maximum_fusion.17), channel_id=1, source_target_pairs={{0,8},{1,9},{2,10},{3,11},{4,12},{5,13},{6,14},{7,15},{8,0},{9,1},... | collective-permute-start | bytes 221192 | tf_op jit(solution)/shard_map/ppermute | solution.py:312
  17.9 1.6 %collective-permute-start.12 = (bf16[2,2,1,1,1,48,384]{6,5,4,3,2,1,0:T(8,128)(2,1)S(1)}, bf16[2,2,1,1,1,48,384]{6,5,4,3,2,1,0:T(8,128)(2,1)S(1)}, u32[]{:S(2)}, u32[]{:S(2)}) collective-permute-start(bf16[2,2,1,1,1,48,384]{6,5,4,3,2,1,0:T(8,128)(2,1)S(1)} %pad_maximum_fusion.14), channel_id=1, source_target_pairs={{0,4},{1,5},{2,6},{3,7},{4,0},{5,1},{6,2},{7,3},{8,12},{9,13},{10,... | collective-permute-start | bytes 442376 | tf_op jit(solution)/shard_map/ppermute | solution.py:312
  19.5 1.6 %collective-permute-start.17 = (bf16[2,2,1,1,1,48,384]{6,5,4,3,2,1,0:T(8,128)(2,1)S(1)}, bf16[2,2,1,1,1,48,384]{6,5,4,3,2,1,0:T(8,128)(2,1)S(1)}, u32[]{:S(2)}, u32[]{:S(2)}) collective-permute-start(bf16[2,2,1,1,1,48,384]{6,5,4,3,2,1,0:T(8,128)(2,1)S(1)} %pad_maximum_fusion.15), channel_id=1, source_target_pairs={{0,2},{1,3},{2,0},{3,1},{4,6},{5,7},{6,4},{7,5},{8,10},{9,11},{10,... | collective-permute-start | bytes 442376 | tf_op jit(solution)/shard_map/ppermute | solution.py:312
  22.0 1.6 %collective-permute-start.2 = (bf16[2,2,1,1,1,80,384]{6,5,4,3,2,1,0:T(8,128)(2,1)S(1)}, bf16[2,2,1,1,1,80,384]{6,5,4,3,2,1,0:T(8,128)(2,1)S(1)}, u32[]{:S(2)}, u32[]{:S(2)}) collective-permute-start(bf16[2,2,1,1,1,80,384]{6,5,4,3,2,1,0:T(8,128)(2,1)S(1)} %pad_maximum_fusion.12), channel_id=1, source_target_pairs={{0,2},{1,3},{2,0},{3,1},{4,6},{5,7},{6,4},{7,5},{8,10},{9,11},{10,... | collective-permute-start | bytes 737288 | tf_op jit(solution)/shard_map/ppermute | solution.py:312
  24.9 1.5 collective-permute-done.17
  28.4 3.2 %collective-permute-done.2 = bf16[2,2,1,1,1,80,384]{6,5,4,3,2,1,0:T(8,128)(2,1)S(1)} collective-permute-done((bf16[2,2,1,1,1,80,384]{6,5,4,3,2,1,0:T(8,128)(2,1)S(1)}, bf16[2,2,1,1,1,80,384]{6,5,4,3,2,1,0:T(8,128)(2,1)S(1)}, u32[]{:S(2)}, u32[]{:S(2)}) %collective-permute-start.2) | collective-permute-done | bytes 245792 | tf_op jit(solution)/shard_map/ppermute | solution.py:312
  32.6 5.3 %collective-permute-done.13 = bf16[2,2,2,1,1,48,384]{6,5,4,3,2,1,0:T(8,128)(2,1)S(1)} collective-permute-done((bf16[2,2,2,1,1,48,384]{6,5,4,3,2,1,0:T(8,128)(2,1)S(1)}, bf16[2,2,2,1,1,48,384]{6,5,4,3,2,1,0:T(8,128)(2,1)S(1)}, u32[]{:S(2)}, u32[]{:S(2)}) %collective-permute-start.13) | collective-permute-done | bytes 294944 | tf_op jit(solution)/shard_map/ppermute | solution.py:312
  38.9 3.0 %collective-permute-done.8 = bf16[2,2,2,1,1,48,384]{6,5,4,3,2,1,0:T(8,128)(2,1)S(1)} collective-permute-done((bf16[2,2,2,1,1,48,384]{6,5,4,3,2,1,0:T(8,128)(2,1)S(1)}, bf16[2,2,2,1,1,48,384]{6,5,4,3,2,1,0:T(8,128)(2,1)S(1)}, u32[]{:S(2)}, u32[]{:S(2)}) %collective-permute-start.8) | collective-permute-done | bytes 294944 | tf_op jit(solution)/shard_map/ppermute | solution.py:312
  49.8 1.7 %slice.38 = bf16[32,72,384]{2,1,0:T(8,128)(2,1)S(1)} slice(bf16[32,80,384]{2,1,0:T(8,128)(2,1)} %bitcast.89), slice={[0:32], [0:72], [0:384]} | slice | bytes 3538944 | tf_op jit(solution)/shard_map/slice | solution.py:383
  53.4 6.2 %attend.1 = (bf16[512,384]{1,0:T(8,128)(2,1)}, bf16[512,1152]{1,0:T(8,128)(2,1)}, bf16[12,256,256]{2,1,0:T(8,128)(2,1)}, bf16[512,384]{1,0:T(8,128)(2,1)}, f32[512,384]{1,0:T(8,128)}, /*index=5*/f32[512,384]{1,0:T(8,128)}) custom-call(f32[512,384]{1,0:T(8,128)} %bitcast.93, f32[2,6,384]{2,1,0:T(8,128)} %copy_add_fusion.mod_ref, bf16[1536,384]{1,0:T(8,128)(2,1)} %bitcast.86, ...), custom_call_target="tpu_custom_call" | custom-call | tf_op jit(solution)/shard_map/attend/pallas_call | solution.py:222
  59.6 11.1 %mlp.1 = (f32[512,384]{1,0:T(8,128)}, f32[512,384]{1,0:T(8,128)}, bf16[1536,384]{1,0:T(8,128)(2,1)}, bf16[1536,384]{1,0:T(8,128)(2,1)}, f32[1,1536]{1,0:T(1,128)...) custom-call(s32[2]{0:T(128)} %bitcast.110, f32[512,384]{1,0:T(8,128)} %get-tuple-element.25.mid_ref, f32[512,384]{1,0:T(8,128)} %bitcast.101, ...), custom_call_target="tpu_custom_call" | custom-call | tf_op jit(solution)/shard_map/mlp/pallas_call | solution.py:244
  70.7 9.6 %attend_back.1 = (f32[512,384]{1,0:T(8,128)}, bf16[1536,384]{1,0:T(8,128)(2,1)}, f32[3,384]{1,0:T(4,128)}, f32[2,3,384]{2,1,0:T(4,128)}) custom-call(f32[512,384]{1,0:T(8,128)} %bitcast.94, f32[2,6,384]{2,1,0:T(8,128)} %copy_add_fusion.mod_ref, bf16[1536,384]{1,0:T(8,128)(2,1)} %bitcast.87, bf16[512,384]{1,0:T(8,128)(2,1)} %get-tuple-element.27.h_ref, ...), custom_call_target="tpu_custom_call" | custom-call | tf_op jit(solution)/shard_map/attend_back/pallas_call | solution.py:288
  86.9 2.2 %collective-permute-done.21 = f32[2,2,1,2,2,1,312]{6,4,3,2,1,0,5:T(2,128)S(1)} collective-permute-done((f32[2,2,1,2,2,1,312]{6,4,3,2,1,0,5:T(2,128)S(1)}, f32[2,2,1,2,2,1,312]{6,4,3,2,1,0,5:T(2,128)S(1)}, u32[]{:S(2)}, u32[]{:S(2)}) %collective-permute-start.21) | collective-permute-done | bytes 20000 | tf_op jit(solution)/shard_map/ppermute | solution.py:312
  89.1 1.6 %collective-permute-start.22 = (f32[2,2,2,1,2,1,312]{6,4,3,2,1,0,5:T(2,128)S(1)}, f32[2,2,2,1,2,1,312]{6,4,3,2,1,0,5:T(2,128)S(1)}, u32[]{:S(2)}, u32[]{:S(2)}) collective-permute-start(f32[2,2,2,1,2,1,312]{6,4,3,2,1,0,5:T(2,128)S(1)} %fusion.13), channel_id=1, source_target_pairs={{0,2},{1,3},{2,0},{3,1},{4,6},{5,7},{6,4},{7,5},{8,10},{9,11},{10,... | collective-permute-start | bytes 59912 | tf_op jit(solution)/shard_map/ppermute | solution.py:312
  93.1 1.5 %collective-permute-start.23 = (f32[2,1,2,2,2,1,312]{6,4,3,2,1,0,5:T(2,128)S(1)}, f32[2,1,2,2,2,1,312]{6,4,3,2,1,0,5:T(2,128)S(1)}, u32[]{:S(2)}, u32[]{:S(2)}) collective-permute-start(f32[2,1,2,2,2,1,312]{6,4,3,2,1,0,5:T(2,128)S(1)} %fusion.11), channel_id=1, source_target_pairs={{0,8},{1,9},{2,10},{3,11},{4,12},{5,13},{6,14},{7,15},{8,0},{9,1},... | collective-permute-start | bytes 59912 | tf_op jit(solution)/shard_map/ppermute | solution.py:312
  95.4 1.6 %collective-permute-done.23 = f32[2,1,2,2,2,1,312]{6,4,3,2,1,0,5:T(2,128)S(1)} collective-permute-done((f32[2,1,2,2,2,1,312]{6,4,3,2,1,0,5:T(2,128)S(1)}, f32[2,1,2,2,2,1,312]{6,4,3,2,1,0,5:T(2,128)S(1)}, u32[]{:S(2)}, u32[]{:S(2)}) %collective-permute-start.23) | collective-permute-done | bytes 20000 | tf_op jit(solution)/shard_map/ppermute | solution.py:312
  97.7 2.4 %collective-permute-start.24 = (f32[1,2,2,2,2,1,312]{6,4,3,2,1,0,5:T(2,128)}, f32[1,2,2,2,2,1,312]{6,4,3,2,1,0,5:T(2,128)}, u32[]{:S(2)}, u32[]{:S(2)}) collective-permute-start(f32[1,2,2,2,2,1,312]{6,4,3,2,1,0,5:T(2,128)} %fusion.9), channel_id=1, source_target_pairs={{0,16},{1,17},{2,18},{3,19},{4,20},{5,21},{6,22},{7,23},{8,24},{9,... | collective-permute-start | bytes 59912 | tf_op jit(solution)/shard_map/ppermute | solution.py:312
  100.2 1.6 %slice.47 = bf16[32,2,384]{2,1,0:T(2,128)(2,1)} slice(bf16[32,80,384]{2,1,0:T(8,128)(2,1)} %bitcast.90), slice={[0:32], [73:75], [0:384]} | slice | bytes 98304 | tf_op jit(solution)/shard_map/slice | solution.py:385
  105.8 1.5 reshape.106
  111.5 1.7 %convolution_bitcast_fusion = f32[1,72,384]{2,1,0:T(8,128)} fusion(f32[64,72]{1,0:T(8,128)} %reshape.107, bf16[64,384]{1,0:T(8,128)(2,1)} %reshape.108), kind=kOutput, calls=%fused_computation.7 | convolution fusion | flops 21233664 | bytes 178176 | tf_op jit(solution)/shard_map/kr,kd->rd/dot_general | solution.py:426
  115.9 1.6 %collective-permute-start.31 = (bf16[2,2,2,1,1,48,384]{6,5,4,3,2,1,0:T(8,128)(2,1)S(1)}, bf16[2,2,2,1,1,48,384]{6,5,4,3,2,1,0:T(8,128)(2,1)S(1)}, u32[]{:S(2)}, u32[]{:S(2)}) collective-permute-start(bf16[2,2,2,1,1,48,384]{6,5,4,3,2,1,0:T(8,128)(2,1)S(1)} %constant_dynamic-slice_fusion.8), channel_id=1, source_target_pairs={{0,2},{1,3},{2,0},{3,1},{4,6},{5,7},{6,4},{7,5},{8,10},{9,11},{10,... | collective-permute-start | bytes 884744 | tf_op jit(solution)/shard_map/ppermute | solution.py:312
  119.3 4.1 %collective-permute-done.36 = bf16[2,2,1,2,1,48,384]{6,5,4,3,2,1,0:T(8,128)(2,1)S(1)} collective-permute-done((bf16[2,2,1,2,1,48,384]{6,5,4,3,2,1,0:T(8,128)(2,1)S(1)}, bf16[2,2,1,2,1,48,384]{6,5,4,3,2,1,0:T(8,128)(2,1)S(1)}, u32[]{:S(2)}, u32[]{:S(2)}) %collective-permute-start.36) | collective-permute-done | bytes 294944 | tf_op jit(solution)/shard_map/ppermute | solution.py:312
  123.6 1.6 %collective-permute-start.37 = (bf16[2,2,1,1,1,48,384]{6,5,4,3,2,1,0:T(8,128)(2,1)S(1)}, bf16[2,2,1,1,1,48,384]{6,5,4,3,2,1,0:T(8,128)(2,1)S(1)}, u32[]{:S(2)}, u32[]{:S(2)}) collective-permute-start(bf16[2,2,1,1,1,48,384]{6,5,4,3,2,1,0:T(8,128)(2,1)S(1)} %constant_dynamic-slice_fusion.2), channel_id=1, source_target_pairs={{0,2},{1,3},{2,0},{3,1},{4,6},{5,7},{6,4},{7,5},{8,10},{9,11},{10,... | collective-permute-start | bytes 442376 | tf_op jit(solution)/shard_map/ppermute | solution.py:312
  126.0 2.0 %collective-permute-start.32 = (bf16[2,2,1,1,1,48,384]{6,5,4,3,2,1,0:T(8,128)(2,1)S(1)}, bf16[2,2,1,1,1,48,384]{6,5,4,3,2,1,0:T(8,128)(2,1)S(1)}, u32[]{:S(2)}, u32[]{:S(2)}) collective-permute-start(bf16[2,2,1,1,1,48,384]{6,5,4,3,2,1,0:T(8,128)(2,1)S(1)} %constant_dynamic-slice_fusion.7), channel_id=1, source_target_pairs={{0,4},{1,5},{2,6},{3,7},{4,0},{5,1},{6,2},{7,3},{8,12},{9,13},{10,... | collective-permute-start | bytes 442376 | tf_op jit(solution)/shard_map/ppermute | solution.py:312
  127.9 4.2 %collective-permute-done.26 = bf16[2,2,2,1,1,48,384]{6,5,4,3,2,1,0:T(8,128)(2,1)S(1)} collective-permute-done((bf16[2,2,2,1,1,48,384]{6,5,4,3,2,1,0:T(8,128)(2,1)S(1)}, bf16[2,2,2,1,1,48,384]{6,5,4,3,2,1,0:T(8,128)(2,1)S(1)}, u32[]{:S(2)}, u32[]{:S(2)}) %collective-permute-start.26) | collective-permute-done | bytes 294944 | tf_op jit(solution)/shard_map/ppermute | solution.py:312
  132.3 2.0 %collective-permute-start.27 = (bf16[2,2,1,1,1,48,384]{6,5,4,3,2,1,0:T(8,128)(2,1)S(1)}, bf16[2,2,1,1,1,48,384]{6,5,4,3,2,1,0:T(8,128)(2,1)S(1)}, u32[]{:S(2)}, u32[]{:S(2)}) collective-permute-start(bf16[2,2,1,1,1,48,384]{6,5,4,3,2,1,0:T(8,128)(2,1)S(1)} %constant_dynamic-slice_fusion.12), channel_id=1, source_target_pairs={{0,4},{1,5},{2,6},{3,7},{4,0},{5,1},{6,2},{7,3},{8,12},{9,13},{10,... | collective-permute-start | bytes 442376 | tf_op jit(solution)/shard_map/ppermute | solution.py:312
  134.5 1.6 %collective-permute-start.38 = (bf16[2,1,1,1,1,48,384]{6,5,4,3,2,1,0:T(8,128)(2,1)S(1)}, bf16[2,1,1,1,1,48,384]{6,5,4,3,2,1,0:T(8,128)(2,1)S(1)}, u32[]{:S(2)}, u32[]{:S(2)}) collective-permute-start(bf16[2,1,1,1,1,48,384]{6,5,4,3,2,1,0:T(8,128)(2,1)S(1)} %constant_dynamic-slice_fusion.1), channel_id=1, source_target_pairs={{0,8},{1,9},{2,10},{3,11},{4,12},{5,13},{6,14},{7,15},{8,0},{9,1},... | collective-permute-start | bytes 221192 | tf_op jit(solution)/shard_map/ppermute | solution.py:312
  137.6 1.7 %collective-permute-start.28 = (bf16[2,1,1,1,1,48,384]{6,5,4,3,2,1,0:T(8,128)(2,1)S(1)}, bf16[2,1,1,1,1,48,384]{6,5,4,3,2,1,0:T(8,128)(2,1)S(1)}, u32[]{:S(2)}, u32[]{:S(2)}) collective-permute-start(bf16[2,1,1,1,1,48,384]{6,5,4,3,2,1,0:T(8,128)(2,1)S(1)} %constant_dynamic-slice_fusion.11), channel_id=1, source_target_pairs={{0,8},{1,9},{2,10},{3,11},{4,12},{5,13},{6,14},{7,15},{8,0},{9,1},... | collective-permute-start | bytes 221192 | tf_op jit(solution)/shard_map/ppermute | solution.py:312
  140.9 1.9 %collective-permute-start.34 = (bf16[1,1,1,1,1,48,384]{6,5,4,3,2,1,0:T(8,128)(2,1)S(1)}, bf16[1,1,1,1,1,48,384]{6,5,4,3,2,1,0:T(8,128)(2,1)S(1)}, u32[]{:S(2)}, u32[]{:S(2)}) collective-permute-start(bf16[1,1,1,1,1,48,384]{6,5,4,3,2,1,0:T(8,128)(2,1)S(1)} %constant_dynamic-slice_fusion.5), channel_id=1, source_target_pairs={{0,16},{1,17},{2,18},{3,19},{4,20},{5,21},{6,22},{7,23},{8,24},{9,... | collective-permute-start | bytes 110600 | tf_op jit(solution)/shard_map/ppermute | solution.py:312
  (191 shorter events, 55.4 us)
Async XLA Ops:
  0.6 9.6 %collective-permute-start.15 = (bf16[1,1,1,1,1,48,384]{6,5,4,3,2,1,0:T(8,128)(2,1)}, bf16[1,1,1,1,1,48,384]{6,5,4,3,2,1,0:T(8,128)(2,1)S(1)}, u32[]{:S(2)}, u32[]{:S(2)}) collective-permute-start(bf16[1,1,1,1,1,48,384]{6,5,4,3,2,1,0:T(8,128)(2,1)} %bitcast.105), channel_id=1, source_target_pairs={{0,16},{1,17},{2,18},{3,19},{4,20},{5,21},{6,22},{7,23},{8,24},{9,... | collective-permute-start | bytes 110600 | tf_op jit(solution)/shard_map/ppermute | solution.py:312
  4.8 5.5 %collective-permute-start.10 = (bf16[1,1,1,1,1,48,384]{6,5,4,3,2,1,0:T(8,128)(2,1)}, bf16[1,1,1,1,1,48,384]{6,5,4,3,2,1,0:T(8,128)(2,1)S(1)}, u32[]{:S(2)}, u32[]{:S(2)}) collective-permute-start(bf16[1,1,1,1,1,48,384]{6,5,4,3,2,1,0:T(8,128)(2,1)} %bitcast.106), channel_id=1, source_target_pairs={{0,16},{1,17},{2,18},{3,19},{4,20},{5,21},{6,22},{7,23},{8,24},{9,... | collective-permute-start | bytes 110600 | tf_op jit(solution)/shard_map/ppermute | solution.py:312
  4.8 8.4 %collective-permute-start.5 = (bf16[1,1,1,1,1,48,384]{6,5,4,3,2,1,0:T(8,128)(2,1)}, bf16[1,1,1,1,1,48,384]{6,5,4,3,2,1,0:T(8,128)(2,1)S(1)}, u32[]{:S(2)}, u32[]{:S(2)}) collective-permute-start(bf16[1,1,1,1,1,48,384]{6,5,4,3,2,1,0:T(8,128)(2,1)} %bitcast.107), channel_id=1, source_target_pairs={{0,16},{1,17},{2,18},{3,19},{4,20},{5,21},{6,22},{7,23},{8,24},{9,... | collective-permute-start | bytes 110600 | tf_op jit(solution)/shard_map/ppermute | solution.py:312
  9.4 6.6 %collective-permute-start = (bf16[1,1,1,1,1,80,384]{6,5,4,3,2,1,0:T(8,128)(2,1)S(1)}, bf16[1,1,1,1,1,80,384]{6,5,4,3,2,1,0:T(8,128)(2,1)S(1)}, u32[]{:S(2)}, u32[]{:S(2)}) collective-permute-start(bf16[1,1,1,1,1,80,384]{6,5,4,3,2,1,0:T(8,128)(2,1)S(1)} %fusion.7), channel_id=1, source_target_pairs={{0,16},{1,17},{2,18},{3,19},{4,20},{5,21},{6,22},{7,23},{8,24},{9,... | collective-permute-start | bytes 184328 | tf_op jit(solution)/shard_map/ppermute | solution.py:312
  11.1 6.7 %collective-permute-start.11 = (bf16[2,1,1,1,1,48,384]{6,5,4,3,2,1,0:T(8,128)(2,1)S(1)}, bf16[2,1,1,1,1,48,384]{6,5,4,3,2,1,0:T(8,128)(2,1)S(1)}, u32[]{:S(2)}, u32[]{:S(2)}) collective-permute-start(bf16[2,1,1,1,1,48,384]{6,5,4,3,2,1,0:T(8,128)(2,1)S(1)} %pad_maximum_fusion.18), channel_id=1, source_target_pairs={{0,8},{1,9},{2,10},{3,11},{4,12},{5,13},{6,14},{7,15},{8,0},{9,1},... | collective-permute-start | bytes 221192 | tf_op jit(solution)/shard_map/ppermute | solution.py:312
  13.0 6.5 %collective-permute-start.16 = (bf16[2,1,1,1,1,48,384]{6,5,4,3,2,1,0:T(8,128)(2,1)S(1)}, bf16[2,1,1,1,1,48,384]{6,5,4,3,2,1,0:T(8,128)(2,1)S(1)}, u32[]{:S(2)}, u32[]{:S(2)}) collective-permute-start(bf16[2,1,1,1,1,48,384]{6,5,4,3,2,1,0:T(8,128)(2,1)S(1)} %pad_maximum_fusion.19), channel_id=1, source_target_pairs={{0,8},{1,9},{2,10},{3,11},{4,12},{5,13},{6,14},{7,15},{8,0},{9,1},... | collective-permute-start | bytes 221192 | tf_op jit(solution)/shard_map/ppermute | solution.py:312
  14.1 7.0 %collective-permute-start.6 = (bf16[2,1,1,1,1,48,384]{6,5,4,3,2,1,0:T(8,128)(2,1)S(1)}, bf16[2,1,1,1,1,48,384]{6,5,4,3,2,1,0:T(8,128)(2,1)S(1)}, u32[]{:S(2)}, u32[]{:S(2)}) collective-permute-start(bf16[2,1,1,1,1,48,384]{6,5,4,3,2,1,0:T(8,128)(2,1)S(1)} %pad_maximum_fusion.17), channel_id=1, source_target_pairs={{0,8},{1,9},{2,10},{3,11},{4,12},{5,13},{6,14},{7,15},{8,0},{9,1},... | collective-permute-start | bytes 221192 | tf_op jit(solution)/shard_map/ppermute | solution.py:312
  16.9 4.9 %collective-permute-start.1 = (bf16[2,1,1,1,1,80,384]{6,5,4,3,2,1,0:T(8,128)(2,1)S(1)}, bf16[2,1,1,1,1,80,384]{6,5,4,3,2,1,0:T(8,128)(2,1)S(1)}, u32[]{:S(2)}, u32[]{:S(2)}) collective-permute-start(bf16[2,1,1,1,1,80,384]{6,5,4,3,2,1,0:T(8,128)(2,1)S(1)} %pad_maximum_fusion.16), channel_id=1, source_target_pairs={{0,8},{1,9},{2,10},{3,11},{4,12},{5,13},{6,14},{7,15},{8,0},{9,1},... | collective-permute-start | bytes 368648 | tf_op jit(solution)/shard_map/ppermute | solution.py:312
  17.9 5.8 %collective-permute-start.12 = (bf16[2,2,1,1,1,48,384]{6,5,4,3,2,1,0:T(8,128)(2,1)S(1)}, bf16[2,2,1,1,1,48,384]{6,5,4,3,2,1,0:T(8,128)(2,1)S(1)}, u32[]{:S(2)}, u32[]{:S(2)}) collective-permute-start(bf16[2,2,1,1,1,48,384]{6,5,4,3,2,1,0:T(8,128)(2,1)S(1)} %pad_maximum_fusion.14), channel_id=1, source_target_pairs={{0,4},{1,5},{2,6},{3,7},{4,0},{5,1},{6,2},{7,3},{8,12},{9,13},{10,... | collective-permute-start | bytes 442376 | tf_op jit(solution)/shard_map/ppermute | solution.py:312
  19.5 6.8 %collective-permute-start.17 = (bf16[2,2,1,1,1,48,384]{6,5,4,3,2,1,0:T(8,128)(2,1)S(1)}, bf16[2,2,1,1,1,48,384]{6,5,4,3,2,1,0:T(8,128)(2,1)S(1)}, u32[]{:S(2)}, u32[]{:S(2)}) collective-permute-start(bf16[2,2,1,1,1,48,384]{6,5,4,3,2,1,0:T(8,128)(2,1)S(1)} %pad_maximum_fusion.15), channel_id=1, source_target_pairs={{0,2},{1,3},{2,0},{3,1},{4,6},{5,7},{6,4},{7,5},{8,10},{9,11},{10,... | collective-permute-start | bytes 442376 | tf_op jit(solution)/shard_map/ppermute | solution.py:312
  21.1 6.8 %collective-permute-start.7 = (bf16[2,2,1,1,1,48,384]{6,5,4,3,2,1,0:T(8,128)(2,1)S(1)}, bf16[2,2,1,1,1,48,384]{6,5,4,3,2,1,0:T(8,128)(2,1)S(1)}, u32[]{:S(2)}, u32[]{:S(2)}) collective-permute-start(bf16[2,2,1,1,1,48,384]{6,5,4,3,2,1,0:T(8,128)(2,1)S(1)} %pad_maximum_fusion.13), channel_id=1, source_target_pairs={{0,4},{1,5},{2,6},{3,7},{4,0},{5,1},{6,2},{7,3},{8,12},{9,13},{10,... | collective-permute-start | bytes 442376 | tf_op jit(solution)/shard_map/ppermute | solution.py:312
  22.0 9.6 %collective-permute-start.2 = (bf16[2,2,1,1,1,80,384]{6,5,4,3,2,1,0:T(8,128)(2,1)S(1)}, bf16[2,2,1,1,1,80,384]{6,5,4,3,2,1,0:T(8,128)(2,1)S(1)}, u32[]{:S(2)}, u32[]{:S(2)}) collective-permute-start(bf16[2,2,1,1,1,80,384]{6,5,4,3,2,1,0:T(8,128)(2,1)S(1)} %pad_maximum_fusion.12), channel_id=1, source_target_pairs={{0,2},{1,3},{2,0},{3,1},{4,6},{5,7},{6,4},{7,5},{8,10},{9,11},{10,... | collective-permute-start | bytes 737288 | tf_op jit(solution)/shard_map/ppermute | solution.py:312
  23.7 14.2 %collective-permute-start.13 = (bf16[2,2,2,1,1,48,384]{6,5,4,3,2,1,0:T(8,128)(2,1)S(1)}, bf16[2,2,2,1,1,48,384]{6,5,4,3,2,1,0:T(8,128)(2,1)S(1)}, u32[]{:S(2)}, u32[]{:S(2)}) collective-permute-start(bf16[2,2,2,1,1,48,384]{6,5,4,3,2,1,0:T(8,128)(2,1)S(1)} %pad_maximum_fusion.10), channel_id=1, source_target_pairs={{0,2},{1,3},{2,0},{3,1},{4,6},{5,7},{6,4},{7,5},{8,10},{9,11},{10,... | collective-permute-start | bytes 884744 | tf_op jit(solution)/shard_map/ppermute | solution.py:312
  26.4 11.7 %collective-permute-start.18 = (bf16[2,2,1,2,1,48,384]{6,5,4,3,2,1,0:T(8,128)(2,1)S(1)}, bf16[2,2,1,2,1,48,384]{6,5,4,3,2,1,0:T(8,128)(2,1)S(1)}, u32[]{:S(2)}, u32[]{:S(2)}) collective-permute-start(bf16[2,2,1,2,1,48,384]{6,5,4,3,2,1,0:T(8,128)(2,1)S(1)} %pad_maximum_fusion.11), channel_id=1, source_target_pairs={{0,4},{1,5},{2,6},{3,7},{4,0},{5,1},{6,2},{7,3},{8,12},{9,13},{10,... | collective-permute-start | bytes 884744 | tf_op jit(solution)/shard_map/ppermute | solution.py:312
  28.0 13.9 %collective-permute-start.8 = (bf16[2,2,2,1,1,48,384]{6,5,4,3,2,1,0:T(8,128)(2,1)S(1)}, bf16[2,2,2,1,1,48,384]{6,5,4,3,2,1,0:T(8,128)(2,1)S(1)}, u32[]{:S(2)}, u32[]{:S(2)}) collective-permute-start(bf16[2,2,2,1,1,48,384]{6,5,4,3,2,1,0:T(8,128)(2,1)S(1)} %pad_maximum_fusion.9), channel_id=1, source_target_pairs={{0,2},{1,3},{2,0},{3,1},{4,6},{5,7},{6,4},{7,5},{8,10},{9,11},{10,... | collective-permute-start | bytes 884744 | tf_op jit(solution)/shard_map/ppermute | solution.py:312
  31.7 11.8 %collective-permute-start.3 = (bf16[2,2,1,2,1,80,384]{6,5,4,3,2,1,0:T(8,128)(2,1)S(1)}, bf16[2,2,1,2,1,80,384]{6,5,4,3,2,1,0:T(8,128)(2,1)S(1)}, u32[]{:S(2)}, u32[]{:S(2)}) collective-permute-start(bf16[2,2,1,2,1,80,384]{6,5,4,3,2,1,0:T(8,128)(2,1)S(1)} %pad_maximum_fusion.8), channel_id=1, source_target_pairs={{0,4},{1,5},{2,6},{3,7},{4,0},{5,1},{6,2},{7,3},{8,12},{9,13},{10,... | collective-permute-start | bytes 1474568 | tf_op jit(solution)/shard_map/ppermute | solution.py:312
  38.1 5.8 %collective-permute-start.14 = (bf16[2,2,2,2,1,48,384]{6,5,4,3,2,1,0:T(8,128)(2,1)S(1)}, bf16[2,2,2,2,1,48,384]{6,5,4,3,2,1,0:T(8,128)(2,1)S(1)}, u32[]{:S(2)}, u32[]{:S(2)}) collective-permute-start(bf16[2,2,2,2,1,48,384]{6,5,4,3,2,1,0:T(8,128)(2,1)S(1)} %pad_maximum_fusion.6), channel_id=1, source_target_pairs={{0,1},{1,0},{2,3},{3,2},{4,5},{5,4},{6,7},{7,6},{8,9},{9,8},{10,11... | collective-permute-start | bytes 1769480 | tf_op jit(solution)/shard_map/ppermute | solution.py:312
  38.3 6.8 %collective-permute-start.19 = (bf16[2,2,2,2,1,48,384]{6,5,4,3,2,1,0:T(8,128)(2,1)S(1)}, bf16[2,2,2,2,1,48,384]{6,5,4,3,2,1,0:T(8,128)(2,1)S(1)}, u32[]{:S(2)}, u32[]{:S(2)}) collective-permute-start(bf16[2,2,2,2,1,48,384]{6,5,4,3,2,1,0:T(8,128)(2,1)S(1)} %pad_maximum_fusion.7), channel_id=1, source_target_pairs={{0,1},{1,0},{2,3},{3,2},{4,5},{5,4},{6,7},{7,6},{8,9},{9,8},{10,11... | collective-permute-start | bytes 1769480 | tf_op jit(solution)/shard_map/ppermute | solution.py:312
  91.6 21.6 %collective-permute-start.35 = (bf16[2,2,2,2,1,48,384]{6,5,4,3,2,1,0:T(8,128)(2,1)}, bf16[2,2,2,2,1,48,384]{6,5,4,3,2,1,0:T(8,128)(2,1)}, u32[]{:S(2)}, u32[]{:S(2)}) collective-permute-start(bf16[2,2,2,2,1,48,384]{6,5,4,3,2,1,0:T(8,128)(2,1)} %constant_dynamic-slice_fusion.4), channel_id=1, source_target_pairs={{0,1},{1,0},{2,3},{3,2},{4,5},{5,4},{6,7},{7,6},{8,9},{9,8},{10,11... | collective-permute-start | bytes 1769480 | tf_op jit(solution)/shard_map/ppermute | solution.py:312
  97.7 6.7 %collective-permute-start.24 = (f32[1,2,2,2,2,1,312]{6,4,3,2,1,0,5:T(2,128)}, f32[1,2,2,2,2,1,312]{6,4,3,2,1,0,5:T(2,128)}, u32[]{:S(2)}, u32[]{:S(2)}) collective-permute-start(f32[1,2,2,2,2,1,312]{6,4,3,2,1,0,5:T(2,128)} %fusion.9), channel_id=1, source_target_pairs={{0,16},{1,17},{2,18},{3,19},{4,20},{5,21},{6,22},{7,23},{8,24},{9,... | collective-permute-start | bytes 59912 | tf_op jit(solution)/shard_map/ppermute | solution.py:312
  103.8 10.7 %collective-permute-start.30 = (bf16[2,2,2,2,1,48,384]{6,5,4,3,2,1,0:T(8,128)(2,1)S(1)}, bf16[2,2,2,2,1,48,384]{6,5,4,3,2,1,0:T(8,128)(2,1)}, u32[]{:S(2)}, u32[]{:S(2)}) collective-permute-start(bf16[2,2,2,2,1,48,384]{6,5,4,3,2,1,0:T(8,128)(2,1)S(1)} %constant_dynamic-slice_fusion.9), channel_id=1, source_target_pairs={{0,1},{1,0},{2,3},{3,2},{4,5},{5,4},{6,7},{7,6},{8,9},{9,8},{10,11... | collective-permute-start | bytes 1769480 | tf_op jit(solution)/shard_map/ppermute | solution.py:312
  103.8 13.6 %collective-permute-start.25 = (bf16[2,2,2,2,1,48,384]{6,5,4,3,2,1,0:T(8,128)(2,1)S(1)}, bf16[2,2,2,2,1,48,384]{6,5,4,3,2,1,0:T(8,128)(2,1)}, u32[]{:S(2)}, u32[]{:S(2)}) collective-permute-start(bf16[2,2,2,2,1,48,384]{6,5,4,3,2,1,0:T(8,128)(2,1)S(1)} %constant_dynamic-slice_fusion.14), channel_id=1, source_target_pairs={{0,1},{1,0},{2,3},{3,2},{4,5},{5,4},{6,7},{7,6},{8,9},{9,8},{10,11... | collective-permute-start | bytes 1769480 | tf_op jit(solution)/shard_map/ppermute | solution.py:312
  114.5 9.0 %collective-permute-start.36 = (bf16[2,2,1,2,1,48,384]{6,5,4,3,2,1,0:T(8,128)(2,1)S(1)}, bf16[2,2,1,2,1,48,384]{6,5,4,3,2,1,0:T(8,128)(2,1)S(1)}, u32[]{:S(2)}, u32[]{:S(2)}) collective-permute-start(bf16[2,2,1,2,1,48,384]{6,5,4,3,2,1,0:T(8,128)(2,1)S(1)} %constant_dynamic-slice_fusion.3), channel_id=1, source_target_pairs={{0,4},{1,5},{2,6},{3,7},{4,0},{5,1},{6,2},{7,3},{8,12},{9,13},{10,... | collective-permute-start | bytes 884744 | tf_op jit(solution)/shard_map/ppermute | solution.py:312
  115.9 9.9 %collective-permute-start.31 = (bf16[2,2,2,1,1,48,384]{6,5,4,3,2,1,0:T(8,128)(2,1)S(1)}, bf16[2,2,2,1,1,48,384]{6,5,4,3,2,1,0:T(8,128)(2,1)S(1)}, u32[]{:S(2)}, u32[]{:S(2)}) collective-permute-start(bf16[2,2,2,1,1,48,384]{6,5,4,3,2,1,0:T(8,128)(2,1)S(1)} %constant_dynamic-slice_fusion.8), channel_id=1, source_target_pairs={{0,2},{1,3},{2,0},{3,1},{4,6},{5,7},{6,4},{7,5},{8,10},{9,11},{10,... | collective-permute-start | bytes 884744 | tf_op jit(solution)/shard_map/ppermute | solution.py:312
  118.7 13.4 %collective-permute-start.26 = (bf16[2,2,2,1,1,48,384]{6,5,4,3,2,1,0:T(8,128)(2,1)S(1)}, bf16[2,2,2,1,1,48,384]{6,5,4,3,2,1,0:T(8,128)(2,1)S(1)}, u32[]{:S(2)}, u32[]{:S(2)}) collective-permute-start(bf16[2,2,2,1,1,48,384]{6,5,4,3,2,1,0:T(8,128)(2,1)S(1)} %constant_dynamic-slice_fusion.13), channel_id=1, source_target_pairs={{0,2},{1,3},{2,0},{3,1},{4,6},{5,7},{6,4},{7,5},{8,10},{9,11},{10,... | collective-permute-start | bytes 884744 | tf_op jit(solution)/shard_map/ppermute | solution.py:312
  123.6 10.8 %collective-permute-start.37 = (bf16[2,2,1,1,1,48,384]{6,5,4,3,2,1,0:T(8,128)(2,1)S(1)}, bf16[2,2,1,1,1,48,384]{6,5,4,3,2,1,0:T(8,128)(2,1)S(1)}, u32[]{:S(2)}, u32[]{:S(2)}) collective-permute-start(bf16[2,2,1,1,1,48,384]{6,5,4,3,2,1,0:T(8,128)(2,1)S(1)} %constant_dynamic-slice_fusion.2), channel_id=1, source_target_pairs={{0,2},{1,3},{2,0},{3,1},{4,6},{5,7},{6,4},{7,5},{8,10},{9,11},{10,... | collective-permute-start | bytes 442376 | tf_op jit(solution)/shard_map/ppermute | solution.py:312
  126.0 10.2 %collective-permute-start.32 = (bf16[2,2,1,1,1,48,384]{6,5,4,3,2,1,0:T(8,128)(2,1)S(1)}, bf16[2,2,1,1,1,48,384]{6,5,4,3,2,1,0:T(8,128)(2,1)S(1)}, u32[]{:S(2)}, u32[]{:S(2)}) collective-permute-start(bf16[2,2,1,1,1,48,384]{6,5,4,3,2,1,0:T(8,128)(2,1)S(1)} %constant_dynamic-slice_fusion.7), channel_id=1, source_target_pairs={{0,4},{1,5},{2,6},{3,7},{4,0},{5,1},{6,2},{7,3},{8,12},{9,13},{10,... | collective-permute-start | bytes 442376 | tf_op jit(solution)/shard_map/ppermute | solution.py:312
  132.3 5.2 %collective-permute-start.27 = (bf16[2,2,1,1,1,48,384]{6,5,4,3,2,1,0:T(8,128)(2,1)S(1)}, bf16[2,2,1,1,1,48,384]{6,5,4,3,2,1,0:T(8,128)(2,1)S(1)}, u32[]{:S(2)}, u32[]{:S(2)}) collective-permute-start(bf16[2,2,1,1,1,48,384]{6,5,4,3,2,1,0:T(8,128)(2,1)S(1)} %constant_dynamic-slice_fusion.12), channel_id=1, source_target_pairs={{0,4},{1,5},{2,6},{3,7},{4,0},{5,1},{6,2},{7,3},{8,12},{9,13},{10,... | collective-permute-start | bytes 442376 | tf_op jit(solution)/shard_map/ppermute | solution.py:312
  134.5 5.2 %collective-permute-start.38 = (bf16[2,1,1,1,1,48,384]{6,5,4,3,2,1,0:T(8,128)(2,1)S(1)}, bf16[2,1,1,1,1,48,384]{6,5,4,3,2,1,0:T(8,128)(2,1)S(1)}, u32[]{:S(2)}, u32[]{:S(2)}) collective-permute-start(bf16[2,1,1,1,1,48,384]{6,5,4,3,2,1,0:T(8,128)(2,1)S(1)} %constant_dynamic-slice_fusion.1), channel_id=1, source_target_pairs={{0,8},{1,9},{2,10},{3,11},{4,12},{5,13},{6,14},{7,15},{8,0},{9,1},... | collective-permute-start | bytes 221192 | tf_op jit(solution)/shard_map/ppermute | solution.py:312
  137.6 5.3 %collective-permute-start.28 = (bf16[2,1,1,1,1,48,384]{6,5,4,3,2,1,0:T(8,128)(2,1)S(1)}, bf16[2,1,1,1,1,48,384]{6,5,4,3,2,1,0:T(8,128)(2,1)S(1)}, u32[]{:S(2)}, u32[]{:S(2)}) collective-permute-start(bf16[2,1,1,1,1,48,384]{6,5,4,3,2,1,0:T(8,128)(2,1)S(1)} %constant_dynamic-slice_fusion.11), channel_id=1, source_target_pairs={{0,8},{1,9},{2,10},{3,11},{4,12},{5,13},{6,14},{7,15},{8,0},{9,1},... | collective-permute-start | bytes 221192 | tf_op jit(solution)/shard_map/ppermute | solution.py:312
  139.7 5.5 %collective-permute-start.39 = (bf16[1,1,1,1,1,48,384]{6,5,4,3,2,1,0:T(8,128)(2,1)S(1)}, bf16[1,1,1,1,1,48,384]{6,5,4,3,2,1,0:T(8,128)(2,1)S(1)}, u32[]{:S(2)}, u32[]{:S(2)}) collective-permute-start(bf16[1,1,1,1,1,48,384]{6,5,4,3,2,1,0:T(8,128)(2,1)S(1)} %constant_dynamic-slice_fusion), channel_id=1, source_target_pairs={{0,16},{1,17},{2,18},{3,19},{4,20},{5,21},{6,22},{7,23},{8,24},{9,... | collective-permute-start | bytes 110600 | tf_op jit(solution)/shard_map/ppermute | solution.py:312
  140.9 5.1 %collective-permute-start.34 = (bf16[1,1,1,1,1,48,384]{6,5,4,3,2,1,0:T(8,128)(2,1)S(1)}, bf16[1,1,1,1,1,48,384]{6,5,4,3,2,1,0:T(8,128)(2,1)S(1)}, u32[]{:S(2)}, u32[]{:S(2)}) collective-permute-start(bf16[1,1,1,1,1,48,384]{6,5,4,3,2,1,0:T(8,128)(2,1)S(1)} %constant_dynamic-slice_fusion.5), channel_id=1, source_target_pairs={{0,16},{1,17},{2,18},{3,19},{4,20},{5,21},{6,22},{7,23},{8,24},{9,... | collective-permute-start | bytes 110600 | tf_op jit(solution)/shard_map/ppermute | solution.py:312
  (22 other events, 129.0 us)

commit v3 on v2

v3 whole, which is shorter than its diff:
```python
import functools
import math

import jax
import jax.numpy as jnp
from jax import lax
from jax.experimental import pallas as pl
from jax.experimental.pallas import tpu as pltpu
from jax.sharding import PartitionSpec as P

HEADS = 6

NORM_EPS = 1e-06


def product(form, left, right):
    return jnp.einsum(form, left, right, preferred_element_type=jnp.float32)


def dot_nn(left, right):
    return lax.dot_general(left, right, (((1,), (0,)), ((), ())), preferred_element_type=jnp.float32)


def dot_nt(left, right):
    return lax.dot_general(left, right, (((1,), (1,)), ((), ())), preferred_element_type=jnp.float32)


def dot_tn(left, right):
    return lax.dot_general(left, right, (((0,), (0,)), ((), ())), preferred_element_type=jnp.float32)


def layer_norm(values):
    center = values - jnp.mean(values, axis=-1, keepdims=True)
    inv_std = lax.rsqrt(jnp.mean(center * center, axis=-1, keepdims=True) + NORM_EPS)
    return (center * inv_std, inv_std)


def norm_back(grad_norm, normed, inv_std):
    return inv_std * (
        grad_norm
        - jnp.mean(grad_norm, axis=-1, keepdims=True)
        - normed * jnp.mean(grad_norm * normed, axis=-1, keepdims=True)
    )


def token_sum(values):
    return jnp.sum(values, axis=0, keepdims=True)


def pair_masks(rows, pair_w):
    lane = lax.broadcasted_iota(jnp.int32, (rows, pair_w), 1)
    return (lane < pair_w // 2, lane >= pair_w // 2)


def block_rows(me_ref, offset, block_n, bits=None):
    me = me_ref[0] if bits is None else me_ref[0] & bits
    return pl.ds(pl.multiple_of((me ^ offset) * block_n, 16), block_n)


def attend_kernel(
    batches, me_ref, x_ref, mod_ref, own_ref, other_ref, bias_ref,
    w_ref, h_ref, qkv_ref, p_ref, ctx_ref, ao_ref, mid_ref,
):
    block_n = own_ref.shape[1]
    for idx in range(own_ref.shape[0]):
        w_ref[block_rows(me_ref, 2 * idx, block_n, 1), :] = own_ref[idx]
        w_ref[block_rows(me_ref, 2 * idx + 1, block_n, 1), :] = other_ref[idx]
    tokens_n, width_n = x_ref.shape[0] // batches, x_ref.shape[1]
    pair_w = 2 * (width_n // HEADS)
    scaling = 1.0 / math.sqrt(width_n // HEADS)
    for b in range(batches):
        rows = pl.ds(b * tokens_n, tokens_n)
        normed, _ = layer_norm(x_ref[rows, :])
        shift = mod_ref[b, 0:1, :]
        scale = mod_ref[b, 1:2, :]
        h_ref[rows, :] = (normed * (1.0 + scale) + shift).astype(jnp.bfloat16)
    for part, bias_row in ((0, 6), (1, None), (2, 7)):
        cols = pl.ds(part * width_n, width_n)
        value = dot_nt(h_ref[...], w_ref[cols, :])
        if bias_row is not None:
            value = value + bias_ref[bias_row : bias_row + 1, :]
        qkv_ref[:, cols] = value.astype(jnp.bfloat16)
    masks = pair_masks(tokens_n, pair_w)
    for b in range(batches):
        rows = pl.ds(b * tokens_n, tokens_n)
        for pair in range(HEADS // 2):
            q_pair = qkv_ref[rows, pl.ds(pair * pair_w, pair_w)]
            k_pair = qkv_ref[rows, pl.ds(width_n + pair * pair_w, pair_w)]
            v_pair = qkv_ref[rows, pl.ds(2 * width_n + pair * pair_w, pair_w)]
            found = []
            for side in range(2):
                q_one = jnp.where(masks[side], q_pair, jnp.zeros_like(q_pair)) * jnp.bfloat16(scaling)
                scores = dot_nt(q_one, k_pair)
                expd = jnp.exp(scores - jnp.max(scores, axis=-1, keepdims=True))
                share = 1.0 / jnp.sum(expd, axis=-1, keepdims=True)
                probs = (expd * share).astype(jnp.bfloat16)
                p_ref[b * HEADS + 2 * pair + side] = probs
                found.append(dot_nn(probs, v_pair))
            ctx_ref[rows, pl.ds(pair * pair_w, pair_w)] = jnp.where(masks[0], *found).astype(jnp.bfloat16)
    attn_out = dot_nt(ctx_ref[...], w_ref[pl.ds(3 * width_n, width_n), :]) + bias_ref[8:9, :]
    ao_ref[...] = attn_out
    for b in range(batches):
        rows = pl.ds(b * tokens_n, tokens_n)
        mid_ref[rows, :] = x_ref[rows, :] + mod_ref[b, 2:3, :] * ao_ref[rows, :]


def mlp_kernel(
    batches, lists, me_ref, live_ref, mid_ref, grad_ref, mod_ref, bias_ref, b_in_ref,
    in_own_ref, in_other_ref, out_own_ref, out_other_ref,
    out_ref, dmid_ref, g0_ref, g1_ref, g2_ref, g3_ref, gb_in_ref, gb_out_ref, dmod_ref,
    h_ref, dmlp_ref, mlp_ref, dh_ref,
):
    step = pl.program_id(0)
    tokens_n, width_n = mid_ref.shape[0] // batches, mid_ref.shape[1]

    @pl.when(step == 0)
    def _():
        total = jnp.zeros((1, width_n), jnp.float32)
        for b in range(batches):
            rows = pl.ds(b * tokens_n, tokens_n)
            normed, _ = layer_norm(mid_ref[rows, :])
            h_ref[rows, :] = (normed * (1.0 + mod_ref[b, 4:5, :]) + mod_ref[b, 3:4, :]).astype(jnp.bfloat16)
            d_mlp = mod_ref[b, 5:6, :] * (live_ref[b].astype(jnp.float32) * grad_ref[rows, :])
            total = total + token_sum(d_mlp)
            dmlp_ref[rows, :] = d_mlp.astype(jnp.bfloat16)
        gb_out_ref[...] = total
        mlp_ref[...] = jnp.zeros_like(mlp_ref)
        dh_ref[...] = jnp.zeros_like(dh_ref)

    def piece(w_in_ref, w_out_ref, offsets, g_ref):
        blocks, both = g_ref.shape[0], g_ref.shape[1]
        one = both // 2
        w_in = jnp.concatenate([w_in_ref[(me_ref[0] ^ at) >> 1] for at in offsets], axis=0)
        w_out = jnp.concatenate([w_out_ref[(me_ref[0] ^ at) >> 1] for at in offsets], axis=0)
        pre = dot_nt(h_ref[...], w_in) + b_in_ref[...]
        root = math.sqrt(2.0 / math.pi)
        square = pre * pre
        tanh = jnp.tanh(root * (pre + 0.044715 * (square * pre)))
        half = 0.5 * (1.0 + tanh)
        act = (pre * half).astype(jnp.bfloat16)
        slope = half + (0.5 * pre) * (1.0 - tanh * tanh) * (root + (3.0 * 0.044715 * root) * square)
        d_pre = dot_nt(dmlp_ref[...], w_out) * slope
        mlp_ref[...] += dot_nn(act, w_out)
        g_ref[:, one:, :] = dot_tn(act, dmlp_ref[...]).astype(jnp.bfloat16).reshape(blocks, one, width_n)
        gb_in_ref[...] = token_sum(d_pre)
        d_pre_b = d_pre.astype(jnp.bfloat16)
        dh_ref[...] += dot_nn(d_pre_b, w_in)
        g_ref[:, :one, :] = dot_tn(d_pre_b, h_ref[...]).astype(jnp.bfloat16).reshape(blocks, one, width_n)

    other = (in_other_ref, out_other_ref)
    own = (in_own_ref, out_own_ref)
    for idx, args in enumerate(
        (
            (*other, lists[0], g0_ref),
            (*other, lists[1], g1_ref),
            (*own, lists[0], g2_ref),
            (*own, lists[1], g3_ref),
        )
    ):
        pl.when(step == idx)(functools.partial(piece, *args))

    @pl.when(step == pl.num_programs(0) - 1)
    def _():
        for b in range(batches):
            rows = pl.ds(b * tokens_n, tokens_n)
            live = live_ref[b].astype(jnp.float32)
            middle = mid_ref[rows, :]
            d_y = live * grad_ref[rows, :]
            mlp_out = mlp_ref[rows, :] + bias_ref[13:14, :]
            out_ref[rows, :] = live * (middle + mod_ref[b, 5:6, :] * mlp_out)
            normed, inv_std = layer_norm(middle)
            d_h = dh_ref[rows, :]
            dmod_ref[b, 0:1, :] = token_sum(d_h)
            dmod_ref[b, 1:2, :] = token_sum(d_h * normed)
            dmod_ref[b, 2:3, :] = token_sum(d_y * mlp_out)
            dmid_ref[rows, :] = d_y + norm_back(d_h * (1.0 + mod_ref[b, 4:5, :]), normed, inv_std)


def attend_back_kernel(
    batches, mod_ref, w_ref, qkv_ref, p_ref, ctx_ref, ao_ref, dmid_ref,
    dqkv_ref, g_ref, gb_ref, dgate_ref, dattn_ref, dctx_ref,
):
    tokens_n, width_n = dmid_ref.shape[0] // batches, dmid_ref.shape[1]
    pair_w = 2 * (width_n // HEADS)
    scaling = 1.0 / math.sqrt(width_n // HEADS)
    total = jnp.zeros((1, width_n), jnp.float32)
    for b in range(batches):
        rows = pl.ds(b * tokens_n, tokens_n)
        d_mid = dmid_ref[rows, :]
        dgate_ref[b, 0:1, :] = token_sum(d_mid * ao_ref[rows, :])
        d_attn = mod_ref[b, 2:3, :] * d_mid
        total = total + token_sum(d_attn)
        dattn_ref[rows, :] = d_attn.astype(jnp.bfloat16)
    gb_ref[2:3, :] = total
    dctx_ref[...] = dot_nn(dattn_ref[...], w_ref[pl.ds(3 * width_n, width_n), :]).astype(jnp.bfloat16)
    g_ref[...] = dot_tn(dattn_ref[...], ctx_ref[...]).astype(jnp.bfloat16)
    masks = pair_masks(tokens_n, pair_w)
    for pair in range(HEADS // 2):
        cols = pl.ds(pair * pair_w, pair_w)
        q_total = jnp.zeros((1, pair_w), jnp.float32)
        v_total = jnp.zeros((1, pair_w), jnp.float32)
        for b in range(batches):
            rows = pl.ds(b * tokens_n, tokens_n)
            q_pair = qkv_ref[rows, cols]
            k_pair = qkv_ref[rows, pl.ds(width_n + pair * pair_w, pair_w)]
            v_pair = qkv_ref[rows, pl.ds(2 * width_n + pair * pair_w, pair_w)]
            dc_pair = dctx_ref[rows, cols]
            d_q, d_k, d_v = [], [], []
            for side in range(2):
                probs_b = p_ref[b * HEADS + 2 * pair + side]
                probs = probs_b.astype(jnp.float32)
                dc_one = jnp.where(masks[side], dc_pair, jnp.zeros_like(dc_pair))
                d_probs = dot_nt(dc_one, v_pair)
                row_dot = jnp.sum(probs * d_probs, axis=-1, keepdims=True)
                d_scores = (probs * (d_probs - row_dot)).astype(jnp.bfloat16)
                d_v.append(dot_tn(probs_b, dc_pair))
                d_q.append(dot_nn(d_scores, k_pair))
                d_k.append(dot_tn(d_scores, q_pair))
            d_query = jnp.where(masks[0], *d_q) * scaling
            d_key = jnp.where(masks[0], *d_k) * scaling
            d_value = jnp.where(masks[0], *d_v)
            q_total = q_total + token_sum(d_query)
            v_total = v_total + token_sum(d_value)
            dqkv_ref[rows, cols] = d_query.astype(jnp.bfloat16)
            dqkv_ref[rows, pl.ds(width_n + pair * pair_w, pair_w)] = d_key.astype(jnp.bfloat16)
            dqkv_ref[rows, pl.ds(2 * width_n + pair * pair_w, pair_w)] = d_value.astype(jnp.bfloat16)
        gb_ref[0:1, cols] = q_total
        gb_ref[1:2, cols] = v_total
def project_back_kernel(
    batches, offsets, me_ref, x_ref, mod_ref, w_ref, h_ref, dqkv_ref, g_out_ref, dmid_ref,
    dx_ref, keep_ref, send_ref, dmod_ref, g_ref,
):
    tokens_n, width_n = x_ref.shape[0] // batches, x_ref.shape[1]
    for part in range(3):
        cols = pl.ds(part * width_n, width_n)
        g_ref[cols, :] = dot_tn(dqkv_ref[:, cols], h_ref[...]).astype(jnp.bfloat16)
    g_ref[pl.ds(3 * width_n, width_n), :] = g_out_ref[...]
    half, block_n = keep_ref.shape[0], keep_ref.shape[1]
    for idx, offset in enumerate(offsets):
        target = keep_ref if idx < half else send_ref
        target[idx % half] = g_ref[block_rows(me_ref, offset, block_n), :]
    d_h_all = dot_nn(dqkv_ref[...], w_ref[pl.ds(0, 3 * width_n), :])
    for b in range(batches):
        rows = pl.ds(b * tokens_n, tokens_n)
        normed, inv_std = layer_norm(x_ref[rows, :])
        d_h = d_h_all[b * tokens_n : (b + 1) * tokens_n]
        dmod_ref[b, 0:1, :] = token_sum(d_h)
        dmod_ref[b, 1:2, :] = token_sum(d_h * normed)
        dx_ref[rows, :] = dmid_ref[rows, :] + norm_back(d_h * (1.0 + mod_ref[b, 1:2, :]), normed, inv_std)


def shaped(shape, dtype):
    return jax.ShapeDtypeStruct(shape, dtype)


SCALARS = pl.BlockSpec(memory_space=pltpu.SMEM)


def blocks_in(count):
    return [pl.BlockSpec(memory_space=pltpu.VMEM)] * count


def cost(flops, moved, exps=0):
    return pl.CostEstimate(flops=flops, bytes_accessed=moved, transcendentals=exps)


def attend(me, x_rows, mods, own, other, bias_rows):
    batches = mods.shape[0]
    total_n, width_n = x_rows.shape
    tokens_n = total_n // batches
    return pl.pallas_call(
        functools.partial(attend_kernel, batches),
        in_specs=[SCALARS] + blocks_in(5),
        out_shape=(
            shaped((4 * width_n, width_n), jnp.bfloat16),
            shaped((total_n, width_n), jnp.bfloat16),
            shaped((total_n, 3 * width_n), jnp.bfloat16),
            shaped((batches * HEADS, tokens_n, tokens_n), jnp.bfloat16),
            shaped((total_n, width_n), jnp.bfloat16),
            shaped((total_n, width_n), jnp.float32),
            shaped((total_n, width_n), jnp.float32),
        ),
        cost_estimate=cost(8 * total_n * width_n * (width_n + tokens_n), 9 << 20, 800000),
        name="attend",
    )(me, x_rows, mods, own, other, bias_rows)


def mlp(me, live_flags, middle, grad_rows, mods, bias_rows, bias_in, weights, lists, piece_shape):
    batches = mods.shape[0]
    total_n, width_n = middle.shape
    hidden = bias_in.shape[1]
    whole = lambda *shape: pl.BlockSpec(shape, lambda i: (0,) * len(shape))
    line = pl.BlockSpec((1, hidden // 4), lambda i: (0, i))
    return pl.pallas_call(
        functools.partial(mlp_kernel, batches, lists),
        grid=(4,),
        in_specs=[
            SCALARS,
            SCALARS,
            whole(total_n, width_n),
            whole(total_n, width_n),
            whole(*mods.shape),
            whole(*bias_rows.shape),
            line,
        ]
        + [whole(*value.shape) for value in weights],
        out_specs=[whole(total_n, width_n)] * 2
        + [whole(*piece_shape)] * 4
        + [line, whole(1, width_n), whole(batches, 3, width_n)],
        out_shape=[shaped((total_n, width_n), jnp.float32)] * 2
        + [shaped(piece_shape, jnp.bfloat16)] * 4
        + [
            shaped((1, hidden), jnp.float32),
            shaped((1, width_n), jnp.float32),
            shaped((batches, 3, width_n), jnp.float32),
        ],
        scratch_shapes=[
            pltpu.VMEM((total_n, width_n), jnp.bfloat16),
            pltpu.VMEM((total_n, width_n), jnp.bfloat16),
            pltpu.VMEM((total_n, width_n), jnp.float32),
            pltpu.VMEM((total_n, width_n), jnp.float32),
        ],
        cost_estimate=cost(12 * total_n * width_n * hidden, 9 << 20, total_n * hidden),
        name="mlp",
    )(me, live_flags, middle, grad_rows, mods, bias_rows, bias_in, *weights)


def attend_back(mods, weight, qkv, probs, context, attn_out, d_mid):
    batches = mods.shape[0]
    total_n, width_n = d_mid.shape
    return pl.pallas_call(
        functools.partial(attend_back_kernel, batches),
        out_shape=(
            shaped((total_n, 3 * width_n), jnp.bfloat16),
            shaped((width_n, width_n), jnp.bfloat16),
            shaped((3, width_n), jnp.float32),
            shaped((batches, 1, width_n), jnp.float32),
        ),
        scratch_shapes=[
            pltpu.VMEM((total_n, width_n), jnp.bfloat16),
            pltpu.VMEM((total_n, width_n), jnp.bfloat16),
        ],
        cost_estimate=cost(8 * total_n * width_n * width_n, 9 << 20),
        name="attend_back",
    )(mods, weight, qkv, probs, context, attn_out, d_mid)


def project_back(me, x_rows, mods, weight, h_in, d_qkv, g_out, d_mid, offsets, block_shape):
    batches = mods.shape[0]
    total_n, width_n = x_rows.shape
    return pl.pallas_call(
        functools.partial(project_back_kernel, batches, offsets),
        in_specs=[SCALARS] + blocks_in(7),
        out_shape=(
            shaped((total_n, width_n), jnp.float32),
            shaped(block_shape, jnp.bfloat16),
            shaped(block_shape, jnp.bfloat16),
            shaped((batches, 2, width_n), jnp.float32),
        ),
        scratch_shapes=[pltpu.VMEM((4 * width_n, width_n), jnp.bfloat16)],
        cost_estimate=cost(12 * total_n * width_n * width_n, 8 << 20),
        name="project_back",
    )(me, x_rows, mods, weight, h_in, d_qkv, g_out, d_mid)


def exchange(value, bit_idx):
    group_n = lax.axis_size("fsdp")
    return lax.ppermute(value, "fsdp", [(dev, dev ^ (1 << bit_idx)) for dev in range(group_n)])


def offsets_of(order):
    return [
        sum(((q >> at) & 1) << bit_idx for at, bit_idx in enumerate(order))
        for q in range(1 << len(order))
    ]


def together(*values):
    return lax.optimization_barrier(values)


def gather_blocks(blocks, order):
    for bit_idx in order:
        blocks = jnp.concatenate([blocks, exchange(blocks, bit_idx)], axis=0)
    return blocks


def gather_ordered(block, order):
    high = max(order)
    cur = block.reshape((1,) * high + block.shape)
    for bit_idx in order:
        other = exchange(cur, bit_idx)
        upper = (lax.axis_index("fsdp") >> bit_idx) & 1 == 1
        cur = jnp.concatenate(
            [jnp.where(upper, other, cur), jnp.where(upper, cur, other)], axis=high - bit_idx
        )
    return cur.reshape((-1,) + block.shape)


def add(left, right, dtype=jnp.bfloat16):
    return (left.astype(jnp.float32) + right.astype(jnp.float32)).astype(dtype)


def scatter_step(keep, other, bit_idx):
    half = keep.shape[0] // 2
    upper = exchange(add(keep[half:], other[half:], keep.dtype), bit_idx)
    return add(keep[:half], other[:half], keep.dtype), upper


def local(inputs, cond, live, ada_w, attn_w, fc1_w, fc2_w, biases, grad_out):
    group_n = lax.axis_size("fsdp")
    count = group_n.bit_length() - 1
    far, near = list(range(count - 1, 2, -1)), [1, 2]
    me = lax.axis_index("fsdp").astype(jnp.int32)
    me_line = me.reshape(1)
    width_n = attn_w.shape[2]
    batches = inputs.shape[0]
    own_attn, own_ada, own_bias = attn_w.shape[1], ada_w.shape[1], biases.shape[1]
    own_hidden = fc1_w.shape[1]

    def chosen(offsets):
        sources = me ^ jnp.array(offsets, jnp.int32)
        return (sources[:, None] == jnp.arange(group_n, dtype=jnp.int32)[None]).astype(jnp.float32)

    def pick(form, left, right):
        return jnp.einsum(form, left, right, precision=lax.Precision.HIGHEST)

    cond_rows = cond[:, 0]
    sigmoid_c = jax.nn.sigmoid(cond_rows)
    sc_own = (cond_rows * sigmoid_c).astype(jnp.bfloat16)
    bias_line = jnp.pad(biases, ((0, 0), (0, width_n - own_bias)))
    pad_rows = -(own_ada + 1 + batches) % 16
    attn_order = far + near + [0]
    attn_offsets = offsets_of(attn_order)
    attn_pick = chosen(attn_offsets)
    ada_own = jnp.concatenate(
        [ada_w[0], bias_line, sc_own, jnp.zeros((pad_rows, width_n), jnp.bfloat16)], axis=0
    )[None]
    attn_own = gather_ordered(attn_w[0], far + near[::-1])
    ada_own = gather_ordered(ada_own[0], far + near)
    in_own = gather_ordered(fc1_w[0], far + near[::-1])
    out_own = gather_ordered(fc2_w[0], far + near)
    attn_other = exchange(attn_own, 0)
    ada_other = exchange(ada_own, 0)
    weights = [in_own, exchange(in_own, 0), out_own, exchange(out_own, 0)]
    ada_halves = (ada_own, ada_other)
    odd = me & 1 == 1

    def interleaved(own, other, axis):
        return jnp.stack([jnp.where(odd, other, own), jnp.where(odd, own, other)], axis=axis + 1).reshape(
            own.shape[:axis] + (group_n,) + own.shape[axis + 1 :]
        )

    side_all = interleaved(*[part[:, own_ada : own_ada + 1 + batches] for part in ada_halves], 0)
    bias_rows = side_all[:, 0, :own_bias].astype(jnp.float32).reshape(-1, width_n)
    mod_blocks = interleaved(
        *[
            product("bd,ed->be", sc_own, part.reshape(-1, width_n)).reshape(
                batches, group_n // 2, -1
            )
            for part in ada_halves
        ],
        1,
    )
    mods = mod_blocks[:, :, :own_ada].reshape(batches, 6, width_n) + bias_rows[:6]
    block_shape = attn_own.shape
    even = own_attn % 16 == 0
    if not even:
        table = me ^ jnp.array(attn_offsets, jnp.int32)
        ordered = interleaved(attn_own, attn_other, 0)
        halves = ordered.reshape(2, 1, 2 * width_n, width_n)
        attn_in = (halves[0], halves[1])
    else:
        attn_in = (attn_own, attn_other)
    a_offsets = offsets_of(far[:-1] + near[::-1])
    b_offsets = [one ^ (1 << far[-1]) for one in offsets_of(far[:-1] + near)]
    hidden_offsets = (
        [one ^ 1 for one in a_offsets] + [one ^ 1 for one in b_offsets] + a_offsets + b_offsets
    )
    hidden_pick = chosen(hidden_offsets)
    bias_in = pick(
        "qj,je->qe", hidden_pick, bias_rows[9:-1].reshape(group_n, own_hidden)
    ).reshape(1, -1)

    lists = [a_offsets, b_offsets]
    piece_shape = (group_n // 4, 2 * own_hidden, width_n)

    def unpacked(piece):
        parts = piece.reshape(2, -1, own_hidden, width_n).swapaxes(0, 1)
        return parts.reshape(-1, 2 * own_hidden, width_n)

    x_rows = inputs.reshape(-1, width_n)
    plain = [0, 1]
    weight, h_in, qkv, probs, context, attn_out, middle = attend(
        me_line if even else jnp.zeros_like(me_line),
        x_rows,
        mods,
        attn_in[0],
        attn_in[1],
        bias_rows,
    )
    if own_hidden % 16:
        own_table = (me ^ jnp.array(a_offsets + b_offsets, jnp.int32)) >> 1
        weights = [value[own_table].reshape(2, -1, width_n) for value in weights]
        lists = [[0], [2]]
        piece_shape = (1, group_n // 4 * 2 * own_hidden, width_n)
    out, d_mid, g_a_send, g_b_send, g_a, g_b, gb_in, gb_out, dmod_b = mlp(
        jnp.zeros_like(me_line) if own_hidden % 16 else me_line,
        live[:, 0],
        middle,
        grad_out.reshape(-1, width_n),
        mods,
        bias_rows,
        bias_in,
        weights,
        lists,
        piece_shape,
    )
    g_hidden = [g_a_send, g_b_send, g_a, g_b]
    if own_hidden % 16:
        g_hidden = [unpacked(piece) for piece in g_hidden]
    g_a_send, g_b_send, g_a, g_b = g_hidden
    got_a, got_b = exchange(g_a_send, 0), exchange(g_b_send, 0)
    d_qkv, g_out, gb_attn, d_gate = attend_back(
        mods, weight, qkv, probs, context, attn_out, d_mid
    )
    got_a, got_b, d_qkv, g_out = together(got_a, got_b, d_qkv, g_out)
    g_a, got_a = scatter_step(g_a, got_a, near[0])
    g_b, got_b = scatter_step(g_b, got_b, near[1])
    d_x, g_keep, g_send, dmod_a = project_back(
        me_line if even else jnp.zeros_like(me_line),
        x_rows,
        mods,
        weight,
        h_in,
        d_qkv,
        g_out,
        d_mid,
        attn_offsets if even else plain,
        block_shape if even else (1, 2 * width_n, width_n),
    )
    if not even:
        ordered = jnp.concatenate([g_keep, g_send], axis=1).reshape((group_n,) + block_shape[1:])[table]
        g_keep, g_send = ordered[: group_n // 2], ordered[group_n // 2 :]
    got_a, got_b, g_send, dmod_a = together(got_a, got_b, g_send, dmod_a)
    top = count - 1
    g_attn, got = g_keep, exchange(g_send, 0)
    g_a, got_a = scatter_step(g_a, got_a, near[1])
    g_b, got_b = scatter_step(g_b, got_b, near[0])
    d_mods = jnp.concatenate([dmod_a, d_gate, dmod_b], axis=1)
    true_in = pick("qj,qe->je", hidden_pick, gb_in.reshape(group_n, own_hidden))
    g_bias = jnp.concatenate(
        [jnp.sum(d_mods, axis=0), gb_attn, true_in.reshape(-1, width_n), gb_out], axis=0
    )
    mod_blocks = d_mods.reshape(batches, group_n, own_ada)
    side_n = batches * own_ada + own_bias
    row_n = -(-side_n // width_n)
    side_blocks = jnp.concatenate(
        [mod_blocks[idx] for idx in range(batches)]
        + [
            g_bias.reshape(group_n, own_bias),
            jnp.zeros((group_n, row_n * width_n - side_n), jnp.float32),
        ],
        axis=1,
    )
    side_blocks = pick("qj,je->qe", attn_pick, side_blocks)
    side_blocks = side_blocks.astype(jnp.bfloat16).reshape(group_n, row_n, width_n)

    def send(values, blocks, at):
        split = blocks.reshape((-1, 2, 1 << at) + blocks.shape[1:])
        parts = [*values, split[:, 1:]]
        flat = [part.reshape(-1, width_n) for part in parts]
        both = exchange(jnp.concatenate(flat, axis=0), attn_order[at]) if values else exchange(flat[0], attn_order[at])
        came, start = [], 0
        for part, rows in zip(parts, flat):
            came.append(both[start : start + rows.shape[0]].reshape(part.shape))
            start += rows.shape[0]
        return came[:-1], jnp.concatenate([split[:, :1], came[-1]], axis=1).reshape(blocks.shape)

    def halves(keep, other):
        half = keep.shape[0] // 2
        return add(keep[:half], other[:half]), add(keep[half:], other[half:])

    _, side_blocks = send([], side_blocks, top)
    got, got_a, got_b, side_blocks = together(got, got_a, got_b, side_blocks)
    for at in range(top - 1, len(far) - 1, -1):
        g_attn, upper = halves(g_attn, got)
        (got,), side_blocks = send([upper], side_blocks, at)
    g_hid, upper_hid = add(g_a, got_a), add(g_b, got_b)
    for at in range(len(far) - 1, -1, -1):
        g_attn, upper = halves(g_attn, got)
        if at < len(far) - 1:
            g_hid, upper_hid = halves(g_hid, got_hid)
        (got, got_hid), side_blocks = send([upper, upper_hid], side_blocks, at)
    mod_pairs = mod_blocks.reshape(batches, group_n // 2, 2, own_ada)
    d_sc = sum(
        jnp.einsum(
            "bqr,qrd->bd",
            jnp.pad(
                lax.dynamic_index_in_dim(mod_pairs, (me & 1) ^ side, 2, keepdims=False),
                ((0, 0), (0, 0), (0, part.shape[1] - own_ada)),
            ),
            part.astype(jnp.float32),
            precision=lax.Precision.HIGHEST,
        )
        for side, part in enumerate(ada_halves)
    )
    d_cond = d_sc * sigmoid_c * (1.0 + cond_rows * (1.0 - sigmoid_c))
    side_got = side_blocks.reshape(group_n, -1).astype(jnp.float32)
    own_mods = side_got[:, : batches * own_ada].reshape(group_n, batches, own_ada)
    d_bias = jnp.sum(side_got[:, batches * own_ada : side_n], axis=0)
    sc_all = pick("qj,jbd->qbd", attn_pick, side_all[:, 1:].astype(jnp.float32))
    d_ada = pick("qbr,qbd->rd", own_mods, sc_all)
    d_attn = add(g_attn, got, jnp.float32)
    d_hidden = add(g_hid, got_hid, jnp.float32)
    return (
        out.reshape(inputs.shape),
        d_x.reshape(inputs.shape),
        d_cond[:, None],
        d_ada[None],
        d_attn,
        d_hidden[:, :own_hidden],
        d_hidden[:, own_hidden:],
        d_bias[None],
    )


def solution(mesh):
    return jax.shard_map(
        local,
        mesh=mesh,
        in_specs=(
            P(None, "fsdp", None, None),
            P(None, "fsdp", None),
            P(None, "fsdp"),
            P(None, "fsdp", None),
            P(None, "fsdp", None),
            P(None, "fsdp", None),
            P(None, "fsdp", None),
            P(None, "fsdp"),
            P(None, "fsdp", None, None),
        ),
        out_specs=(
            P(None, "fsdp", None, None),
            P(None, "fsdp", None, None),
            P(None, "fsdp", None),
            P(None, "fsdp", None),
            P(None, "fsdp", None),
            P(None, "fsdp", None),
            P(None, "fsdp", None),
            P(None, "fsdp"),
        ),
        check_vma=False,
    )
```

time: 150 us -> 138 us (0.920)
  starting transfers between devices: 43.2 us -> 34.4 us
  local copies, waits for them, and re-layouts: 14.5 us -> 6.74 us
  Pallas kernels: 26.8 us -> 31.2 us
  matrix products: 3.08 us -> 5.77 us
  other arithmetic: 24 us -> 22 us
    ppermute x40 -> x32, starting transfers between devices: 43.2 us -> 34.4 us  [exchange(): lax.ppermute(value, 'fsdp', [(dev, dev ^ 1 << bit_idx) for dev in range(g...]
    pallas_call x2 -> x3, Pallas kernels: 17.2 us -> 23.2 us  [the longest x1 12.2 us: mlp(): pl.pallas_call(functools.partial(mlp_kernel, batches, lists), grid=(4,),...]
    convert_element_type x13 -> x10, other arithmetic: 4.19 us -> 8 us  [the longest x9 7.39 us: add(): return (left.astype(jnp.float32) + right.astype(jnp.float32)).astype(dtype)]
    concatenate x28 -> x26, other arithmetic: 7.46 us -> 3.73 us  [the longest x16 1.46 us: gather_ordered(): jnp.concatenate([jnp.where(upper, other, cur), jnp.where(upper, cur, othe...]
    slice x4 -> x14, local copies, waits for them, and re-layouts: 4.66 us -> 1.48 us  [the longest x5 0.75 us: send(): split[:, :1]]
    dynamic_slice x16 -> x3, local copies, waits for them, and re-layouts: 2.39 us -> 0.05 us  [local(): lax.dynamic_index_in_dim(mod_pairs, me & 1 ^ side, 2, keepdims=False)]
    dot_general x2 -> x7, matrix products: 2.52 us -> 4.72 us  [the longest x5 3.17 us: pick(): return jnp.einsum(form, left, right, precision=lax.Precision.HIGHEST)]
    unnamed x30 -> x18, local copies, waits for them, and re-layouts: 2.53 us -> 0.63 us
  transfers between devices with their start and end apart: 40 -> 32, of which waited for: 22 -> 14; matrix products, arithmetic and copies ran while one was open for 22% -> 17% of each run, Pallas kernels for 0% -> 14%
where the time goes in v3:
time: 138 us; the launch traced here: 137 us
  waiting for transfers between devices  35.4 us (26%)
  starting transfers between devices  34.4 us (25%)
  Pallas kernels  31.2 us (23%)
  other arithmetic  22 us (16%)
  local copies, waits for them, and re-layouts  6.74 us (5%)
  matrix products  5.77 us (4%)
    ppermute x32, waiting for transfers between devices, exchange(): lax.ppermute(value, 'fsdp', [(dev, dev ^ 1 << bit_idx) for dev in range(g...  35.4 us
    ppermute x32, starting transfers between devices, exchange(): lax.ppermute(value, 'fsdp', [(dev, dev ^ 1 << bit_idx) for dev in range(g...  34.4 us
    pallas_call x1, Pallas kernels, mlp(): pl.pallas_call(functools.partial(mlp_kernel, batches, lists), grid=(4,),...  12.2 us
    pallas_call x1, Pallas kernels, attend_back(): pl.pallas_call(functools.partial(attend_back_kernel, batches), out_shape=...  7.97 us
    convert_element_type x9, other arithmetic, add(): return (left.astype(jnp.float32) + right.astype(jnp.float32)).astype(dtype)  7.39 us
    pallas_call x1, Pallas kernels, attend(): pl.pallas_call(functools.partial(attend_kernel, batches), in_specs=[SCALA...  6.02 us
    pallas_call x1, Pallas kernels, project_back(): pl.pallas_call(functools.partial(project_back_kernel, batches, offsets),...  4.98 us
    dot_general x5, matrix products, pick(): return jnp.einsum(form, left, right, precision=lax.Precision.HIGHEST)  3.17 us
  transfers between devices with their start and end apart: 32, of which 14 were waited for; matrix products, arithmetic and copies ran while one was open for 17% of the time, Pallas kernels for 14%

profile of v3, /device:TPU:0, one launch (start us, length us, event | category | flops | bytes accessed | tf_op | source)
XLA Modules:
  0.0 136.8 jit_solution(4841159367827324845)
XLA Ops:
  0.6 4.1 %collective-permute-start.10 = (bf16[1,1,1,1,48,384]{5,4,3,2,1,0:T(8,128)(2,1)}, bf16[1,1,1,1,48,384]{5,4,3,2,1,0:T(8,128)(2,1)S(1)}, u32[]{:S(2)}, u32[]{:S(2)}) collective-permute-start(bf16[1,1,1,1,48,384]{5,4,3,2,1,0:T(8,128)(2,1)} %bitcast.206), channel_id=1, source_target_pairs={{0,16},{1,17},{2,18},{3,19},{4,20},{5,21},{6,22},{7,23},{8,24},{9,... | collective-permute-start | bytes 110600 | tf_op jit(solution)/shard_map/ppermute | solution.py:368
  4.8 2.8 %collective-permute-start.5 = (bf16[1,1,1,1,48,384]{5,4,3,2,1,0:T(8,128)(2,1)}, bf16[1,1,1,1,48,384]{5,4,3,2,1,0:T(8,128)(2,1)S(1)}, u32[]{:S(2)}, u32[]{:S(2)}) collective-permute-start(bf16[1,1,1,1,48,384]{5,4,3,2,1,0:T(8,128)(2,1)} %bitcast.207), channel_id=1, source_target_pairs={{0,16},{1,17},{2,18},{3,19},{4,20},{5,21},{6,22},{7,23},{8,24},{9,... | collective-permute-start | bytes 110600 | tf_op jit(solution)/shard_map/ppermute | solution.py:368
  10.2 1.3 broadcast_xor_fusion
  12.3 1.9 %collective-permute-start.16 = (bf16[2,1,1,1,48,384]{5,4,3,2,1,0:T(8,128)(2,1)S(1)}, bf16[2,1,1,1,48,384]{5,4,3,2,1,0:T(8,128)(2,1)S(1)}, u32[]{:S(2)}, u32[]{:S(2)}) collective-permute-start(bf16[2,1,1,1,48,384]{5,4,3,2,1,0:T(8,128)(2,1)S(1)} %pad_maximum_fusion.20), channel_id=1, source_target_pairs={{0,8},{1,9},{2,10},{3,11},{4,12},{5,13},{6,14},{7,15},{8,0},{9,1},... | collective-permute-start | bytes 221192 | tf_op jit(solution)/shard_map/ppermute | solution.py:368
  15.3 1.9 %collective-permute-start.6 = (bf16[2,1,1,1,48,384]{5,4,3,2,1,0:T(8,128)(2,1)S(1)}, bf16[2,1,1,1,48,384]{5,4,3,2,1,0:T(8,128)(2,1)S(1)}, u32[]{:S(2)}, u32[]{:S(2)}) collective-permute-start(bf16[2,1,1,1,48,384]{5,4,3,2,1,0:T(8,128)(2,1)S(1)} %pad_maximum_fusion.18), channel_id=1, source_target_pairs={{0,8},{1,9},{2,10},{3,11},{4,12},{5,13},{6,14},{7,15},{8,0},{9,1},... | collective-permute-start | bytes 221192 | tf_op jit(solution)/shard_map/ppermute | solution.py:368
  18.5 1.8 %collective-permute-start.17 = (bf16[2,2,1,1,48,384]{5,4,3,2,1,0:T(8,128)(2,1)S(1)}, bf16[2,2,1,1,48,384]{5,4,3,2,1,0:T(8,128)(2,1)S(1)}, u32[]{:S(2)}, u32[]{:S(2)}) collective-permute-start(bf16[2,2,1,1,48,384]{5,4,3,2,1,0:T(8,128)(2,1)S(1)} %pad_maximum_fusion.14), channel_id=1, source_target_pairs={{0,2},{1,3},{2,0},{3,1},{4,6},{5,7},{6,4},{7,5},{8,10},{9,11},{10,... | collective-permute-start | bytes 442376 | tf_op jit(solution)/shard_map/ppermute | solution.py:368
  20.4 1.6 %collective-permute-start.12 = (bf16[2,2,1,1,48,384]{5,4,3,2,1,0:T(8,128)(2,1)S(1)}, bf16[2,2,1,1,48,384]{5,4,3,2,1,0:T(8,128)(2,1)S(1)}, u32[]{:S(2)}, u32[]{:S(2)}) collective-permute-start(bf16[2,2,1,1,48,384]{5,4,3,2,1,0:T(8,128)(2,1)S(1)} %pad_maximum_fusion.13), channel_id=1, source_target_pairs={{0,4},{1,5},{2,6},{3,7},{4,0},{5,1},{6,2},{7,3},{8,12},{9,13},{10,... | collective-permute-start | bytes 442376 | tf_op jit(solution)/shard_map/ppermute | solution.py:368
  23.2 1.6 %collective-permute-start.2 = (bf16[2,2,1,1,80,384]{5,4,3,2,1,0:T(8,128)(2,1)S(1)}, bf16[2,2,1,1,80,384]{5,4,3,2,1,0:T(8,128)(2,1)S(1)}, u32[]{:S(2)}, u32[]{:S(2)}) collective-permute-start(bf16[2,2,1,1,80,384]{5,4,3,2,1,0:T(8,128)(2,1)S(1)} %pad_maximum_fusion.9), channel_id=1, source_target_pairs={{0,2},{1,3},{2,0},{3,1},{4,6},{5,7},{6,4},{7,5},{8,10},{9,11},{10,... | collective-permute-start | bytes 737288 | tf_op jit(solution)/shard_map/ppermute | solution.py:368
  24.8 1.6 %collective-permute-start.18 = (bf16[2,2,1,2,48,384]{5,4,3,2,1,0:T(8,128)(2,1)S(1)}, bf16[2,2,1,2,48,384]{5,4,3,2,1,0:T(8,128)(2,1)S(1)}, u32[]{:S(2)}, u32[]{:S(2)}) collective-permute-start(bf16[2,2,1,2,48,384]{5,4,3,2,1,0:T(8,128)(2,1)S(1)} %pad_maximum_fusion.8), channel_id=1, source_target_pairs={{0,4},{1,5},{2,6},{3,7},{4,0},{5,1},{6,2},{7,3},{8,12},{9,13},{10,... | collective-permute-start | bytes 884744 | tf_op jit(solution)/shard_map/ppermute | solution.py:368
  27.6 1.7 %collective-permute-done.7 = bf16[2,2,1,1,48,384]{5,4,3,2,1,0:T(8,128)(2,1)S(1)} collective-permute-done((bf16[2,2,1,1,48,384]{5,4,3,2,1,0:T(8,128)(2,1)S(1)}, bf16[2,2,1,1,48,384]{5,4,3,2,1,0:T(8,128)(2,1)S(1)}, u32[]{:S(2)}, u32[]{:S(2)}) %collective-permute-start.7) | collective-permute-done | bytes 147488 | tf_op jit(solution)/shard_map/ppermute | solution.py:368
  29.4 2.7 %collective-permute-done.2 = bf16[2,2,1,1,80,384]{5,4,3,2,1,0:T(8,128)(2,1)S(1)} collective-permute-done((bf16[2,2,1,1,80,384]{5,4,3,2,1,0:T(8,128)(2,1)S(1)}, bf16[2,2,1,1,80,384]{5,4,3,2,1,0:T(8,128)(2,1)S(1)}, u32[]{:S(2)}, u32[]{:S(2)}) %collective-permute-start.2) | collective-permute-done | bytes 245792 | tf_op jit(solution)/shard_map/ppermute | solution.py:368
  32.2 1.6 %collective-permute-start.3 = (bf16[2,2,1,2,80,384]{5,4,3,2,1,0:T(8,128)(2,1)S(1)}, bf16[2,2,1,2,80,384]{5,4,3,2,1,0:T(8,128)(2,1)S(1)}, u32[]{:S(2)}, u32[]{:S(2)}) collective-permute-start(bf16[2,2,1,2,80,384]{5,4,3,2,1,0:T(8,128)(2,1)S(1)} %pad_maximum_fusion.4), channel_id=1, source_target_pairs={{0,4},{1,5},{2,6},{3,7},{4,0},{5,1},{6,2},{7,3},{8,12},{9,13},{10,... | collective-permute-start | bytes 1474568 | tf_op jit(solution)/shard_map/ppermute | solution.py:368
  33.8 1.6 %collective-permute-start.8 = (bf16[2,2,2,1,48,384]{5,4,3,2,1,0:T(8,128)(2,1)S(1)}, bf16[2,2,2,1,48,384]{5,4,3,2,1,0:T(8,128)(2,1)S(1)}, u32[]{:S(2)}, u32[]{:S(2)}) collective-permute-start(bf16[2,2,2,1,48,384]{5,4,3,2,1,0:T(8,128)(2,1)S(1)} %pad_maximum_fusion.6), channel_id=1, source_target_pairs={{0,2},{1,3},{2,0},{3,1},{4,6},{5,7},{6,4},{7,5},{8,10},{9,11},{10,... | collective-permute-start | bytes 884744 | tf_op jit(solution)/shard_map/ppermute | solution.py:368
  35.9 8.1 %collective-permute-done.3 = bf16[2,2,1,2,80,384]{5,4,3,2,1,0:T(8,128)(2,1)S(1)} collective-permute-done((bf16[2,2,1,2,80,384]{5,4,3,2,1,0:T(8,128)(2,1)S(1)}, bf16[2,2,1,2,80,384]{5,4,3,2,1,0:T(8,128)(2,1)S(1)}, u32[]{:S(2)}, u32[]{:S(2)}) %collective-permute-start.3) | collective-permute-done | bytes 491552 | tf_op jit(solution)/shard_map/ppermute | solution.py:368
  50.2 6.0 %attend.1 = (bf16[1536,384]{1,0:T(8,128)(2,1)}, bf16[512,384]{1,0:T(8,128)(2,1)}, bf16[512,1152]{1,0:T(8,128)(2,1)}, bf16[12,256,256]{2,1,0:T(8,128)(2,1)}, bf16...) custom-call(s32[1]{0:T(128)} %bitcast.me_ref, f32[512,384]{1,0:T(8,128)} %bitcast.186, ...), custom_call_target="tpu_custom_call" | custom-call | flops 1006632960 | bytes 9437184 | tf_op jit(solution)/shard_map/attend/pallas_call | solution.py:271
  56.2 12.2 %mlp.1 = (f32[512,384]{1,0:T(8,128)}, f32[512,384]{1,0:T(8,128)}, bf16[8,96,384]{2,1,0:T(8,128)(2,1)}, bf16[8,96,384]{2,1,0:T(8,128)(2,1)}, bf16[8,96,384]{2,1,0...) custom-call(s32[1]{0:T(128)} %bitcast.me_ref, ...), custom_call_target="tpu_custom_call" | custom-call | flops 3623878656 | bytes 9437184 | tf_op jit(solution)/shard_map/mlp/pallas_call | solution.py:294
  70.5 8.0 %attend_back.1 = (bf16[512,1152]{1,0:T(8,128)(2,1)}, bf16[384,384]{1,0:T(8,128)(2,1)}, f32[3,384]{1,0:T(4,128)}, f32[2,1,384]{2,1,0:T(1,128)}) custom-call(f32[2,6,384]{2,1,0:T(8,128)} %broadcast_add_fusion.mod_ref, bf16[1536,384]{1,0:T(8,128)(2,1)} %get-tuple-element.46.w_ref, bf16[512,1152]{1,0:T(8,128)(2,1)} %get-tuple-element.50.qkv_ref, ...), custom_call_target="tpu_custom_call" | custom-call | flops 603979776 | bytes 9437184 | tf_op jit(solution)/shard_map/attend_back/pallas_call | solution.py:331
  78.5 2.0 %add_convert_fusion.2 = (bf16[4,96,384]{2,1,0:T(8,128)(2,1)S(1)}, bf16[4,96,384]{2,1,0:T(8,128)(2,1)}) fusion(bf16[8,96,384]{2,1,0:T(8,128)(2,1)} %collective-permute-done.21, bf16[8,96,384]{2,1,0:T(8,128)(2,1)S(1)} %copy-done.2), kind=kLoop, calls=%fused_computation.14 | loop fusion | flops 1179648 | bytes 1769472 | tf_op jit(solution)/shard_map/convert_element_type | solution.py:401
  80.4 1.5 %collective-permute-start.23 = (bf16[4,96,384]{2,1,0:T(8,128)(2,1)}, bf16[4,96,384]{2,1,0:T(8,128)(2,1)}, u32[]{:S(2)}, u32[]{:S(2)}) collective-permute-start(bf16[4,96,384]{2,1,0:T(8,128)(2,1)} %get-tuple-element.101), channel_id=1, source_target_pairs={{0,4},{1,5},{2,6},{3,7},{4,0},{5,1},{6,2},{7,3},{8,12},{9,13},{10,... | collective-permute-start | bytes 884744 | tf_op jit(solution)/shard_map/ppermute | solution.py:368
  83.1 5.0 %project_back.1 = (f32[512,384]{1,0:T(8,128)}, bf16[16,48,384]{2,1,0:T(8,128)(2,1)}, bf16[16,48,384]{2,1,0:T(8,128)(2,1)}, f32[2,2,384]{2,1,0:T(2,128)}) custom-call(s32[1]{0:T(128)} %bitcast.me_ref, f32[512,384]{1,0:T(8,128)} %bitcast.187, f32[2,6,384]{2,1,0:T(8,128)} %broadcast_add_fusion.mod_ref, bf16[1536,384]{1,0:T(8,128)(2,1)} %get-tuple-element.46.w_ref, ...), custom_call_target="tpu_custom_call" | custom-call | flops 905969664 | bytes 8388608 | tf_op jit(solution)/shard_map/project_back/pallas_call | solution.py:351
  88.1 1.8 %collective-permute-done.23 = bf16[4,96,384]{2,1,0:T(8,128)(2,1)} collective-permute-done((bf16[4,96,384]{2,1,0:T(8,128)(2,1)}, bf16[4,96,384]{2,1,0:T(8,128)(2,1)}, u32[]{:S(2)}, u32[]{:S(2)}) %collective-permute-start.23) | collective-permute-done | bytes 294944 | tf_op jit(solution)/shard_map/ppermute | solution.py:368
  89.9 1.2 collective-permute-done.22
  96.9 1.6 %convolution_convert_fusion = bf16[32,384]{1,0:T(8,128)(2,1)} fusion(f32[32,168]{1,0:T(8,128)} %reshape.194, f32[32,72]{1,0:T(8,128)} %squeeze.32, f32[32,72]{1,0:T(8,128)S(1)} %squeeze.31, f32[384]{0:T(512)} %pad.37.clone, s32[32]{0:T(128)} %get-tuple-element.162), kind=kOutput, calls=%fused_computation.1 | convolution fusion | flops 4768768 | bytes 66176 | tf_op jit(solution)/shard_map/qj,je->qe/dot_general | solution.py:426
  101.3 1.7 %collective-permute-done.25 = bf16[2,96,384]{2,1,0:T(8,128)(2,1)} collective-permute-done((bf16[2,96,384]{2,1,0:T(8,128)(2,1)S(1)}, bf16[2,96,384]{2,1,0:T(8,128)(2,1)}, u32[]{:S(2)}, u32[]{:S(2)}) %collective-permute-start.25) | collective-permute-done | bytes 147488 | tf_op jit(solution)/shard_map/ppermute | solution.py:368
  103.0 1.2 add_convert_fusion
  106.4 7.6 %collective-permute-done.28 = bf16[400,384]{1,0:T(8,128)(2,1)S(1)} collective-permute-done((bf16[400,384]{1,0:T(8,128)(2,1)}, bf16[400,384]{1,0:T(8,128)(2,1)S(1)}, u32[]{:S(2)}, u32[]{:S(2)}) %collective-permute-start.28) | collective-permute-done | bytes 307232 | tf_op jit(solution)/shard_map/ppermute | solution.py:368
  114.2 1.5 %collective-permute-start.29 = (bf16[208,384]{1,0:T(8,128)(2,1)S(1)}, bf16[208,384]{1,0:T(8,128)(2,1)S(1)}, u32[]{:S(2)}, u32[]{:S(2)}) collective-permute-start(bf16[208,384]{1,0:T(8,128)(2,1)S(1)} %pad_maximum_fusion.11), channel_id=1, source_target_pairs={{0,2},{1,3},{2,0},{3,1},{4,6},{5,7},{6,4},{7,5},{8,10},{9,11},{10,... | collective-permute-start | bytes 479240 | tf_op jit(solution)/shard_map/ppermute | solution.py:368
  116.8 2.7 %collective-permute-done.29 = bf16[208,384]{1,0:T(8,128)(2,1)S(1)} collective-permute-done((bf16[208,384]{1,0:T(8,128)(2,1)S(1)}, bf16[208,384]{1,0:T(8,128)(2,1)S(1)}, u32[]{:S(2)}, u32[]{:S(2)}) %collective-permute-start.29) | collective-permute-done | bytes 159776 | tf_op jit(solution)/shard_map/ppermute | solution.py:368
  119.8 1.6 %collective-permute-start.30 = (bf16[304,384]{1,0:T(8,128)(2,1)S(1)}, bf16[304,384]{1,0:T(8,128)(2,1)S(1)}, u32[]{:S(2)}, u32[]{:S(2)}) collective-permute-start(bf16[304,384]{1,0:T(8,128)(2,1)S(1)} %pad_maximum_fusion.10), channel_id=1, source_target_pairs={{0,8},{1,9},{2,10},{3,11},{4,12},{5,13},{6,14},{7,15},{8,0},{9,1},... | collective-permute-start | bytes 700424 | tf_op jit(solution)/shard_map/ppermute | solution.py:368
  122.5 3.4 %collective-permute-done.30 = bf16[304,384]{1,0:T(8,128)(2,1)S(1)} collective-permute-done((bf16[304,384]{1,0:T(8,128)(2,1)S(1)}, bf16[304,384]{1,0:T(8,128)(2,1)S(1)}, u32[]{:S(2)}, u32[]{:S(2)}) %collective-permute-start.30) | collective-permute-done | bytes 233504 | tf_op jit(solution)/shard_map/ppermute | solution.py:368
  126.1 3.4 %collective-permute-start.31 = (bf16[160,384]{1,0:T(8,128)(2,1)S(1)}, bf16[160,384]{1,0:T(8,128)(2,1)S(1)}, u32[]{:S(2)}, u32[]{:S(2)}) collective-permute-start(bf16[160,384]{1,0:T(8,128)(2,1)S(1)} %pad_maximum_fusion.16), channel_id=1, source_target_pairs={{0,16},{1,17},{2,18},{3,19},{4,20},{5,21},{6,22},{7,23},{8,24},{9,... | collective-permute-start | bytes 368648 | tf_op jit(solution)/shard_map/ppermute | solution.py:368
  130.9 2.8 %collective-permute-done.31 = bf16[160,384]{1,0:T(8,128)(2,1)S(1)} collective-permute-done((bf16[160,384]{1,0:T(8,128)(2,1)S(1)}, bf16[160,384]{1,0:T(8,128)(2,1)S(1)}, u32[]{:S(2)}, u32[]{:S(2)}) %collective-permute-start.31) | collective-permute-done | bytes 122912 | tf_op jit(solution)/shard_map/ppermute | solution.py:368
  (179 shorter events, 35.8 us)
Async XLA Ops:
  0.6 10.9 %collective-permute-start.10 = (bf16[1,1,1,1,48,384]{5,4,3,2,1,0:T(8,128)(2,1)}, bf16[1,1,1,1,48,384]{5,4,3,2,1,0:T(8,128)(2,1)S(1)}, u32[]{:S(2)}, u32[]{:S(2)}) collective-permute-start(bf16[1,1,1,1,48,384]{5,4,3,2,1,0:T(8,128)(2,1)} %bitcast.206), channel_id=1, source_target_pairs={{0,16},{1,17},{2,18},{3,19},{4,20},{5,21},{6,22},{7,23},{8,24},{9,... | collective-permute-start | bytes 110600 | tf_op jit(solution)/shard_map/ppermute | solution.py:368
  4.8 6.7 %collective-permute-start.15 = (bf16[1,1,1,1,48,384]{5,4,3,2,1,0:T(8,128)(2,1)}, bf16[1,1,1,1,48,384]{5,4,3,2,1,0:T(8,128)(2,1)S(1)}, u32[]{:S(2)}, u32[]{:S(2)}) collective-permute-start(bf16[1,1,1,1,48,384]{5,4,3,2,1,0:T(8,128)(2,1)} %bitcast.205), channel_id=1, source_target_pairs={{0,16},{1,17},{2,18},{3,19},{4,20},{5,21},{6,22},{7,23},{8,24},{9,... | collective-permute-start | bytes 110600 | tf_op jit(solution)/shard_map/ppermute | solution.py:368
  4.8 9.7 %collective-permute-start.5 = (bf16[1,1,1,1,48,384]{5,4,3,2,1,0:T(8,128)(2,1)}, bf16[1,1,1,1,48,384]{5,4,3,2,1,0:T(8,128)(2,1)S(1)}, u32[]{:S(2)}, u32[]{:S(2)}) collective-permute-start(bf16[1,1,1,1,48,384]{5,4,3,2,1,0:T(8,128)(2,1)} %bitcast.207), channel_id=1, source_target_pairs={{0,16},{1,17},{2,18},{3,19},{4,20},{5,21},{6,22},{7,23},{8,24},{9,... | collective-permute-start | bytes 110600 | tf_op jit(solution)/shard_map/ppermute | solution.py:368
  9.4 7.8 %collective-permute-start = (bf16[1,1,1,1,80,384]{5,4,3,2,1,0:T(8,128)(2,1)S(1)}, bf16[1,1,1,1,80,384]{5,4,3,2,1,0:T(8,128)(2,1)S(1)}, u32[]{:S(2)}, u32[]{:S(2)}) collective-permute-start(bf16[1,1,1,1,80,384]{5,4,3,2,1,0:T(8,128)(2,1)S(1)} %fusion.18), channel_id=1, source_target_pairs={{0,16},{1,17},{2,18},{3,19},{4,20},{5,21},{6,22},{7,23},{8,24},{9,... | collective-permute-start | bytes 184328 | tf_op jit(solution)/shard_map/ppermute | solution.py:368
  12.3 6.1 %collective-permute-start.16 = (bf16[2,1,1,1,48,384]{5,4,3,2,1,0:T(8,128)(2,1)S(1)}, bf16[2,1,1,1,48,384]{5,4,3,2,1,0:T(8,128)(2,1)S(1)}, u32[]{:S(2)}, u32[]{:S(2)}) collective-permute-start(bf16[2,1,1,1,48,384]{5,4,3,2,1,0:T(8,128)(2,1)S(1)} %pad_maximum_fusion.20), channel_id=1, source_target_pairs={{0,8},{1,9},{2,10},{3,11},{4,12},{5,13},{6,14},{7,15},{8,0},{9,1},... | collective-permute-start | bytes 221192 | tf_op jit(solution)/shard_map/ppermute | solution.py:368
  14.3 6.1 %collective-permute-start.11 = (bf16[2,1,1,1,48,384]{5,4,3,2,1,0:T(8,128)(2,1)S(1)}, bf16[2,1,1,1,48,384]{5,4,3,2,1,0:T(8,128)(2,1)S(1)}, u32[]{:S(2)}, u32[]{:S(2)}) collective-permute-start(bf16[2,1,1,1,48,384]{5,4,3,2,1,0:T(8,128)(2,1)S(1)} %pad_maximum_fusion.19), channel_id=1, source_target_pairs={{0,8},{1,9},{2,10},{3,11},{4,12},{5,13},{6,14},{7,15},{8,0},{9,1},... | collective-permute-start | bytes 221192 | tf_op jit(solution)/shard_map/ppermute | solution.py:368
  15.3 6.6 %collective-permute-start.6 = (bf16[2,1,1,1,48,384]{5,4,3,2,1,0:T(8,128)(2,1)S(1)}, bf16[2,1,1,1,48,384]{5,4,3,2,1,0:T(8,128)(2,1)S(1)}, u32[]{:S(2)}, u32[]{:S(2)}) collective-permute-start(bf16[2,1,1,1,48,384]{5,4,3,2,1,0:T(8,128)(2,1)S(1)} %pad_maximum_fusion.18), channel_id=1, source_target_pairs={{0,8},{1,9},{2,10},{3,11},{4,12},{5,13},{6,14},{7,15},{8,0},{9,1},... | collective-permute-start | bytes 221192 | tf_op jit(solution)/shard_map/ppermute | solution.py:368
  18.2 4.9 %collective-permute-start.1 = (bf16[2,1,1,1,80,384]{5,4,3,2,1,0:T(8,128)(2,1)S(1)}, bf16[2,1,1,1,80,384]{5,4,3,2,1,0:T(8,128)(2,1)S(1)}, u32[]{:S(2)}, u32[]{:S(2)}) collective-permute-start(bf16[2,1,1,1,80,384]{5,4,3,2,1,0:T(8,128)(2,1)S(1)} %pad_maximum_fusion.15), channel_id=1, source_target_pairs={{0,8},{1,9},{2,10},{3,11},{4,12},{5,13},{6,14},{7,15},{8,0},{9,1},... | collective-permute-start | bytes 368648 | tf_op jit(solution)/shard_map/ppermute | solution.py:368
  18.5 6.3 %collective-permute-start.17 = (bf16[2,2,1,1,48,384]{5,4,3,2,1,0:T(8,128)(2,1)S(1)}, bf16[2,2,1,1,48,384]{5,4,3,2,1,0:T(8,128)(2,1)S(1)}, u32[]{:S(2)}, u32[]{:S(2)}) collective-permute-start(bf16[2,2,1,1,48,384]{5,4,3,2,1,0:T(8,128)(2,1)S(1)} %pad_maximum_fusion.14), channel_id=1, source_target_pairs={{0,2},{1,3},{2,0},{3,1},{4,6},{5,7},{6,4},{7,5},{8,10},{9,11},{10,... | collective-permute-start | bytes 442376 | tf_op jit(solution)/shard_map/ppermute | solution.py:368
  20.4 6.1 %collective-permute-start.12 = (bf16[2,2,1,1,48,384]{5,4,3,2,1,0:T(8,128)(2,1)S(1)}, bf16[2,2,1,1,48,384]{5,4,3,2,1,0:T(8,128)(2,1)S(1)}, u32[]{:S(2)}, u32[]{:S(2)}) collective-permute-start(bf16[2,2,1,1,48,384]{5,4,3,2,1,0:T(8,128)(2,1)S(1)} %pad_maximum_fusion.13), channel_id=1, source_target_pairs={{0,4},{1,5},{2,6},{3,7},{4,0},{5,1},{6,2},{7,3},{8,12},{9,13},{10,... | collective-permute-start | bytes 442376 | tf_op jit(solution)/shard_map/ppermute | solution.py:368
  22.0 7.3 %collective-permute-start.7 = (bf16[2,2,1,1,48,384]{5,4,3,2,1,0:T(8,128)(2,1)S(1)}, bf16[2,2,1,1,48,384]{5,4,3,2,1,0:T(8,128)(2,1)S(1)}, u32[]{:S(2)}, u32[]{:S(2)}) collective-permute-start(bf16[2,2,1,1,48,384]{5,4,3,2,1,0:T(8,128)(2,1)S(1)} %pad_maximum_fusion.12), channel_id=1, source_target_pairs={{0,4},{1,5},{2,6},{3,7},{4,0},{5,1},{6,2},{7,3},{8,12},{9,13},{10,... | collective-permute-start | bytes 442376 | tf_op jit(solution)/shard_map/ppermute | solution.py:368
  23.2 8.9 %collective-permute-start.2 = (bf16[2,2,1,1,80,384]{5,4,3,2,1,0:T(8,128)(2,1)S(1)}, bf16[2,2,1,1,80,384]{5,4,3,2,1,0:T(8,128)(2,1)S(1)}, u32[]{:S(2)}, u32[]{:S(2)}) collective-permute-start(bf16[2,2,1,1,80,384]{5,4,3,2,1,0:T(8,128)(2,1)S(1)} %pad_maximum_fusion.9), channel_id=1, source_target_pairs={{0,2},{1,3},{2,0},{3,1},{4,6},{5,7},{6,4},{7,5},{8,10},{9,11},{10,... | collective-permute-start | bytes 737288 | tf_op jit(solution)/shard_map/ppermute | solution.py:368
  24.8 10.8 %collective-permute-start.18 = (bf16[2,2,1,2,48,384]{5,4,3,2,1,0:T(8,128)(2,1)S(1)}, bf16[2,2,1,2,48,384]{5,4,3,2,1,0:T(8,128)(2,1)S(1)}, u32[]{:S(2)}, u32[]{:S(2)}) collective-permute-start(bf16[2,2,1,2,48,384]{5,4,3,2,1,0:T(8,128)(2,1)S(1)} %pad_maximum_fusion.8), channel_id=1, source_target_pairs={{0,4},{1,5},{2,6},{3,7},{4,0},{5,1},{6,2},{7,3},{8,12},{9,13},{10,... | collective-permute-start | bytes 884744 | tf_op jit(solution)/shard_map/ppermute | solution.py:368
  26.5 17.8 %collective-permute-start.13 = (bf16[2,2,2,1,48,384]{5,4,3,2,1,0:T(8,128)(2,1)S(1)}, bf16[2,2,2,1,48,384]{5,4,3,2,1,0:T(8,128)(2,1)S(1)}, u32[]{:S(2)}, u32[]{:S(2)}) collective-permute-start(bf16[2,2,2,1,48,384]{5,4,3,2,1,0:T(8,128)(2,1)S(1)} %pad_maximum_fusion.7), channel_id=1, source_target_pairs={{0,2},{1,3},{2,0},{3,1},{4,6},{5,7},{6,4},{7,5},{8,10},{9,11},{10,... | collective-permute-start | bytes 884744 | tf_op jit(solution)/shard_map/ppermute | solution.py:368
  32.2 11.8 %collective-permute-start.3 = (bf16[2,2,1,2,80,384]{5,4,3,2,1,0:T(8,128)(2,1)S(1)}, bf16[2,2,1,2,80,384]{5,4,3,2,1,0:T(8,128)(2,1)S(1)}, u32[]{:S(2)}, u32[]{:S(2)}) collective-permute-start(bf16[2,2,1,2,80,384]{5,4,3,2,1,0:T(8,128)(2,1)S(1)} %pad_maximum_fusion.4), channel_id=1, source_target_pairs={{0,4},{1,5},{2,6},{3,7},{4,0},{5,1},{6,2},{7,3},{8,12},{9,13},{10,... | collective-permute-start | bytes 1474568 | tf_op jit(solution)/shard_map/ppermute | solution.py:368
  33.8 11.2 %collective-permute-start.8 = (bf16[2,2,2,1,48,384]{5,4,3,2,1,0:T(8,128)(2,1)S(1)}, bf16[2,2,2,1,48,384]{5,4,3,2,1,0:T(8,128)(2,1)S(1)}, u32[]{:S(2)}, u32[]{:S(2)}) collective-permute-start(bf16[2,2,2,1,48,384]{5,4,3,2,1,0:T(8,128)(2,1)S(1)} %pad_maximum_fusion.6), channel_id=1, source_target_pairs={{0,2},{1,3},{2,0},{3,1},{4,6},{5,7},{6,4},{7,5},{8,10},{9,11},{10,... | collective-permute-start | bytes 884744 | tf_op jit(solution)/shard_map/ppermute | solution.py:368
  35.8 20.4 %collective-permute-start.19 = (bf16[16,48,384]{2,1,0:T(8,128)(2,1)S(1)}, bf16[16,48,384]{2,1,0:T(8,128)(2,1)}, u32[]{:S(2)}, u32[]{:S(2)}) collective-permute-start(bf16[16,48,384]{2,1,0:T(8,128)(2,1)S(1)} %bitcast.189), channel_id=1, source_target_pairs={{0,1},{1,0},{2,3},{3,2},{4,5},{5,4},{6,7},{7,6},{8,9},{9,8},{10,11... | collective-permute-start | bytes 1769480 | tf_op jit(solution)/shard_map/ppermute | solution.py:368
  44.3 2.6 %collective-permute-start.4 = (bf16[16,80,384]{2,1,0:T(8,128)(2,1)S(1)}, bf16[16,80,384]{2,1,0:T(8,128)(2,1)S(1)}, u32[]{:S(2)}, u32[]{:S(2)}) collective-permute-start(bf16[16,80,384]{2,1,0:T(8,128)(2,1)S(1)} %bitcast.181), channel_id=1, source_target_pairs={{0,1},{1,0},{2,3},{3,2},{4,5},{5,4},{6,7},{7,6},{8,9},{9,8},{10,11... | collective-permute-start | bytes 2949128 | tf_op jit(solution)/shard_map/ppermute | solution.py:368
  44.5 11.7 %collective-permute-start.14 = (bf16[16,48,384]{2,1,0:T(8,128)(2,1)S(1)}, bf16[16,48,384]{2,1,0:T(8,128)(2,1)}, u32[]{:S(2)}, u32[]{:S(2)}) collective-permute-start(bf16[16,48,384]{2,1,0:T(8,128)(2,1)S(1)} %bitcast.191), channel_id=1, source_target_pairs={{0,1},{1,0},{2,3},{3,2},{4,5},{5,4},{6,7},{7,6},{8,9},{9,8},{10,11... | collective-permute-start | bytes 1769480 | tf_op jit(solution)/shard_map/ppermute | solution.py:368
  46.0 4.1 %collective-permute-start.9 = (bf16[16,48,384]{2,1,0:T(8,128)(2,1)}, bf16[16,48,384]{2,1,0:T(8,128)(2,1)}, u32[]{:S(2)}, u32[]{:S(2)}) collective-permute-start(bf16[16,48,384]{2,1,0:T(8,128)(2,1)} %bitcast.12.own_ref), channel_id=1, source_target_pairs={{0,1},{1,0},{2,3},{3,2},{4,5},{5,4},{6,7},{7,6},{8,9},{9,8},{10,11... | collective-permute-start | bytes 1769480 | tf_op jit(solution)/shard_map/ppermute | solution.py:368
  68.5 10.0 %collective-permute-start.20 = (bf16[8,96,384]{2,1,0:T(8,128)(2,1)}, bf16[8,96,384]{2,1,0:T(8,128)(2,1)S(1)}, u32[]{:S(2)}, u32[]{:S(2)}) collective-permute-start(bf16[8,96,384]{2,1,0:T(8,128)(2,1)} %get-tuple-element.48), channel_id=1, source_target_pairs={{0,1},{1,0},{2,3},{3,2},{4,5},{5,4},{6,7},{7,6},{8,9},{9,8},{10,11... | collective-permute-start | bytes 1769480 | tf_op jit(solution)/shard_map/ppermute | solution.py:368
  68.7 9.7 %collective-permute-start.21 = (bf16[8,96,384]{2,1,0:T(8,128)(2,1)}, bf16[8,96,384]{2,1,0:T(8,128)(2,1)}, u32[]{:S(2)}, u32[]{:S(2)}) collective-permute-start(bf16[8,96,384]{2,1,0:T(8,128)(2,1)} %get-tuple-element.49), channel_id=1, source_target_pairs={{0,1},{1,0},{2,3},{3,2},{4,5},{5,4},{6,7},{7,6},{8,9},{9,8},{10,11... | collective-permute-start | bytes 1769480 | tf_op jit(solution)/shard_map/ppermute | solution.py:368
  80.4 9.4 %collective-permute-start.23 = (bf16[4,96,384]{2,1,0:T(8,128)(2,1)}, bf16[4,96,384]{2,1,0:T(8,128)(2,1)}, u32[]{:S(2)}, u32[]{:S(2)}) collective-permute-start(bf16[4,96,384]{2,1,0:T(8,128)(2,1)} %get-tuple-element.101), channel_id=1, source_target_pairs={{0,4},{1,5},{2,6},{3,7},{4,0},{5,1},{6,2},{7,3},{8,12},{9,13},{10,... | collective-permute-start | bytes 884744 | tf_op jit(solution)/shard_map/ppermute | solution.py:368
  82.1 9.0 %collective-permute-start.22 = (bf16[4,96,384]{2,1,0:T(8,128)(2,1)S(1)}, bf16[4,96,384]{2,1,0:T(8,128)(2,1)}, u32[]{:S(2)}, u32[]{:S(2)}) collective-permute-start(bf16[4,96,384]{2,1,0:T(8,128)(2,1)S(1)} %get-tuple-element.103), channel_id=1, source_target_pairs={{0,2},{1,3},{2,0},{3,1},{4,6},{5,7},{6,4},{7,5},{8,10},{9,11},{10,... | collective-permute-start | bytes 884744 | tf_op jit(solution)/shard_map/ppermute | solution.py:368
  95.0 6.3 %collective-permute-start.26 = (bf16[2,96,384]{2,1,0:T(8,128)(2,1)S(1)}, bf16[2,96,384]{2,1,0:T(8,128)(2,1)}, u32[]{:S(2)}, u32[]{:S(2)}) collective-permute-start(bf16[2,96,384]{2,1,0:T(8,128)(2,1)S(1)} %add_convert_fusion.10), channel_id=1, source_target_pairs={{0,2},{1,3},{2,0},{3,1},{4,6},{5,7},{6,4},{7,5},{8,10},{9,11},{10,... | collective-permute-start | bytes 442376 | tf_op jit(solution)/shard_map/ppermute | solution.py:368
  95.6 7.4 %collective-permute-start.24 = (bf16[16,48,384]{2,1,0:T(8,128)(2,1)}, bf16[16,48,384]{2,1,0:T(8,128)(2,1)}, u32[]{:S(2)}, u32[]{:S(2)}) collective-permute-start(bf16[16,48,384]{2,1,0:T(8,128)(2,1)} %get-tuple-element.69), channel_id=1, source_target_pairs={{0,1},{1,0},{2,3},{3,2},{4,5},{5,4},{6,7},{7,6},{8,9},{9,8},{10,11... | collective-permute-start | bytes 1769480 | tf_op jit(solution)/shard_map/ppermute | solution.py:368
  96.6 6.4 %collective-permute-start.25 = (bf16[2,96,384]{2,1,0:T(8,128)(2,1)S(1)}, bf16[2,96,384]{2,1,0:T(8,128)(2,1)}, u32[]{:S(2)}, u32[]{:S(2)}) collective-permute-start(bf16[2,96,384]{2,1,0:T(8,128)(2,1)S(1)} %add_convert_fusion.11), channel_id=1, source_target_pairs={{0,4},{1,5},{2,6},{3,7},{4,0},{5,1},{6,2},{7,3},{8,12},{9,13},{10,... | collective-permute-start | bytes 442376 | tf_op jit(solution)/shard_map/ppermute | solution.py:368
  99.3 1.3 collective-permute-start.27
  105.0 9.0 %collective-permute-start.28 = (bf16[400,384]{1,0:T(8,128)(2,1)}, bf16[400,384]{1,0:T(8,128)(2,1)S(1)}, u32[]{:S(2)}, u32[]{:S(2)}) collective-permute-start(bf16[400,384]{1,0:T(8,128)(2,1)} %pad_maximum_fusion.5), channel_id=1, source_target_pairs={{0,4},{1,5},{2,6},{3,7},{4,0},{5,1},{6,2},{7,3},{8,12},{9,13},{10,... | collective-permute-start | bytes 921608 | tf_op jit(solution)/shard_map/ppermute | solution.py:368
  114.2 5.3 %collective-permute-start.29 = (bf16[208,384]{1,0:T(8,128)(2,1)S(1)}, bf16[208,384]{1,0:T(8,128)(2,1)S(1)}, u32[]{:S(2)}, u32[]{:S(2)}) collective-permute-start(bf16[208,384]{1,0:T(8,128)(2,1)S(1)} %pad_maximum_fusion.11), channel_id=1, source_target_pairs={{0,2},{1,3},{2,0},{3,1},{4,6},{5,7},{6,4},{7,5},{8,10},{9,11},{10,... | collective-permute-start | bytes 479240 | tf_op jit(solution)/shard_map/ppermute | solution.py:368
  119.8 6.1 %collective-permute-start.30 = (bf16[304,384]{1,0:T(8,128)(2,1)S(1)}, bf16[304,384]{1,0:T(8,128)(2,1)S(1)}, u32[]{:S(2)}, u32[]{:S(2)}) collective-permute-start(bf16[304,384]{1,0:T(8,128)(2,1)S(1)} %pad_maximum_fusion.10), channel_id=1, source_target_pairs={{0,8},{1,9},{2,10},{3,11},{4,12},{5,13},{6,14},{7,15},{8,0},{9,1},... | collective-permute-start | bytes 700424 | tf_op jit(solution)/shard_map/ppermute | solution.py:368
  126.1 7.6 %collective-permute-start.31 = (bf16[160,384]{1,0:T(8,128)(2,1)S(1)}, bf16[160,384]{1,0:T(8,128)(2,1)S(1)}, u32[]{:S(2)}, u32[]{:S(2)}) collective-permute-start(bf16[160,384]{1,0:T(8,128)(2,1)S(1)} %pad_maximum_fusion.16), channel_id=1, source_target_pairs={{0,16},{1,17},{2,18},{3,19},{4,20},{5,21},{6,22},{7,23},{8,24},{9,... | collective-permute-start | bytes 368648 | tf_op jit(solution)/shard_map/ppermute | solution.py:368
  (8 other events, 57.4 us)
